TPU v7x, 32 devices: a whole 2x2x4 slice. The times are simulated.
32 devices in a mesh: group: 2 (over y), dp: 16 (over z, x, core).
Axes of the slice: x: 2, y: 2, z: 4, core: 2. Of those that a mesh axis runs over, the one named last changes fastest.
Arguments:
- frames: bfloat16 [2, 64, 128, 84, 336], P('group', 'dp'), may hold values from 0 to 1
- actions: int32 [2, 64, 128], P('group', 'dp'), may hold values from 0 to 17
- rewards: float32 [2, 64, 128], P('group', 'dp'), may hold values from 0 to 0.75
- old_values: float32 [2, 64, 128], P('group', 'dp'), may hold values from -6 to 6
- next_values: float32 [2, 64, 128], P('group', 'dp'), may hold values from -6 to 6
- terminal: int32 [2, 64, 128], P('group', 'dp'), may hold values 0 or 1
- truncated: int32 [2, 64, 128], P('group', 'dp'), may hold values 0 or 1
- behavior_logprob: float32 [2, 64, 128], P('group', 'dp'), may hold values from -3.5 to -2.3
- master: float32 [1695744], P('dp'), may hold values from -2 to 2
- first_moment: float32 [2, 1695744], P('group', 'dp'), may hold values from -1 to 1
- second_moment: float32 [2, 1695744], P('group', 'dp'), may hold values from 0 to 1, as said below
- outer_momentum: float32 [1695744], P('dp'), may hold values from -0.15625 to 0.15625
- step_count: int32 [1], replicated, may hold values from 2 to 20
Outputs:
- grads: float32 [2, 1695744], P('group', 'dp')
- norms: float32 [2], P('group')
- losses: float32 [2], P('group')
- first_new: float32 [2, 1695744], P('group', 'dp')
- second_new: float32 [2, 1695744], P('group', 'dp')
- moved: float32 [1695744], P('dp')
- momentum_new: float32 [1695744], P('dp')
- final: float32 [1695744], P('dp')
- final_low: bfloat16 [1695744], P('dp')
Inputs may be any that keep to these rules, and one draw needn't show every extreme that they name: `second_moment`: entries are positive.
All inputs are finite; a program needn't handle non-finite values. No bound on the sum of `terminal` or of `truncated` on one device may be relied on, other than what follows from the above.
Results may differ from a plain program's by a relative error of at most 0.0011.
The roundings to bfloat16 on the way count: a program that leaves them out, or rounds other values in their place, can miss the bound.
Values may be sent and summed in bfloat16 or wider, within the bound.
No kernel may reach another device: no remote copies, remote signals or barrier semaphores. Data moves between devices by JAX's collectives and lax.ppermute only.
A program may use at most 320 MiB of HBM per device.

v0:
```python
import math

import jax
import jax.numpy as jnp
from jax import lax
from jax.sharding import PartitionSpec as P

C1 = 32
C2 = 64
C3 = 64
HID = 512
ACTIONS = 18
PARAMS = 1693875


BETA_ONE = 0.9
BETA_TWO = 0.999
ADAM_EPSILON = 1e-08
LEARN_RATE = 0.005
WEIGHT_DECAY = 0.01
CLIP_NORM = 0.5
OUTER_RATE = 0.7
OUTER_MOMENTUM = 0.9
DISCOUNT = 0.99
TRACE_DECAY = 0.95
RATIO_CLIP = 0.1
VALUE_COEF = 0.5
ENTROPY_COEF = 0.01


def param_shapes():
    return [
        (8, 8, 4, C1),
        (C1,),
        (4, 4, C1, C2),
        (C2,),
        (3, 3, C2, C3),
        (C3,),
        (49 * C3, HID),
        (HID,),
        (HID, ACTIONS + 1),
        (ACTIONS + 1,),
    ]


def unpack(packed):
    pieces = []
    offset = 0
    for layout in param_shapes():
        length = math.prod(layout)
        pieces.append(packed[offset : offset + length].reshape(layout))
        offset += length
    return pieces


def trajectory_advantages(rewards, values, next_values, terminal, truncated):
    alive = 1.0 - terminal.astype(jnp.float32)
    cutoff = truncated.astype(jnp.float32)
    following = jnp.concatenate([values[:, 1:], next_values[:, -1:]], axis=1)
    following = cutoff * next_values + (1.0 - cutoff) * following
    deltas = rewards + DISCOUNT * alive * following - values
    keeping = DISCOUNT * TRACE_DECAY * alive * (1.0 - cutoff)

    def backward_step(carry, item):
        delta, keep = item
        result = delta + keep * carry
        return (result, result)

    start = jnp.zeros((rewards.shape[0],), jnp.float32)
    _, series = lax.scan(backward_step, start, (deltas.T, keeping.T), reverse=True)
    return series.T


def frame_losses(out, normed, returns, actions, behavior):
    logits = out[:, :ACTIONS]
    value = out[:, ACTIONS]
    log_probs = jax.nn.log_softmax(logits, axis=-1)
    chosen = actions[:, None] == jnp.arange(ACTIONS, dtype=jnp.int32)[None, :]
    taken = jnp.sum(jnp.where(chosen, log_probs, 0.0), axis=-1)
    ratio = jnp.exp(taken - behavior)
    surrogate = jnp.minimum(
        ratio * normed, jnp.clip(ratio, 1.0 - RATIO_CLIP, 1.0 + RATIO_CLIP) * normed
    )
    entropy = -jnp.sum(jnp.exp(log_probs) * log_probs, axis=-1)
    return jnp.sum(-surrogate + 0.5 * VALUE_COEF * (value - returns) ** 2 - ENTROPY_COEF * entropy)


def shifted_conv(inputs, kernel, extent):
    result = 0.0
    for vertical in range(kernel.shape[0]):
        for lateral in range(kernel.shape[1]):
            window = inputs[:, vertical : vertical + extent, lateral : lateral + extent, :]
            result = result + jnp.einsum(
                "bhwc,co->bhwo",
                window,
                kernel[vertical, lateral],
                preferred_element_type=jnp.float32,
            )
    return result


def kernel_grad(inputs, upstream, taps, extent):
    rows_out = []
    for vertical in range(taps):
        line = []
        for lateral in range(taps):
            window = inputs[:, vertical : vertical + extent, lateral : lateral + extent, :]
            line.append(
                jnp.einsum("bhwc,bhwo->co", window, upstream, preferred_element_type=jnp.float32)
            )
        rows_out.append(jnp.stack(line))
    return jnp.stack(rows_out)


def input_grad(upstream, kernel, extent):
    inner_size = upstream.shape[1]
    result = 0.0
    for vertical in range(kernel.shape[0]):
        for lateral in range(kernel.shape[1]):
            term = jnp.einsum(
                "bhwo,co->bhwc",
                upstream,
                kernel[vertical, lateral],
                preferred_element_type=jnp.float32,
            )
            result = result + jnp.pad(
                term,
                (
                    (0, 0),
                    (vertical, extent - inner_size - vertical),
                    (lateral, extent - inner_size - lateral),
                    (0, 0),
                ),
            )
    return result


def column_sum(values):
    return jnp.sum(values.astype(jnp.float32).reshape(-1, values.shape[-1]), axis=0)


def on_device(
    frames,
    actions,
    rewards,
    old_values,
    next_values,
    terminal,
    truncated,
    behavior_logprob,
    master,
    first_moment,
    second_moment,
    outer_momentum,
    step_count,
):
    lanes = lax.axis_size("dp")
    shard_len = master.shape[0]
    weights = lax.all_gather(master.astype(jnp.bfloat16), "dp", axis=0, tiled=True)
    w_one, b_one, w_two, b_two, w_three, b_three, w_dense, b_dense, w_head, b_head = unpack(weights)
    advantage = trajectory_advantages(
        rewards[0], old_values[0], next_values[0], terminal[0], truncated[0]
    )
    envs_here, steps_here = advantage.shape
    batch = envs_here * steps_here
    total_frames = batch * lanes
    first_sum, square_sum = lax.psum((jnp.sum(advantage), jnp.sum(advantage * advantage)), "dp")
    mean = first_sum / total_frames
    spread = square_sum / total_frames - mean * mean
    normed = ((advantage - mean) * lax.rsqrt(spread + 1e-05)).reshape(-1)
    returns = (advantage + old_values[0]).reshape(-1)
    taken_actions = actions[0].reshape(-1)
    behavior = behavior_logprob[0].reshape(-1)
    pixels = (
        frames[0]
        .reshape(batch, 21, 4, 21, 4, 4)
        .transpose(0, 1, 3, 2, 4, 5)
        .reshape(batch, 21, 21, 64)
    )
    kernel_one = w_one.reshape(2, 4, 2, 4, 4, C1).transpose(0, 2, 1, 3, 4, 5).reshape(2, 2, 64, C1)
    conv_one = shifted_conv(pixels, kernel_one, 20) + b_one.astype(jnp.float32)
    act_one = jnp.maximum(conv_one, 0.0).astype(jnp.bfloat16)
    folded_one = (
        act_one.reshape(batch, 10, 2, 10, 2, C1)
        .transpose(0, 1, 3, 2, 4, 5)
        .reshape(batch, 10, 10, 4 * C1)
    )
    kernel_two = (
        w_two.reshape(2, 2, 2, 2, C1, C2).transpose(0, 2, 1, 3, 4, 5).reshape(2, 2, 4 * C1, C2)
    )
    conv_two = shifted_conv(folded_one, kernel_two, 9) + b_two.astype(jnp.float32)
    act_two = jnp.maximum(conv_two, 0.0).astype(jnp.bfloat16)
    conv_three = shifted_conv(act_two, w_three, 7) + b_three.astype(jnp.float32)
    features = jnp.maximum(conv_three, 0.0).astype(jnp.bfloat16).reshape(batch, 49 * C3)
    hidden_pre = jnp.dot(features, w_dense, preferred_element_type=jnp.float32) + b_dense.astype(
        jnp.float32
    )
    hidden = jnp.maximum(hidden_pre, 0.0).astype(jnp.bfloat16)
    out = jnp.dot(hidden, w_head, preferred_element_type=jnp.float32) + b_head.astype(jnp.float32)

    def local_loss(values):
        return frame_losses(values, normed, returns, taken_actions, behavior) / total_frames

    loss_local, pullback = jax.vjp(local_loss, out)
    grad_out = pullback(jnp.ones((), jnp.float32))[0].astype(jnp.bfloat16)
    grad_head = jnp.einsum("bh,bo->ho", hidden, grad_out, preferred_element_type=jnp.float32)
    grad_head_bias = column_sum(grad_out)
    back_hidden = jnp.einsum("bo,ho->bh", grad_out, w_head, preferred_element_type=jnp.float32)
    grad_hidden = jnp.where(hidden_pre > 0, back_hidden, 0.0).astype(jnp.bfloat16)
    grad_dense = jnp.einsum("bi,bh->ih", features, grad_hidden, preferred_element_type=jnp.float32)
    grad_dense_bias = column_sum(grad_hidden)
    back_three = jnp.einsum(
        "bh,ih->bi", grad_hidden, w_dense, preferred_element_type=jnp.float32
    ).reshape(batch, 7, 7, C3)
    grad_conv_three = jnp.where(conv_three > 0, back_three, 0.0).astype(jnp.bfloat16)
    grad_three = kernel_grad(act_two, grad_conv_three, 3, 7)
    grad_three_bias = column_sum(grad_conv_three)
    back_two = input_grad(grad_conv_three, w_three, 9)
    grad_conv_two = jnp.where(conv_two > 0, back_two, 0.0).astype(jnp.bfloat16)
    grad_two_folded = kernel_grad(folded_one, grad_conv_two, 2, 9)
    grad_two = (
        grad_two_folded.reshape(2, 2, 2, 2, C1, C2)
        .transpose(0, 2, 1, 3, 4, 5)
        .reshape(4, 4, C1, C2)
    )
    grad_two_bias = column_sum(grad_conv_two)
    back_folded = input_grad(grad_conv_two, kernel_two, 10)
    back_one = (
        back_folded.reshape(batch, 10, 10, 2, 2, C1)
        .transpose(0, 1, 3, 2, 4, 5)
        .reshape(batch, 20, 20, C1)
    )
    grad_conv_one = jnp.where(conv_one > 0, back_one, 0.0).astype(jnp.bfloat16)
    grad_one_folded = kernel_grad(pixels, grad_conv_one, 2, 20)
    grad_one = (
        grad_one_folded.reshape(2, 2, 4, 4, 4, C1).transpose(0, 2, 1, 3, 4, 5).reshape(8, 8, 4, C1)
    )
    grad_one_bias = column_sum(grad_conv_one)
    pieces = [
        grad_one,
        grad_one_bias,
        grad_two,
        grad_two_bias,
        grad_three,
        grad_three_bias,
        grad_dense,
        grad_dense_bias,
        grad_head,
        grad_head_bias,
    ]
    padding = jnp.zeros((shard_len * lanes - PARAMS,), jnp.float32)
    grad_flat = jnp.concatenate([piece.reshape(-1) for piece in pieces] + [padding])
    summed, loss_total = lax.psum((grad_flat, loss_local), "dp")
    norm = jnp.sqrt(jnp.sum(summed * summed))
    owned = lax.dynamic_slice_in_dim(summed, lax.axis_index("dp") * shard_len, shard_len, 0)
    factor = jnp.minimum(1.0, CLIP_NORM / (norm + 1e-06))
    clipped = owned * factor
    moment_step = step_count[0].astype(jnp.float32)
    first_next = BETA_ONE * first_moment[0] + (1.0 - BETA_ONE) * clipped
    second_next = BETA_TWO * second_moment[0] + (1.0 - BETA_TWO) * clipped * clipped
    first_hat = first_next / (1.0 - jnp.power(BETA_ONE, moment_step))
    second_hat = second_next / (1.0 - jnp.power(BETA_TWO, moment_step))
    inner = master - LEARN_RATE * (
        first_hat / (jnp.sqrt(second_hat) + ADAM_EPSILON) + WEIGHT_DECAY * master
    )
    moved = lax.psum(master - inner, "group") / lax.axis_size("group")
    momentum_next = OUTER_MOMENTUM * outer_momentum + moved
    final = master - OUTER_RATE * (moved + OUTER_MOMENTUM * momentum_next)
    return (
        clipped[None],
        norm.reshape(1),
        loss_total.reshape(1),
        first_next[None],
        second_next[None],
        moved,
        momentum_next,
        final,
        final.astype(jnp.bfloat16),
    )


def solution(mesh):
    return jax.shard_map(
        on_device,
        mesh=mesh,
        in_specs=(
            P("group", "dp", None, None, None),
            P("group", "dp", None),
            P("group", "dp", None),
            P("group", "dp", None),
            P("group", "dp", None),
            P("group", "dp", None),
            P("group", "dp", None),
            P("group", "dp", None),
            P("dp"),
            P("group", "dp"),
            P("group", "dp"),
            P("dp"),
            P(),
        ),
        out_specs=(
            P("group", "dp"),
            P("group"),
            P("group"),
            P("group", "dp"),
            P("group", "dp"),
            P("dp"),
            P("dp"),
            P("dp"),
            P("dp"),
        ),
        check_vma=False,
    )
```

profile of v0, /device:TPU:0, one launch (start us, length us, event | category | flops | bytes accessed | tf_op | source)
XLA Modules:
  0.0 1024.8 jit_solution(7701893610544286102)
XLA Ops:
  11.9 9.6 while.17
  24.1 37.2 %all-reduce.15 = (f32[]{:T(128)}, f32[]{:T(128)}) all-reduce(f32[]{:T(128)} %get-tuple-element.174, f32[]{:T(128)} %reduce_sum.128), channel_id=1, replica_groups=mesh['group'=2,'dp'=16] {'dp'}, use_global_device_ids=true, to_apply=%region_8.9 | all-reduce | flops 2 | bytes 16 | tf_op jit(solution)/shard_map/psum | solution.py:167
  63.9 21.7 %copy.91 = bf16[1,4,128,84,336]{2,1,4,3,0:T(4,128)(2,1)} copy(bf16[1,4,128,84,336]{2,4,3,1,0:T(8,128)(2,1)} %param.15) | data formatting | bytes 57802752 | tf_op args[0]
  85.7 50.5 %reshape_squeeze.8 = bf16[512,21,4,21,4,4]{0,5,4,3,2,1:T(4,128)(2,1)} reshape(bf16[1,4,128,84,336]{2,1,4,3,0:T(4,128)(2,1)} %copy.91) | data formatting | bytes 57802752 | tf_op jit(solution)/shard_map/reshape;squeeze | solution.py:176
  136.1 20.4 %copy.92 = bf16[512,21,21,4,4,4]{0,5,4,3,2,1:T(4,128)(2,1)} copy(bf16[512,21,21,4,4,4]{0,5,4,2,3,1:T(4,128)(2,1)} %bitcast.500) | data formatting | bytes 57802752 | tf_op jit(solution)/shard_map/transpose | solution.py:177
  156.6 45.4 %reshape.158 = bf16[512,21,21,64]{0,3,2,1:T(8,128)(2,1)} reshape(bf16[512,21,21,4,4,4]{0,5,4,3,2,1:T(4,128)(2,1)} %copy.92) | data formatting | bytes 57802752 | tf_op jit(solution)/shard_map/reshape | solution.py:178
  202.0 70.1 %reduce.5 = bf16[16,105984]{1,0:T(8,128)(2,1)S(1)} reduce(bf16[16,1,105984]{2,1,0:T(2,128)(2,1)} %all-gather.3.cloned.1.call-done, bf16[]{:T(256)} %constant.178), dimensions={1}, to_apply=%all-gather.reduce_sub_computation | reduce | bytes 6782978 | tf_op jit(solution)/shard_map/all_gather | solution.py:159
  272.0 6.8 reshape.177
  296.5 19.2 %fusion.4 = f32[512,20,20,32]{0,3,2,1:T(8,128)} fusion(bf16[512,21,21,64]{0,3,2,1:T(8,128)(2,1)} %reshape.158, bf16[2,2,64,32]{3,2,1,0:T(8,128)(2,1)S(1)} %bitcast.516), kind=kOutput, calls=%fused_computation.12 | convolution fusion | flops 838860800 | bytes 52445184 | tf_op jit(solution)/shard_map/bhwc,co->bhwo/dot_general | solution.py:93
  315.7 19.1 %fusion.8 = f32[512,20,20,32]{0,3,2,1:T(8,128)} fusion(bf16[512,21,21,64]{0,3,2,1:T(8,128)(2,1)} %reshape.158, bf16[2,2,64,32]{3,2,1,0:T(8,128)(2,1)S(1)} %bitcast.517), kind=kOutput, calls=%fused_computation.16 | convolution fusion | flops 838860800 | bytes 52445184 | tf_op jit(solution)/shard_map/bhwc,co->bhwo/dot_general | solution.py:93
  334.7 20.3 %fusion.12 = f32[512,20,20,32]{0,3,2,1:T(8,128)} fusion(bf16[512,21,21,64]{0,3,2,1:T(8,128)(2,1)} %reshape.158, bf16[2,2,64,32]{3,2,1,0:T(8,128)(2,1)S(1)} %bitcast.518), kind=kOutput, calls=%fused_computation.20 | convolution fusion | flops 838860800 | bytes 52445184 | tf_op jit(solution)/shard_map/bhwc,co->bhwo/dot_general | solution.py:93
  355.2 46.6 %maximum_convert_fusion = (bf16[512,20,20,32]{0,3,2,1:T(8,128)(2,1)}, f32[512,20,20,32]{0,3,2,1:T(8,128)}) fusion(f32[32]{0:T(128)S(1)} %slice_convert_fusion.4, f32[512,20,20,32]{0,3,2,1:T(8,128)} %fusion.4, f32[512,20,20,32]{0,3,2,1:T(8,128)} %fusion.8, f32[512,20,20,32]{0,3,2,1:T(8,128)} %fusion.12, bf16[512,21,21,64]{0,3,2,1:T(8,128)(2,1)} %reshape.158, ...), kind=kOutput, calls=%fused_computation.8 | convolution fusion | flops 878182400 | bytes 144196096 | tf_op jit(solution)/shard_map/bhwc,co->bhwo/dot_general | solution.py:93
  401.8 6.4 copy.98
  408.2 5.4 fusion.66
  413.6 5.8 fusion.64
  419.4 4.9 fusion.62
  424.4 25.2 %maximum_convert_fusion.1 = (bf16[512,9,9,64]{0,3,2,1:T(8,128)(2,1)}, f32[512,9,9,64]{0,3,2,1:T(8,128)}) fusion(f32[64]{0:T(128)S(1)} %get-tuple-element.168, bf16[512,10,10,128]{0,3,2,1:T(8,128)(2,1)} %bitcast.489, bf16[2,2,128,64]{3,2,1,0:T(8,128)(2,1)S(1)} %bitcast.510, f32[512,9,9,64]{0,3,2,1:T(8,128)} %fusion.66, f32[512,9,9,64]{0,3,2,1:T(8,128)} %fusion.62, ...), kind=kOutput, calls=%fused_computation.30 | convolution fusion | flops 695402496 | bytes 60916224 | tf_op jit(solution)/shard_map/bhwc,co->bhwo/dot_general | solution.py:93
  449.6 5.8 fusion.21
  455.4 3.7 fusion.23
  459.1 3.7 fusion.25
  477.5 3.8 fusion.35
  481.6 18.7 %fusion.41 = (u8[512,7,64]{0,2,1:T(8,128)(4,1)S(1)}, bf16[512,7,7,64]{0,3,2,1:T(8,128)(2,1)S(1)}) fusion(f32[64]{0:T(128)S(1)} %copy-done.39, f32[512,7,7,64]{0,3,2,1:T(8,128)} %fusion.21, f32[512,7,7,64]{0,3,2,1:T(8,128)} %fusion.23, f32[512,7,7,64]{0,3,2,1:T(8,128)} %fusion.25, f32[512,7,7,64]{0,3,2,1:T(8,128)} %fusion.27, f32[512,7,7,64]{0,3,2,1:T(8,128)} %fusion.29, ...), kind=kOutput, calls=%fused_computation.59 | convolution fusion | flops 229376000 | bytes 58049024 | tf_op jit(solution)/shard_map/bhwc,co->bhwo/dot_general | solution.py:93
  525.7 4.5 convolution_bitcast_fusion
  530.3 3.7 fusion.67
  534.0 4.1 fusion.68
  548.9 5.4 fusion.74
  554.3 5.5 fusion.72
  559.8 5.4 fusion.71
  565.2 5.5 fusion.20
  570.7 22.1 %convert_reduce_fusion.2 = (f32[64]{0:T(128)}, bf16[512,9,9,64]{0,3,2,1:T(8,128)(2,1)S(1)}) fusion(bf16[512,7,7,64]{0,3,2,1:T(8,128)(2,1)S(1)} %get-tuple-element.184, bf16[3,3,64,64]{3,2,1,0:T(8,128)(2,1)S(1)} %reshape.163, f32[512,9,9,64]{0,3,2,1:T(8,128)} %fusion.74, f32[512,7,7,64]{0,3,2,1:T(8,128)} %fusion.73, f32[512,9,9,64]{0,3,2,1:T(8,128)} %fusion.72, ...), kind=kOutput, calls=%fused_computation.28 | convolution fusion | flops 247988160 | bytes 73089280 | tf_op jit(solution)/shard_map/jit(_pad)/pad | solution.py:126
  592.8 8.2 fusion.99
  601.0 6.6 fusion.98
  614.7 8.8 fusion.61
  623.5 8.8 fusion.63
  632.3 8.7 fusion.65
  641.0 9.4 convert_reduce_fusion
  650.4 28.9 %add_add_fusion = bf16[512,10,10,128]{0,3,2,1:T(8,128)(2,1)} fusion(f32[512,9,9,128]{0,3,2,1:T(8,128)} %fusion.65, f32[512,9,9,128]{0,3,2,1:T(8,128)} %fusion.63, f32[512,9,9,128]{0,3,2,1:T(8,128)} %fusion.61, bf16[512,9,9,64]{0,3,2,1:T(8,128)(2,1)} %copy-done.1, bf16[2,2,128,64]{3,2,1,0:T(8,128)(2,1)S(1)} %bitcast.514), kind=kOutput, calls=%fused_computation.7 | convolution fusion | flops 705691648 | bytes 82149376 | tf_op jit(solution)/shard_map/jit(_pad)/pad | solution.py:126
  679.3 6.1 copy.129
  685.4 8.3 convert_reduce_fusion.1
  693.7 15.2 %fusion.52 = f32[64,32]{0,1:T(8,128)S(1)} fusion(bf16[512,20,20,32]{0,3,2,1:T(8,128)(2,1)} %get-tuple-element.166, bf16[512,21,21,64]{0,3,2,1:T(8,128)(2,1)} %reshape.158), kind=kOutput, calls=%fused_computation.76 | convolution fusion | flops 838860800 | bytes 39329792 | tf_op jit(solution)/shard_map/bhwc,bhwo->co/dot_general | solution.py:109
  708.9 15.0 %fusion.49 = f32[64,32]{0,1:T(8,128)S(1)} fusion(bf16[512,20,20,32]{0,3,2,1:T(8,128)(2,1)} %get-tuple-element.166, bf16[512,21,21,64]{0,3,2,1:T(8,128)(2,1)} %reshape.158), kind=kOutput, calls=%fused_computation.75 | convolution fusion | flops 838860800 | bytes 39329792 | tf_op jit(solution)/shard_map/bhwc,bhwo->co/dot_general | solution.py:109
  723.9 15.4 %fusion.46 = f32[64,32]{0,1:T(8,128)S(1)} fusion(bf16[512,20,20,32]{0,3,2,1:T(8,128)(2,1)} %get-tuple-element.166, bf16[512,21,21,64]{0,3,2,1:T(8,128)(2,1)} %reshape.158), kind=kOutput, calls=%fused_computation.74 | convolution fusion | flops 838860800 | bytes 39329792 | tf_op jit(solution)/shard_map/bhwc,bhwo->co/dot_general | solution.py:109
  739.4 15.5 %fusion.43 = f32[64,32]{0,1:T(8,128)S(1)} fusion(bf16[512,20,20,32]{0,3,2,1:T(8,128)(2,1)} %get-tuple-element.166, bf16[512,21,21,64]{0,3,2,1:T(8,128)(2,1)} %reshape.158), kind=kOutput, calls=%fused_computation.73 | convolution fusion | flops 838860800 | bytes 39329792 | tf_op jit(solution)/shard_map/bhwc,bhwo->co/dot_general | solution.py:109
  755.5 7.2 copy.220
  763.4 62.0 %concatenate.13 = f32[1695744]{0:T(1024)} concatenate(f32[8192]{0:T(1024)S(1)} %reshape_reshape.14, f32[32]{0:T(128)S(1)} %get-tuple-element.165, f32[32768]{0:T(1024)S(1)} %reshape_reshape.15, f32[64]{0:T(128)S(1)} %copy-done.38, f32[36864]{0:T(1024)S(1)} %reshape.171, f32[64]{0:T(128)S(1)} %copy-done.40, f32[1605632]{0:T(1024)} %bitcast.504, f32[512]{0:T(512)S(1)} %copy-done.30, ...), dimensions={0} | concatenate | bytes 13565952 | tf_op jit(solution)/shard_map/concatenate | solution.py:252
  829.1 140.4 %all-reduce.19.cloned.1.call-done = f32[1695744]{0:T(1024)} async-done(((f32[1695744]{0:T(1024)}), f32[1695744]{0:T(1024)}) %all-reduce.19.cloned.1.call-update) | async-done | bytes 6782992 | tf_op jit(solution)/shard_map/psum | solution.py:253
  969.4 4.5 multiply_reduce_fusion
  978.2 33.3 %psum.38 = f32[1]{0:T(128)} all-reduce(f32[1]{0:T(128)} %bitcast.155), channel_id=1, replica_groups=mesh['group'=2,'dp'=16] {'dp'}, use_global_device_ids=true, to_apply=%region_19.20 | all-reduce | flops 1 | bytes 8 | tf_op jit(solution)/shard_map/psum | solution.py:253
  (454 shorter events, 102.6 us)
Async XLA Ops:
  7.2 194.8 %all-gather.3.cloned.1.call-start = ((), (), s32[]{:S(2)}) async-start(), calls=%async_computation.2 | async-start | bytes 7206912 | tf_op jit(solution)/shard_map/all_gather | solution.py:159
  9.3 960.2 %all-reduce.19.cloned.1.call-start = ((), (), s32[]{:S(2)}) async-start(), calls=%async_computation | async-start | bytes 13565952 | tf_op jit(solution)/shard_map/psum | solution.py:253
  22.2 63.5 %copy-start.24 = (f32[128,4]{0,1:T(4,128)}, f32[128,4]{0,1:T(4,128)S(1)}, u32[]{:S(2)}) copy-start(f32[128,4]{0,1:T(4,128)S(1)} %copy.119) | copy-start | bytes 6148
  289.8 6.6 slice-start.8
  408.2 11.2 %copy-start = (bf16[512,10,2,10,2,32]{0,5,4,2,3,1:T(8,128)(2,1)}, bf16[512,10,2,10,2,32]{0,5,4,2,3,1:T(8,128)(2,1)S(1)}, u32[]{:S(2)}) copy-start(bf16[512,10,2,10,2,32]{0,5,4,2,3,1:T(8,128)(2,1)S(1)} %copy.98) | copy-start | bytes 39321604
  449.6 5.8 slice-start.4
  449.6 5.8 slice-start.5
  477.5 3.8 copy-start.22
  477.5 4.1 copy-start.39
  502.3 2.3 copy-start.35
  502.3 2.9 copy-start.27
  502.3 3.0 copy-start.25
  502.3 3.0 copy-start.32
  502.3 6.3 copy-start.3
  506.6 4.9 slice-start.6
  508.6 2.9 slice-start.7
  592.8 39.5 %copy-start.1 = (bf16[512,9,9,64]{0,3,2,1:T(8,128)(2,1)}, bf16[512,9,9,64]{0,3,2,1:T(8,128)(2,1)S(1)}, u32[]{:S(2)}) copy-start(bf16[512,9,9,64]{0,3,2,1:T(8,128)(2,1)S(1)} %get-tuple-element.182) | copy-start | bytes 15925252
  592.8 14.8 %slice-start = ((s8[13107200]{0:T(1024)(128)(4,1)}), s8[4194304]{0:T(1024)(128)(4,1)S(1)}, s32[]{:S(2)}) async-start(s8[13107200]{0:T(1024)(128)(4,1)} %bitcast.492), calls=%async_computation.3 | async-start | bytes 8388608
  592.8 14.8 %slice-start.1 = ((s8[13107200]{0:T(1024)(128)(4,1)}), s8[4194304]{0:T(1024)(128)(4,1)S(1)}, s32[]{:S(2)}) async-start(s8[13107200]{0:T(1024)(128)(4,1)} %bitcast.492), calls=%async_computation.4 | async-start | bytes 8388608
  601.0 6.6 slice-start.2
  601.0 6.6 slice-start.3
  739.3 15.6 %copy-start.5 = (f32[512,19]{1,0:T(8,128)S(1)}, f32[512,19]{1,0:T(8,128)}, u32[]{:S(2)}) copy-start(f32[512,19]{1,0:T(8,128)} %fusion.57) | copy-start | bytes 116740
  739.3 15.8 %copy-start.19 = (f32[1,64,64]{2,1,0:T(8,128)S(1)}, f32[1,64,64]{2,1,0:T(8,128)}, u32[]{:S(2)}) copy-start(f32[1,64,64]{2,1,0:T(8,128)} %convolution_bitcast_fusion.1) | copy-start | bytes 49156
  739.3 15.8 %copy-start.20 = (f32[1,64,64]{2,1,0:T(8,128)S(1)}, f32[1,64,64]{2,1,0:T(8,128)}, u32[]{:S(2)}) copy-start(f32[1,64,64]{2,1,0:T(8,128)} %convolution_bitcast_fusion.2) | copy-start | bytes 49156
  739.3 15.8 %copy-start.21 = (f32[1,64,64]{2,1,0:T(8,128)S(1)}, f32[1,64,64]{2,1,0:T(8,128)}, u32[]{:S(2)}) copy-start(f32[1,64,64]{2,1,0:T(8,128)} %convolution_bitcast_fusion.3) | copy-start | bytes 49156
  739.3 15.8 %copy-start.13 = (f32[1,64,64]{2,1,0:T(8,128)S(1)}, f32[1,64,64]{2,1,0:T(8,128)}, u32[]{:S(2)}) copy-start(f32[1,64,64]{2,1,0:T(8,128)} %convolution_bitcast_fusion.4) | copy-start | bytes 49156
  739.4 15.8 %copy-start.14 = (f32[1,64,64]{2,1,0:T(8,128)S(1)}, f32[1,64,64]{2,1,0:T(8,128)}, u32[]{:S(2)}) copy-start(f32[1,64,64]{2,1,0:T(8,128)} %convolution_bitcast_fusion.5) | copy-start | bytes 49156
  739.4 15.8 %copy-start.15 = (f32[1,64,64]{2,1,0:T(8,128)S(1)}, f32[1,64,64]{2,1,0:T(8,128)}, u32[]{:S(2)}) copy-start(f32[1,64,64]{2,1,0:T(8,128)} %convolution_bitcast_fusion.6) | copy-start | bytes 49156
  739.4 15.8 %copy-start.16 = (f32[1,64,64]{2,1,0:T(8,128)S(1)}, f32[1,64,64]{2,1,0:T(8,128)}, u32[]{:S(2)}) copy-start(f32[1,64,64]{2,1,0:T(8,128)} %convolution_bitcast_fusion.7) | copy-start | bytes 49156
  739.4 15.8 %copy-start.17 = (f32[1,64,64]{2,1,0:T(8,128)S(1)}, f32[1,64,64]{2,1,0:T(8,128)}, u32[]{:S(2)}) copy-start(f32[1,64,64]{2,1,0:T(8,128)} %convolution_bitcast_fusion.8) | copy-start | bytes 49156
  739.4 15.8 %copy-start.18 = (f32[1,64,64]{2,1,0:T(8,128)S(1)}, f32[1,64,64]{2,1,0:T(8,128)}, u32[]{:S(2)}) copy-start(f32[1,64,64]{2,1,0:T(8,128)} %convolution_bitcast_fusion.9) | copy-start | bytes 49156
  755.4 7.3 copy-start.9
  755.4 7.3 copy-start.10
  755.4 7.3 copy-start.11
  755.4 7.3 copy-start.12
  755.4 7.9 copy-start.30
  755.4 7.9 copy-start.36
  755.5 7.9 copy-start.38
  755.5 7.9 copy-start.40
  825.4 149.2 %copy-start.2 = (f32[105984]{0:T(1024)S(1)}, f32[105984]{0:T(1024)}, u32[]{:S(2)}) copy-start(f32[105984]{0:T(1024)} %param.23) | copy-start | bytes 1271812
  825.5 151.4 %copy-start.23 = (f32[1,4,128]{2,1,0:T(4,128)S(1)}, f32[1,4,128]{2,1,0:T(4,128)}, u32[]{:S(2)}) copy-start(f32[1,4,128]{2,1,0:T(4,128)} %param.18) | copy-start | bytes 6148
  825.5 151.4 %copy-start.26 = (f32[128,4]{0,1:T(4,128)S(1)}, f32[128,4]{0,1:T(4,128)}, u32[]{:S(2)}) copy-start(f32[128,4]{0,1:T(4,128)} %copy-done.24) | copy-start | bytes 6148
  825.5 151.4 %copy-start.29 = (f32[512]{0:T(512)S(1)}, f32[512]{0:T(512)}, u32[]{:S(2)}) copy-start(f32[512]{0:T(512)} %copy-done.28) | copy-start | bytes 6148
  825.5 151.4 %copy-start.31 = (f32[512]{0:T(512)S(1)}, f32[512]{0:T(512)}, u32[]{:S(2)}) copy-start(f32[512]{0:T(512)} %get-tuple-element.141) | copy-start | bytes 6148
  825.5 151.4 %copy-start.33 = (f32[1,4,128]{2,1,0:T(4,128)S(1)}, f32[1,4,128]{2,1,0:T(4,128)}, u32[]{:S(2)}) copy-start(f32[1,4,128]{2,1,0:T(4,128)} %param.22) | copy-start | bytes 6148
  825.5 151.4 %copy-start.34 = (f32[512,1]{0,1:T(1,128)S(1)}, f32[512,1]{0,1:T(1,128)}, u32[]{:S(2)}) copy-start(f32[512,1]{0,1:T(1,128)} %get-tuple-element.169) | copy-start | bytes 6148
  825.5 189.1 %all-reduce.21.cloned.1.call-start = ((), (), s32[]{:S(2)}) async-start(), calls=%async_computation.1 | async-start | bytes 851968 | tf_op jit(solution)/shard_map/psum | solution.py:266
  829.1 185.6 %copy-start.6 = (f32[105984]{0:T(1024)S(1)}, f32[105984]{0:T(1024)}, u32[]{:S(2)}) copy-start(f32[105984]{0:T(1024)} %param.26) | copy-start | bytes 1271812
  (6 other events, 8.6 us)
Sparse Core Ops, SparseCore 0:
  10.7 67.2 all-gather.2
  825.6 143.8 all-reduce.18
  977.0 26.5 all-reduce.20
where the time goes:
time: 1040 us; the launch traced here: 1020 us
  matrix products  418 us (40%)
  local copies, waits for them, and re-layouts  253 us (24%)
  waiting for transfers between devices  140 us (13%)
  other arithmetic  119 us (11%)
  blocking collectives  70.6 us (7%)
  between operations  20.8 us (2%)
    dot_general x17, matrix products, shifted_conv(): jnp.einsum('bhwc,co->bhwo', window, kernel[vertical, lateral], preferred_...  197 us
    psum x1, waiting for transfers between devices, on_device(): summed, loss_total = lax.psum((grad_flat, loss_local), 'dp')  140 us
    dot_general x17, matrix products, kernel_grad(): jnp.einsum('bhwc,bhwo->co', window, upstream, preferred_element_type=jnp....  97.1 us
    all_gather x1, other arithmetic, on_device(): lax.all_gather(master.astype(jnp.bfloat16), 'dp', axis=0, tiled=True)  70.1 us
    pad x5, matrix products, input_grad(): jnp.pad(term, ((0, 0), (vertical, extent - inner_size - vertical), (later...  67.2 us
    concatenate x1, local copies, waits for them, and re-layouts, on_device(): jnp.concatenate([piece.reshape(-1) for piece in pieces] + [padding])  62 us
    another operation x1, local copies, waits for them, and re-layouts, on_device(): pixels = frames[0].reshape(batch, 21, 4, 21, 4, 4).transpose(0, 1, 3, 2,...  50.5 us
    reshape x1, local copies, waits for them, and re-layouts, on_device(): pixels = frames[0].reshape(batch, 21, 4, 21, 4, 4).transpose(0, 1, 3, 2,...  45.4 us
  transfers between devices with their start and end apart: 3, of which 1 were waited for; matrix products, arithmetic and copies ran while one was open for 15% of the time, Pallas kernels for 0%

commit v1 on v0

v1 whole, which is shorter than its diff:
```python
import math

import jax
import jax.numpy as jnp
from jax import lax
from jax.experimental import pallas as pl
from jax.experimental.pallas import tpu as pltpu
from jax.sharding import PartitionSpec as P

C1 = 32
C2 = 64
C3 = 64
HID = 512
ACTIONS = 18
PARAMS = 1693875
FEATURES = 49 * C3
CONV_LEN = 256 * C1 + C1 + 16 * C1 * C2 + C2 + 9 * C2 * C3 + C3
TOP = CONV_LEN // HID
PHASE = CONV_LEN % HID
HEAD_LEN = HID * (ACTIONS + 1) + ACTIONS + 1

BETA_ONE = 0.9
BETA_TWO = 0.999
ADAM_EPSILON = 1e-08
LEARN_RATE = 0.005
WEIGHT_DECAY = 0.01
CLIP_NORM = 0.5
OUTER_RATE = 0.7
OUTER_MOMENTUM = 0.9
DISCOUNT = 0.99
TRACE_DECAY = 0.95
RATIO_CLIP = 0.1
VALUE_COEF = 0.5
ENTROPY_COEF = 0.01

F32 = jnp.float32
BF16 = jnp.bfloat16
VMEM_LIMIT = 63 * 1024 * 1024


def mm(a, b):
    return jnp.dot(a, b, preferred_element_type=F32)


def mm_nt(a, b):
    return lax.dot_general(a, b, (((1,), (1,)), ((), ())), preferred_element_type=F32)


def mm_tn(a, b):
    return lax.dot_general(a, b, (((0,), (0,)), ((), ())), preferred_element_type=F32)


def trajectory_advantages(rewards, values, next_values, terminal, truncated):
    alive = 1.0 - terminal.astype(F32)
    cutoff = truncated.astype(F32)
    following = jnp.concatenate([values[:, 1:], next_values[:, -1:]], axis=1)
    following = cutoff * next_values + (1.0 - cutoff) * following
    deltas = rewards + DISCOUNT * alive * following - values
    keeping = DISCOUNT * TRACE_DECAY * alive * (1.0 - cutoff)

    def backward_step(carry, item):
        delta, keep = item
        result = delta + keep * carry
        return (result, result)

    start = jnp.zeros((rewards.shape[0],), F32)
    _, series = lax.scan(backward_step, start, (deltas.T, keeping.T), reverse=True)
    return series.T


def forward_body(x_ref, t1_ref, b1_ref, t2_ref, b2_ref, t3_ref, b3_ref, a1_ref, a2_ref, a3_ref):
    def conv_one(m, carry):
        for n in range(5):
            window = jnp.concatenate(
                [
                    x_ref[e, pl.ds(8 * m, 12), 64 * n : 64 * n + 80, :].reshape(960, 128)
                    for e in range(2)
                ],
                axis=1,
            )
            out = jnp.maximum(mm(t1_ref[...], window) + b1_ref[...], 0.0).astype(BF16)
            a1_ref[pl.ds(2 * m, 2), 4 * n : 4 * n + 4] = out.reshape(2, 4, C1, 256)
        return carry

    lax.fori_loop(0, 10, conv_one, 0)

    def conv_two(p, carry):
        for g in range(3):
            window = a1_ref[pl.ds(2 * p, 4), 6 * g : 6 * g + 8].reshape(1024, 256)
            out = jnp.maximum(mm(t2_ref[...], window) + b2_ref[...], 0.0).astype(BF16)
            a2_ref[p, 3 * g : 3 * g + 3] = out.reshape(3, C2, 256)
        a2_ref[p, 9] = jnp.zeros((C2, 256), BF16)
        return carry

    lax.fori_loop(0, 9, conv_two, 0)

    def conv_three(p, carry):
        window = a2_ref[pl.ds(p, 3), 0:9].reshape(1728, 256)
        out = jnp.maximum(mm(t3_ref[...], window) + b3_ref[...], 0.0).astype(BF16)
        a3_ref[p] = out.reshape(7, C3, 256)
        return carry

    lax.fori_loop(0, 7, conv_three, 0)


def whole(shape):
    return pl.BlockSpec(shape, lambda j: (0,) * len(shape), pipeline_mode=pl.Buffered(1))


def conv_forward(x, t1, b1, t2, b2, t3, b3):
    envs = x.shape[0]
    frames = envs * 128
    return pl.pallas_call(
        forward_body,
        grid=(envs // 2,),
        in_specs=[
            pl.BlockSpec((2, 84, 336, 128), lambda j: (j, 0, 0, 0)),
            whole((256, 960)),
            whole((256, 256)),
            whole((192, 1024)),
            whole((192, 256)),
            whole((448, 1728)),
            whole((448, 256)),
        ],
        out_specs=[
            pl.BlockSpec((20, 20, C1, 256), lambda j: (0, 0, 0, j)),
            pl.BlockSpec((9, 10, C2, 256), lambda j: (0, 0, 0, j)),
            pl.BlockSpec((7, 7, C3, 256), lambda j: (0, 0, 0, j)),
        ],
        out_shape=[
            jax.ShapeDtypeStruct((20, 20, C1, frames), BF16),
            jax.ShapeDtypeStruct((9, 10, C2, frames), BF16),
            jax.ShapeDtypeStruct((7, 7, C3, frames), BF16),
        ],
        compiler_params=pltpu.CompilerParams(vmem_limit_bytes=VMEM_LIMIT),
        name="conv_forward",
    )(x, t1, b1, t2, b2, t3, b3)


def dense_body(
    scale,
    a3_ref,
    wd_ref,
    bd_ref,
    wh_ref,
    bh_ref,
    normed_ref,
    returns_ref,
    actions_ref,
    behavior_ref,
    gwd_ref,
    dc3_ref,
    gbd_ref,
    gwh_ref,
    gbh_ref,
    loss_ref,
):
    hidden_pre = mm_tn(wd_ref[...], a3_ref[...]) + bd_ref[...]
    hidden = jnp.maximum(hidden_pre, 0.0).astype(BF16)
    out = mm(wh_ref[...], hidden) + bh_ref[...]
    row = lax.broadcasted_iota(jnp.int32, out.shape, 0)
    is_logit = row < ACTIONS
    logits = jnp.where(is_logit, out, -jnp.inf)
    top = jnp.max(logits, axis=0, keepdims=True)
    shifted = out - top
    exps = jnp.where(is_logit, jnp.exp(shifted), 0.0)
    total = jnp.sum(exps, axis=0, keepdims=True)
    log_probs = jnp.where(is_logit, shifted - jnp.log(total), 0.0)
    probs = jnp.where(is_logit, jnp.exp(log_probs), 0.0)
    value = jnp.sum(jnp.where(row == ACTIONS, out, 0.0), axis=0, keepdims=True)
    normed = normed_ref[...]
    chosen = row == actions_ref[...]
    taken = jnp.sum(jnp.where(chosen, log_probs, 0.0), axis=0, keepdims=True)
    ratio = jnp.exp(taken - behavior_ref[...])
    low = 1.0 - RATIO_CLIP
    high = 1.0 + RATIO_CLIP
    clipped = jnp.clip(ratio, low, high)
    plain = ratio * normed
    cut = clipped * normed
    entropy = -jnp.sum(probs * log_probs, axis=0, keepdims=True)
    error = value - returns_ref[...]
    losses = -jnp.minimum(plain, cut) + 0.5 * VALUE_COEF * error * error - ENTROPY_COEF * entropy
    loss_ref[...] = jnp.sum(losses, axis=1, keepdims=True) * scale
    plain_share = jnp.where(plain < cut, 1.0, jnp.where(plain == cut, 0.5, 0.0))
    inside = jnp.where(
        (ratio > low) & (ratio < high), 1.0, jnp.where((ratio == low) | (ratio == high), 0.5, 0.0)
    )
    d_taken = -scale * normed * ratio * (plain_share + (1.0 - plain_share) * inside)
    d_logits = d_taken * (jnp.where(chosen, 1.0, 0.0) - probs) + (scale * ENTROPY_COEF) * probs * (
        log_probs + entropy
    )
    d_value = scale * VALUE_COEF * error
    d_out = jnp.where(is_logit, d_logits, jnp.where(row == ACTIONS, d_value, 0.0)).astype(BF16)
    gwh_ref[...] = mm_nt(d_out, hidden)
    gbh_ref[...] = jnp.sum(d_out.astype(F32), axis=1, keepdims=True)
    back = mm_tn(wh_ref[...], d_out)
    d_hidden = jnp.where(hidden_pre > 0, back, 0.0).astype(BF16)
    gbd_ref[...] = jnp.sum(d_hidden.astype(F32), axis=1, keepdims=True)
    gwd_ref[...] = mm_nt(a3_ref[...], d_hidden)
    d_a3 = mm(wd_ref[...], d_hidden)
    dc3_ref[...] = jnp.where(a3_ref[...] > 0, d_a3, 0.0).astype(BF16)


def dense_step(scale, a3, wd, bd, wh, bh, normed, returns, actions, behavior):
    frames = a3.shape[1]
    rows = wh.shape[0]
    return pl.pallas_call(
        lambda *refs: dense_body(scale, *refs),
        out_shape=[
            jax.ShapeDtypeStruct((FEATURES, HID), F32),
            jax.ShapeDtypeStruct((FEATURES, frames), BF16),
            jax.ShapeDtypeStruct((HID, 1), F32),
            jax.ShapeDtypeStruct((rows, HID), F32),
            jax.ShapeDtypeStruct((rows, 1), F32),
            jax.ShapeDtypeStruct((1, 1), F32),
        ],
        compiler_params=pltpu.CompilerParams(vmem_limit_bytes=VMEM_LIMIT),
        name="dense_step",
    )(a3, wd, bd, wh, bh, normed, returns, actions, behavior)


def backward_body(
    x_hbm,
    a1_hbm,
    a2_ref,
    dc3_ref,
    t3_ref,
    t2_ref,
    r1_ref,
    r2_ref,
    r3_ref,
    s1_ref,
    s2_ref,
    s3_ref,
    x_ref,
    a1_ref,
    d3_ref,
    d2_ref,
    d1_ref,
    sems,
):
    step = pl.program_id(0)
    load_x = pltpu.make_async_copy(x_hbm.at[pl.ds(2 * step, 2)], x_ref, sems.at[0])
    lanes = pl.ds(pl.multiple_of(256 * step, 256), 256)
    load_a1 = pltpu.make_async_copy(a1_hbm.at[:, :, :, lanes], a1_ref, sems.at[1])
    load_a1.start()
    load_x.start()

    @pl.when(step == 0)
    def _():
        for ref in (r1_ref, r2_ref, r3_ref, s1_ref, s2_ref, s3_ref):
            ref[...] = jnp.zeros(ref.shape, F32)
        for p in (0, 1, 9, 10):
            d3_ref[p] = jnp.zeros((8, C3, 256), BF16)
        for p in (0, 10):
            d2_ref[p] = jnp.zeros((11, C2, 256), BF16)

        def edge(p, carry):
            d2_ref[p, 0] = jnp.zeros((C2, 256), BF16)
            d2_ref[p, 10] = jnp.zeros((C2, 256), BF16)
            return carry

        lax.fori_loop(1, 10, edge, 0)

    def fill(p, carry):
        d3_ref[p + 2, 0:7] = dc3_ref[p]
        d3_ref[p + 2, 7] = jnp.zeros((C3, 256), BF16)
        s3_ref[...] += jnp.sum(dc3_ref[p].astype(F32), axis=0)
        return carry

    lax.fori_loop(0, 7, fill, 0)

    def three_weights(p, carry):
        left = mm_nt(a2_ref[pl.ds(p, 3), 0:6].reshape(1152, 256), d3_ref[p + 2, 0:4].reshape(256, 256))
        right = mm_nt(
            a2_ref[pl.ds(p, 3), 4:10].reshape(1152, 256), d3_ref[p + 2, 4:8].reshape(256, 256)
        )
        r3_ref[...] += left + right
        return carry

    lax.fori_loop(0, 7, three_weights, 0)

    def three_input(y, carry):
        back = mm(t3_ref[...], d3_ref[pl.ds(y, 3)].reshape(1536, 256)).reshape(9, C2, 256)
        masked = jnp.where(a2_ref[y, 0:9] > 0, back, 0.0).astype(BF16)
        d2_ref[y + 1, 1:10] = masked
        s2_ref[...] += jnp.sum(masked.astype(F32), axis=0)
        return carry

    lax.fori_loop(0, 9, three_input, 0)
    load_a1.wait()

    def two_weights(p, carry):
        total = 0.0
        for g in range(3):
            total = total + mm_nt(
                a1_ref[pl.ds(2 * p, 4), 6 * g : 6 * g + 8].reshape(1024, 256),
                d2_ref[p + 1, 1 + 3 * g : 4 + 3 * g].reshape(192, 256),
            )
        r2_ref[...] += total
        return carry

    lax.fori_loop(0, 9, two_weights, 0)
    load_x.wait()

    def one_weights(m, carry):
        total = 0.0
        sums = jnp.zeros((C1, 256), F32)
        for n in range(5):
            back = mm(t2_ref[...], d2_ref[pl.ds(m, 2), 2 * n : 2 * n + 3].reshape(384, 256))
            kept = a1_ref[pl.ds(2 * m, 2), 4 * n : 4 * n + 4].reshape(256, 256) > 0
            masked = jnp.where(kept, back, 0.0).astype(BF16)
            sums = sums + jnp.sum(masked.astype(F32).reshape(8, C1, 256), axis=0)
            window = jnp.concatenate(
                [
                    x_ref[e, pl.ds(8 * m, 12), 64 * n : 64 * n + 80, :].reshape(960, 128)
                    for e in range(2)
                ],
                axis=1,
            )
            total = total + mm_nt(window, masked)
        r1_ref[...] += total
        s1_ref[...] += sums
        return carry

    lax.fori_loop(0, 10, one_weights, 0)


def conv_backward(x, a1, a2, dc3, t3, t2):
    envs = x.shape[0]
    sums = [(960, 256), (1024, 192), (1152, 256), (C1, 256), (C2, 256), (C3, 256)]
    return pl.pallas_call(
        backward_body,
        grid=(envs // 2,),
        in_specs=[
            pl.BlockSpec(memory_space=pl.ANY),
            pl.BlockSpec(memory_space=pl.ANY),
            pl.BlockSpec((9, 10, C2, 256), lambda j: (0, 0, 0, j)),
            pl.BlockSpec((7, 7, C3, 256), lambda j: (0, 0, 0, j)),
            whole((576, 1536)),
            whole((256, 384)),
        ],
        out_specs=[whole(shape) for shape in sums],
        out_shape=[jax.ShapeDtypeStruct(shape, F32) for shape in sums],
        scratch_shapes=[
            pltpu.VMEM((2, 84, 336, 128), BF16),
            pltpu.VMEM((20, 20, C1, 256), BF16),
            pltpu.VMEM((11, 8, C3, 256), BF16),
            pltpu.VMEM((11, 11, C2, 256), BF16),
            pltpu.VMEM((8, 128), F32),
            pltpu.SemaphoreType.DMA((2,)),
        ],
        compiler_params=pltpu.CompilerParams(vmem_limit_bytes=VMEM_LIMIT),
        name="conv_backward",
    )(x, a1, a2, dc3, t3, t2)


def forward_weights(w_one, w_two, w_three):
    base = w_one.reshape(8, 32, C1).transpose(2, 0, 1)
    t1 = jnp.stack(
        [
            jnp.pad(base, ((0, 0), (4 * i, 4 - 4 * i), (16 * j, 48 - 16 * j)))
            for i in range(2)
            for j in range(4)
        ]
    ).reshape(256, 960)
    base = w_two.reshape(4, 4 * C1, C2).transpose(2, 0, 1)
    t2 = jnp.stack(
        [jnp.pad(base, ((0, 0), (0, 0), (64 * j, 128 - 64 * j))) for j in range(3)]
    ).reshape(192, 1024)
    base = w_three.reshape(3, 3 * C2, C3).transpose(2, 0, 1)
    t3 = jnp.stack(
        [jnp.pad(base, ((0, 0), (0, 0), (64 * j, 384 - 64 * j))) for j in range(7)]
    ).reshape(448, 1728)
    return t1, t2, t3


def backward_weights(w_two, w_three):
    zero = jnp.zeros((), BF16)
    base = w_three[::-1, ::-1].transpose(2, 0, 1, 3).reshape(C2, 3, 3 * C3)
    t3 = jnp.stack(
        [
            lax.pad(base, zero, ((0, 0, 0), (0, 0, 0), (64 * (x - 2), 512 - 192 - 64 * (x - 2), 0)))
            for x in range(9)
        ]
    ).reshape(576, 1536)
    empty = jnp.zeros((C1, C2), BF16)
    blocks = []
    for dy in range(2):
        for dx in range(4):
            line = []
            for r in range(2):
                for s in range(3):
                    j = dx + 2 - 2 * s
                    line.append(w_two[dy + 2 - 2 * r, j] if 0 <= j < 4 else empty)
            blocks.append(jnp.concatenate(line, axis=1))
    return t3, jnp.concatenate(blocks, axis=0)


def conv_gradients(r1, r2, r3):
    r1 = r1.reshape(12, 80, 2, 4, C1)
    g1 = 0.0
    for i in range(2):
        for j in range(4):
            g1 = g1 + r1[4 * i : 4 * i + 8, 16 * j : 16 * j + 32, i, j]
    r2 = r2.reshape(4, 8, C1, 3, C2)
    g2 = 0.0
    for j in range(3):
        g2 = g2 + r2[:, 2 * j : 2 * j + 4, :, j]
    r3 = r3.reshape(3, 6, C2, 4, C3)
    g3 = 0.0
    for j in range(4):
        g3 = g3 + r3[:, j : j + 3, :, j]
    return g1, g2, g3


def on_device(
    frames,
    actions,
    rewards,
    old_values,
    next_values,
    terminal,
    truncated,
    behavior_logprob,
    master,
    first_moment,
    second_moment,
    outer_momentum,
    step_count,
):
    lanes = lax.axis_size("dp")
    place = lax.axis_index("dp")
    shard_len = master.shape[0]
    rows = shard_len // HID
    gathered = lax.all_gather(master.reshape(rows, HID).astype(BF16), "dp", axis=0)
    gathered = gathered.reshape(lanes * rows, HID)

    advantage = trajectory_advantages(
        rewards[0], old_values[0], next_values[0], terminal[0], truncated[0]
    )
    envs_here, steps_here = advantage.shape
    batch = envs_here * steps_here
    total_frames = batch * lanes
    first_sum, square_sum = lax.psum((jnp.sum(advantage), jnp.sum(advantage * advantage)), "dp")
    mean = first_sum / total_frames
    spread = square_sum / total_frames - mean * mean
    normed = ((advantage - mean) * lax.rsqrt(spread + 1e-05)).reshape(1, batch)
    returns = (advantage + old_values[0]).reshape(1, batch)

    column = lax.broadcasted_iota(jnp.int32, (1, HID), 1)
    late = column >= PHASE
    conv_flat = gathered[: TOP + 1].reshape(-1)
    offset = 0
    pieces = []
    for shape in ((8, 8, 4, C1), (C1,), (4, 4, C1, C2), (C2,), (3, 3, C2, C3), (C3,)):
        length = math.prod(shape)
        pieces.append(conv_flat[offset : offset + length].reshape(shape))
        offset += length
    w_one, b_one, w_two, b_two, w_three, b_three = pieces
    w_dense = jnp.where(
        late, gathered[TOP : TOP + FEATURES], gathered[TOP + 1 : TOP + 1 + FEATURES]
    )
    b_dense = jnp.where(
        late[0], gathered[TOP + FEATURES], gathered[TOP + 1 + FEATURES]
    ).astype(F32)
    tail = TOP + FEATURES + 1
    head_flat = gathered[tail:].reshape(-1)[PHASE : PHASE + HEAD_LEN]
    w_head = head_flat[: HID * (ACTIONS + 1)].reshape(HID, ACTIONS + 1)
    w_head = jnp.pad(jnp.roll(w_head, PHASE, axis=0).T, ((0, 13), (0, 0)))
    b_head = jnp.pad(head_flat[HID * (ACTIONS + 1) :], (0, 13)).astype(F32)

    x = frames[0].transpose(0, 2, 3, 1)
    t1, t2, t3 = forward_weights(w_one, w_two, w_three)

    def spread_bias(bias, count):
        bias = jnp.tile(bias.astype(F32), count)
        return jnp.broadcast_to(bias[:, None], (bias.shape[0], 256))

    a1, a2, a3 = conv_forward(
        x, t1, spread_bias(b_one, 8), t2, spread_bias(b_two, 3), t3, spread_bias(b_three, 7)
    )
    g_dense, d_c3, g_dense_bias, g_head, g_head_bias, loss_local = dense_step(
        1.0 / total_frames,
        a3.reshape(FEATURES, batch),
        w_dense,
        b_dense[:, None],
        w_head,
        b_head[:, None],
        normed,
        returns,
        actions[0].reshape(1, batch),
        behavior_logprob[0].reshape(1, batch),
    )
    total_rows = lanes * rows
    extended = jnp.concatenate([g_dense, g_dense_bias.reshape(1, HID)], axis=0)
    spare = total_rows - TOP - FEATURES - 1
    dense_rows = jnp.where(
        late,
        jnp.pad(extended, ((TOP, spare), (0, 0))),
        jnp.pad(extended, ((TOP + 1, spare - 1), (0, 0))),
    )
    dense_owned = lax.psum_scatter(
        dense_rows.reshape(lanes, rows, HID), "dp", scatter_dimension=0, tiled=False
    )

    back3, back2 = backward_weights(w_two, w_three)
    r1, r2, r3, s1, s2, s3 = conv_backward(x, a1, a2, d_c3.reshape(7, 7, C3, batch), back3, back2)
    g1, g2, g3 = conv_gradients(r1, r2, r3)
    small = jnp.concatenate(
        [
            g1.reshape(-1),
            jnp.sum(s1, axis=1),
            g2.reshape(-1),
            jnp.sum(s2, axis=1),
            g3.reshape(-1),
            jnp.sum(s3, axis=1),
            jnp.roll(g_head[: ACTIONS + 1].T, -PHASE, axis=0).reshape(-1),
            g_head_bias[: ACTIONS + 1, 0],
            loss_local.reshape(-1),
        ]
    )
    small = lax.psum(small, "dp")
    loss_total = small[CONV_LEN + HEAD_LEN]
    top_blocks = -(-(TOP + 1) // rows)
    top_part = jnp.pad(small[:CONV_LEN], (0, top_blocks * shard_len - CONV_LEN))
    tail_start = tail * HID + PHASE
    tail_block = tail_start // shard_len
    tail_part = jnp.pad(
        small[CONV_LEN : CONV_LEN + HEAD_LEN],
        (
            tail_start - tail_block * shard_len,
            lanes * shard_len - tail_start - HEAD_LEN,
        ),
    )

    def own_block(part, first):
        blocks = part.shape[0] // shard_len
        here = (place >= first) & (place < first + blocks)
        start = jnp.clip(place - first, 0, blocks - 1) * shard_len
        return jnp.where(here, lax.dynamic_slice_in_dim(part, start, shard_len, 0), 0.0)

    owned = dense_owned.reshape(-1) + own_block(top_part, 0) + own_block(tail_part, tail_block)
    norm = jnp.sqrt(lax.psum(jnp.sum(owned * owned), "dp"))
    factor = jnp.minimum(1.0, CLIP_NORM / (norm + 1e-06))
    clipped = owned * factor
    moment_step = step_count[0].astype(F32)
    first_next = BETA_ONE * first_moment[0] + (1.0 - BETA_ONE) * clipped
    second_next = BETA_TWO * second_moment[0] + (1.0 - BETA_TWO) * clipped * clipped
    first_hat = first_next / (1.0 - jnp.power(BETA_ONE, moment_step))
    second_hat = second_next / (1.0 - jnp.power(BETA_TWO, moment_step))
    inner = master - LEARN_RATE * (
        first_hat / (jnp.sqrt(second_hat) + ADAM_EPSILON) + WEIGHT_DECAY * master
    )
    moved = lax.psum(master - inner, "group") / lax.axis_size("group")
    momentum_next = OUTER_MOMENTUM * outer_momentum + moved
    final = master - OUTER_RATE * (moved + OUTER_MOMENTUM * momentum_next)
    return (
        clipped[None],
        norm.reshape(1),
        loss_total.reshape(1),
        first_next[None],
        second_next[None],
        moved,
        momentum_next,
        final,
        final.astype(BF16),
    )


def solution(mesh):
    return jax.shard_map(
        on_device,
        mesh=mesh,
        in_specs=(
            P("group", "dp", None, None, None),
            P("group", "dp", None),
            P("group", "dp", None),
            P("group", "dp", None),
            P("group", "dp", None),
            P("group", "dp", None),
            P("group", "dp", None),
            P("group", "dp", None),
            P("dp"),
            P("group", "dp"),
            P("group", "dp"),
            P("dp"),
            P(),
        ),
        out_specs=(
            P("group", "dp"),
            P("group"),
            P("group"),
            P("group", "dp"),
            P("group", "dp"),
            P("dp"),
            P("dp"),
            P("dp"),
            P("dp"),
        ),
        check_vma=False,
    )
```

time: 1040 us -> 544 us (0.52); the launches traced: 1020 us -> 542 us
  matrix products: 418 us -> 0 us
  local copies, waits for them, and re-layouts: 253 us -> 109 us
  Pallas kernels: 0 us -> 128 us
  other arithmetic: 119 us -> 33.5 us
  waiting for transfers between devices: 140 us -> 182 us
    dot_general x48 -> x0, matrix products: 351 us -> none  [the longest x17 197 us: shifted_conv(): jnp.einsum('bhwc,co->bhwo', window, kernel[vertical, lateral], preferred_...]
    pallas_call x0 -> x3, Pallas kernels: none -> 128 us  [the longest x1 73 us: conv_backward(): pl.pallas_call(backward_body, grid=(envs // 2,), in_specs=[pl.BlockSpec(m...]
    reduce_scatter x0 -> x1, waiting for transfers between devices: none -> 91.1 us  [on_device(): lax.psum_scatter(dense_rows.reshape(lanes, rows, HID), 'dp', scatter_dime...]
    all_gather x1 -> x0, other arithmetic: 70.1 us -> none  [on_device(): lax.all_gather(master.astype(jnp.bfloat16), 'dp', axis=0, tiled=True)]
    psum x1, waiting for transfers between devices: 140 us -> 71.2 us  [on_device(): small = lax.psum(small, 'dp')]
    pad x5 -> x0, matrix products: 67.2 us -> none  [input_grad(): jnp.pad(term, ((0, 0), (vertical, extent - inner_size - vertical), (later...]
    concatenate x1 -> x11, local copies, waits for them, and re-layouts: 62 us -> 9.42 us  [the longest x1 8.48 us: on_device(): jnp.concatenate([g1.reshape(-1), jnp.sum(s1, axis=1), g2.reshape(-1), jnp...]
    reshape x8 -> x12, local copies, waits for them, and re-layouts: 61.8 us -> 22.9 us  [the longest x1 5.46 us: forward_weights(): t3 = jnp.stack([jnp.pad(base, ((0, 0), (0, 0), (64 * j, 384 - 64 * j))) f...]
  transfers between devices with their start and end apart: 3 -> 4, of which waited for: 1 -> 3; matrix products, arithmetic and copies ran while one was open for 15% -> 6% of each run, Pallas kernels for 0% -> 0%
where the time goes in v1:
time: 544 us; the launch traced here: 542 us
  waiting for transfers between devices  182 us (33%)
  Pallas kernels  128 us (24%)
  local copies, waits for them, and re-layouts  109 us (20%)
  blocking collectives  67.4 us (12%)
  other arithmetic  33.5 us (6%)
  between operations  19.5 us (4%)
    reduce_scatter x1, waiting for transfers between devices, on_device(): lax.psum_scatter(dense_rows.reshape(lanes, rows, HID), 'dp', scatter_dime...  91.1 us
    pallas_call x1, Pallas kernels, conv_backward(): pl.pallas_call(backward_body, grid=(envs // 2,), in_specs=[pl.BlockSpec(m...  73 us
    psum x1, waiting for transfers between devices, on_device(): small = lax.psum(small, 'dp')  71.2 us
    pallas_call x1, Pallas kernels, conv_forward(): pl.pallas_call(forward_body, grid=(envs // 2,), in_specs=[pl.BlockSpec((2...  44.3 us
    psum x1, blocking collectives, on_device(): lax.psum((jnp.sum(advantage), jnp.sum(advantage * advantage)), 'dp')  36 us
    psum x1, blocking collectives, on_device(): norm = jnp.sqrt(lax.psum(jnp.sum(owned * owned), 'dp'))  31.4 us
    unnamed x70, local copies, waits for them, and re-layouts  21.4 us
    psum x1, waiting for transfers between devices, on_device(): moved = lax.psum(master - inner, 'group') / lax.axis_size('group')  19.5 us
  transfers between devices with their start and end apart: 4, of which 3 were waited for; matrix products, arithmetic and copies ran while one was open for 6% of the time, Pallas kernels for 0%

profile of v1, /device:TPU:0, one launch (start us, length us, event | category | flops | bytes accessed | tf_op | source)
XLA Modules:
  0.0 542.0 jit_solution(13044583626759689297)
XLA Ops:
  7.2 1.0 convert_element_type.98
  11.7 9.6 %while.17 = (s32[]{:T(128)}, f32[4]{0:T(128)S(1)}, f32[128,4]{1,0:T(8,128)S(1)}, f32[128,4]{1,0:T(8,128)S(1)}, f32[128,4]{1,0:T(8,128)S(1)}, /*index=5*/s32[]{:T(128)}, s32[]{:T(128)}, s32[]{:T(128)}) while((s32[]{:T(128)}, f32[4]{0:T(128)S(1)}, f32[128,4]{1,0:T(8,128)S(1)}, f32[128,4]{1,0:T(8,128)S(1)}, f32[128,4]{1,0:T(8,128)S(1)}, ...), condition=%wide.region_1.2_spmd.clone, body=%wide.region_0.1_spmd.clone.sunk | while | flops 16 | bytes 211 | solution.py:67
  22.1 1.9 bitcast_add_fusion
  23.9 36.0 %all-reduce.33 = (f32[]{:T(128)}, f32[]{:T(128)}) all-reduce(f32[]{:T(128)} %get-tuple-element.212, f32[]{:T(128)} %reduce_sum.54), channel_id=1, replica_groups=mesh['group'=2,'dp'=16] {'dp'}, use_global_device_ids=true, to_apply=%region_5.6 | all-reduce | flops 2 | bytes 16 | tf_op jit(solution)/shard_map/psum | solution.py:445
  63.7 2.5 reshape.192
  67.6 1.6 slice.268
  69.2 1.6 slice.266
  70.8 1.3 slice_convert_fusion
  72.2 1.2 slice_convert_fusion.2
  75.4 1.0 reshape_reshape.11
  82.0 6.2 %copy.72 = bf16[7,64,3,576]{3,2,1,0:T(4,128)(2,1)} copy(bf16[7,64,3,576]{1,3,2,0:T(8,128)(2,1)} %bitcast_dynamic-update-slice_fusion) | data formatting | bytes 3096576 | tf_op jit(solution)/shard_map/stack | solution.py:372
  88.3 5.5 %reshape.196.t3_ref = bf16[448,1728]{1,0:T(8,128)(2,1)} reshape(bf16[7,64,3,576]{3,2,1,0:T(4,128)(2,1)} %copy.72) | data formatting | bytes 3096576 | tf_op jit(solution)/shard_map/reshape | solution.py:374
  101.3 2.7 reshape.193.t1_ref
  104.8 1.2 pad_bitcast_fusion.2
  106.0 1.1 pad_maximum_fusion.1
  107.1 2.2 copy.71
  109.3 1.8 copy.86
  115.2 1.0 copy.76
  116.5 1.5 copy.73
  120.2 3.3 slice_select_fusion.refs_1_
  127.4 44.3 %conv_forward.1 = (bf16[20,20,32,512]{3,2,1,0:T(8,128)(2,1)}, bf16[9,10,64,512]{3,2,1,0:T(8,128)(2,1)}, bf16[7,7,64,512]{3,2,1,0:T(8,128)(2,1)}) custom-call(bf16[4,84,336,128]{3,2,1,0:T(8,128)(2,1)} %bitcast.184, bf16[256,960]{1,0:T(8,128)(2,1)} %reshape.193.t1_ref, f32[256,256]{1,0:T(8,128)} %broadcast_in_dim.75.b1_ref, bf16[192,1024]{1,0:T(8,128)(2,1)} %bitcast.214, ...), custom_call_target="tpu_custom_call" | custom-call | tf_op jit(solution)/shard_map/conv_forward/pallas_call | solution.py:113
  171.7 11.2 %dense_step.1 = (f32[3136,512]{1,0:T(8,128)}, bf16[3136,512]{1,0:T(8,128)(2,1)}, f32[512,1]{1,0:T(8,128)}, f32[32,512]{1,0:T(8,128)}, f32[32,1]{1,0:T(8,128)}, /*index=5*/f32[1,1]{1,0:T(1,128)}) custom-call(bf16[3136,512]{1,0:T(8,128)(2,1)} %bitcast.213, bf16[3136,512]{1,0:T(8,128)(2,1)} %slice_select_fusion.refs_1_, f32[512,1]{1,0:T(8,128)} %fusion.12.refs_2_, ...), custom_call_target="tpu_custom_call" | custom-call | tf_op jit(solution)/shard_map/dense_step/pallas_call | solution.py:207
  192.6 4.7 copy.82
  197.3 1.9 copy.87
  200.0 73.0 %conv_backward.1 = (f32[960,256]{1,0:T(8,128)}, f32[1024,192]{1,0:T(8,128)}, f32[1152,256]{1,0:T(8,128)}, f32[32,256]{1,0:T(8,128)}, f32[64,256]{1,0:T(8,128)}, /*index=5*/f32[64,256]{1,0:T(8,128)}) custom-call(bf16[4,84,336,128]{3,2,1,0:T(8,128)(2,1)} %bitcast.185, bf16[20,20,32,512]{3,2,1,0:T(8,128)(2,1)} %get-tuple-element.131.a1_hbm, ...), custom_call_target="tpu_custom_call" | custom-call | tf_op jit(solution)/shard_map/conv_backward/pallas_call | solution.py:332
  273.0 1.5 copy.83
  274.6 1.1 reshape.208
  276.2 2.2 reshape.210
  278.4 1.4 fusion.9
  279.9 2.5 reshape.209
  282.4 1.1 fusion.10
  284.1 8.5 %concatenate.57 = f32[87732]{0:T(1024)} concatenate(f32[8192]{0:T(1024)S(1)} %reshape.217, f32[32]{0:T(128)S(1)} %reduce_sum.56, f32[32768]{0:T(1024)S(1)} %add.225, f32[64]{0:T(128)S(1)} %reduce_sum.57, f32[36864]{0:T(1024)S(1)} %add.229, f32[64]{0:T(128)S(1)} %reduce_sum.58, f32[9728]{0:T(1024)S(1)} %reshape.211, f32[19]{0:T(128)S(1)} %slice_reduce_fusion, f32[1]{0:T(128)} %bitcast.71), dimensions={0} | concatenate | bytes 701856 | tf_op jit(solution)/shard_map/concatenate | solution.py:510
  292.8 3.6 pad_maximum_fusion
  296.4 3.6 pad_select_fusion
  299.9 5.2 reshape.202
  306.3 2.6 multiply_reduce_fusion.1
  308.9 71.2 %all-reduce.37.cloned.1.call-done = f32[87732]{0:T(1024)} async-done(((f32[87732]{0:T(1024)}), f32[87732]{0:T(1024)}) %all-reduce.37.cloned.1.call-update) | async-done | bytes 350944 | tf_op jit(solution)/shard_map/psum | solution.py:523
  380.1 1.0 slice.311
  381.9 91.1 %reduce-scatter.2.cloned.1.call-done = f32[1,207,512]{2,1,0:T(8,128)} async-done(((f32[16,207,512]{2,1,0:T(8,128)}), f32[1,207,512]{2,1,0:T(8,128)}) %reduce-scatter.2.cloned.1.call-update) | async-done | bytes 423952 | tf_op jit(solution)/shard_map/reduce_scatter | solution.py:503
  473.0 1.0 reshape_reduce_scatter.3
  474.8 31.4 %psum.38 = f32[]{:T(128)} all-reduce(f32[]{:T(128)} %multiply_reduce_fusion), channel_id=1, replica_groups=mesh['group'=2,'dp'=16] {'dp'}, use_global_device_ids=true, to_apply=%region_12.13 | all-reduce | flops 1 | bytes 8 | tf_op jit(solution)/shard_map/psum | solution.py:544
  506.9 1.1 subtract_subtract_fusion
  508.1 1.3 slice.313
  509.4 1.0 broadcast_in_dim.86
  510.4 1.0 broadcast_in_dim.87
  511.5 1.0 broadcast_in_dim.88
  512.5 19.5 %all-reduce.39.cloned.1.call-done = f32[105984]{0:T(1024)} async-done(((f32[105984]{0:T(1024)}), f32[105984]{0:T(1024)}) %all-reduce.39.cloned.1.call-update) | async-done | bytes 423952 | tf_op jit(solution)/shard_map/psum | solution.py:555
  532.0 2.3 fusion.21
  (409 shorter events, 54.4 us)
Async XLA Ops:
  7.2 56.6 %all-gather.2.cloned.1.call-start = ((), (), s32[]{:S(2)}) async-start(), calls=%async_computation.1 | async-start | bytes 3620864 | tf_op jit(solution)/shard_map/all_gather | solution.py:436
  9.1 371.0 %all-reduce.37.cloned.1.call-start = ((), (), s32[]{:S(2)}) async-start(), calls=%async_computation.3 | async-start | bytes 704512 | tf_op jit(solution)/shard_map/psum | solution.py:523
  82.0 11.7 %copy-start.9 = (bf16[16,512]{1,0:T(8,128)(2,1)S(1)}, bf16[16,512]{1,0:T(8,128)(2,1)}, u32[]{:S(2)}) copy-start(bf16[16,512]{1,0:T(8,128)(2,1)} %slice.263) | copy-start | bytes 49156
  88.3 15.8 %copy-start.2 = (bf16[32768]{0:T(1024)(128)(2,1)S(1)}, bf16[32768]{0:T(1024)(128)(2,1)}, u32[]{:S(2)}) copy-start(bf16[32768]{0:T(1024)(128)(2,1)} %slice.266) | copy-start | bytes 196612
  99.8 16.4 %copy-start.13 = (bf16[3040]{0:T(1024)(128)(2,1)S(1)}, bf16[3040]{0:T(1024)(128)(2,1)}, u32[]{:S(2)}) copy-start(bf16[3040]{0:T(1024)(128)(2,1)} %slice.275) | copy-start | bytes 18244
  100.6 17.4 %copy-start.15 = (bf16[512,1]{0,1:T(2,128)(2,1)S(1)}, bf16[512,1]{0,1:T(2,128)(2,1)}, u32[]{:S(2)}) copy-start(bf16[512,1]{0,1:T(2,128)(2,1)} %get-tuple-element.186) | copy-start | bytes 3076
  120.2 4.0 copy-start.3
  120.2 4.0 copy-start.4
  120.2 5.6 %copy-start.16 = (f32[192]{0:T(256)S(1)}, f32[192]{0:T(256)}, u32[]{:S(2)}) copy-start(f32[192]{0:T(256)} %broadcast_in_dim.76) | copy-start | bytes 2308
  120.2 6.4 %copy-start.17 = (f32[256]{0:T(256)S(1)}, f32[256]{0:T(256)}, u32[]{:S(2)}) copy-start(f32[256]{0:T(256)} %broadcast_in_dim.74) | copy-start | bytes 3076
  171.7 13.0 %copy-start.1 = (bf16[36864]{0:T(1024)(128)(2,1)S(1)}, bf16[36864]{0:T(1024)(128)(2,1)}, u32[]{:S(2)}) copy-start(bf16[36864]{0:T(1024)(128)(2,1)} %slice.268) | copy-start | bytes 221188
  199.3 0.7 copy-start.8
  278.4 5.2 copy-start.12
  278.4 5.3 copy-start.11
  278.4 5.4 %copy-start.10 = (f32[64,256]{1,0:T(8,128)S(1)}, f32[64,256]{1,0:T(8,128)}, u32[]{:S(2)}) copy-start(f32[64,256]{1,0:T(8,128)} %get-tuple-element.139) | copy-start | bytes 196612
  278.4 5.5 %copy-start.14 = (f32[32,1]{1,0:T(8,128)S(1)}, f32[32,1]{1,0:T(8,128)}, u32[]{:S(2)}) copy-start(f32[32,1]{1,0:T(8,128)} %get-tuple-element.141) | copy-start | bytes 388
  279.8 12.8 %copy-start.7 = (f32[512,1]{1,0:T(8,128)S(1)}, f32[512,1]{1,0:T(8,128)}, u32[]{:S(2)}) copy-start(f32[512,1]{1,0:T(8,128)} %get-tuple-element.130) | copy-start | bytes 6148
  292.6 180.5 %reduce-scatter.2.cloned.1.call-start = ((), (), s32[]{:S(2)}) async-start(), calls=%async_computation.2 | async-start | bytes 7241728 | tf_op jit(solution)/shard_map/reduce_scatter | solution.py:503
  292.8 3.6 copy-start.18
  305.2 1.0 copy-start.5
  305.2 1.2 copy-start.6
  305.2 201.7 %copy-start = (f32[105984]{0:T(1024)S(1)}, f32[105984]{0:T(1024)}, u32[]{:S(2)}) copy-start(f32[105984]{0:T(1024)} %param.23) | copy-start | bytes 1271812
  305.2 226.8 %all-reduce.39.cloned.1.call-start = ((), (), s32[]{:S(2)}) async-start(), calls=%async_computation.4 | async-start | bytes 851968 | tf_op jit(solution)/shard_map/psum | solution.py:555
Sparse Core Ops, SparseCore 0:
  10.8 49.3 all-gather.1
  292.7 87.3 all-reduce.36
  384.1 88.9 reduce-scatter.1
  508.2 23.7 all-reduce.38

commit v2 on v1

v2 whole, which is shorter than its diff:
```python
import math

import jax
import jax.numpy as jnp
from jax import lax
from jax.experimental import pallas as pl
from jax.experimental.pallas import tpu as pltpu
from jax.sharding import PartitionSpec as P

C1 = 32
C2 = 64
C3 = 64
HID = 512
ACTIONS = 18
PARAMS = 1693875
FEATURES = 49 * C3
CONV_LEN = 256 * C1 + C1 + 16 * C1 * C2 + C2 + 9 * C2 * C3 + C3
TOP = CONV_LEN // HID
LEAD = (TOP + 8) // 8 * 8
BLOCK_ROWS = LEAD + 8
PHASE = CONV_LEN % HID
HEAD_LEN = HID * (ACTIONS + 1) + ACTIONS + 1

BETA_ONE = 0.9
BETA_TWO = 0.999
ADAM_EPSILON = 1e-08
LEARN_RATE = 0.005
WEIGHT_DECAY = 0.01
CLIP_NORM = 0.5
OUTER_RATE = 0.7
OUTER_MOMENTUM = 0.9
DISCOUNT = 0.99
TRACE_DECAY = 0.95
RATIO_CLIP = 0.1
VALUE_COEF = 0.5
ENTROPY_COEF = 0.01

F32 = jnp.float32
BF16 = jnp.bfloat16
VMEM_LIMIT = 63 * 1024 * 1024


def mm(a, b):
    return jnp.dot(a, b, preferred_element_type=F32)


def mm_nt(a, b):
    return lax.dot_general(a, b, (((1,), (1,)), ((), ())), preferred_element_type=F32)


def mm_tn(a, b):
    return lax.dot_general(a, b, (((0,), (0,)), ((), ())), preferred_element_type=F32)


def trajectory_advantages(rewards, values, next_values, terminal, truncated):
    alive = 1.0 - terminal.astype(F32)
    cutoff = truncated.astype(F32)
    following = jnp.concatenate([values[:, 1:], next_values[:, -1:]], axis=1)
    following = cutoff * next_values + (1.0 - cutoff) * following
    deltas = rewards + DISCOUNT * alive * following - values
    keeping = DISCOUNT * TRACE_DECAY * alive * (1.0 - cutoff)

    def backward_step(carry, item):
        delta, keep = item
        result = delta + keep * carry
        return (result, result)

    start = jnp.zeros((rewards.shape[0],), F32)
    _, series = lax.scan(backward_step, start, (deltas.T, keeping.T), reverse=True)
    return series.T


def unfold(block, phase, width, rows):
    lane = lax.broadcasted_iota(jnp.int32, (1, HID), 1)
    if phase:
        turned = pltpu.roll(block, HID - phase, 1)
        block = jnp.where(lane < HID - phase, turned[:rows], turned[1 : rows + 1])
    pieces = []
    for k in range(HID // width):
        start = k * width // 128 * 128
        piece = block[:rows, start : start + 128]
        turn = k * width % 128
        pieces.append(pltpu.roll(piece, 128 - turn, 1) if turn else piece)
    return pieces


def weights_body(
    conv_ref,
    t1_ref,
    b1_ref,
    t2_ref,
    b2_ref,
    t3_ref,
    b3_ref,
    back3_ref,
    back2_ref,
    wide_ref,
    w1_ref,
    w2_ref,
    w3_ref,
):
    wide_ref[...] = conv_ref[...].astype(F32)
    for k, piece in enumerate(unfold(wide_ref[0:24], 0, C1, 24)):
        w1_ref[pl.ds(k, 24, stride=16), :] = piece
    for k, piece in enumerate(unfold(wide_ref[16:96], 32, C2, 72)):
        w2_ref[pl.ds(k, 72, stride=8), :] = piece
    for k, piece in enumerate(unfold(wide_ref[80:168], 96, C3, 80)):
        w3_ref[pl.ds(k, 80, stride=8), :] = piece
    w1 = w1_ref[...].T
    w2 = w2_ref[...].T
    w3 = w3_ref[...].T
    w1_low = w1.astype(BF16)
    w2_low = w2.astype(BF16)
    w3_low = w3.astype(BF16)
    for ref in (t1_ref, t2_ref, t3_ref, back3_ref, back2_ref):
        ref[...] = jnp.zeros(ref.shape, BF16)
    for p in range(2):
        for q in range(4):
            d = 4 * p + q
            for i in range(8):
                lane = (i + 4 * p) * 80 + 16 * q
                t1_ref[32 * d : 32 * d + 32, lane : lane + 32] = w1_low[0:32, 32 * i : 32 * i + 32]
            b1_ref[32 * d : 32 * d + 32] = jnp.broadcast_to(w1[0:32, 256:257], (32, 256))
    for q in range(3):
        for i in range(4):
            lane = 256 * i + 64 * q
            t2_ref[64 * q : 64 * q + 64, lane : lane + 128] = w2_low[0:64, 128 * i : 128 * i + 128]
        b2_ref[64 * q : 64 * q + 64] = jnp.broadcast_to(w2[0:64, 512:513], (64, 256))
    for q in range(7):
        for i in range(3):
            lane = 576 * i + 64 * q
            t3_ref[64 * q : 64 * q + 64, lane : lane + 192] = w3_low[0:64, 192 * i : 192 * i + 192]
        b3_ref[64 * q : 64 * q + 64] = jnp.broadcast_to(w3[0:64, 576:577], (64, 256))
    for x in range(9):
        for r in range(3):
            for q in range(max(0, x - 2), min(6, x) + 1):
                k = ((2 - r) * 3 + x - q) * 64
                lane = 512 * r + 64 * q
                back3_ref[64 * x : 64 * x + 64, lane : lane + 64] = w3_ref[k : k + 64, 0:64].astype(
                    BF16
                )
    for y in range(2):
        for x in range(4):
            for r in range(2):
                for q in range(3):
                    j = x + 2 - 2 * q
                    if 0 <= j < 4:
                        k = ((y + 2 - 2 * r) * 4 + j) * 32
                        row = 32 * (4 * y + x)
                        lane = 64 * (3 * r + q)
                        back2_ref[row : row + 32, lane : lane + 64] = w2_ref[
                            k : k + 32, 0:64
                        ].astype(BF16)


def conv_weights(block):
    shapes = [
        ((256, 960), BF16),
        ((256, 256), F32),
        ((192, 1024), BF16),
        ((192, 256), F32),
        ((448, 1728), BF16),
        ((448, 256), F32),
        ((576, 1536), BF16),
        ((256, 384), BF16),
    ]
    return pl.pallas_call(
        weights_body,
        out_shape=[jax.ShapeDtypeStruct(shape, kind) for shape, kind in shapes],
        scratch_shapes=[
            pltpu.VMEM((BLOCK_ROWS, HID), F32),
            pltpu.VMEM((384, 128), F32),
            pltpu.VMEM((640, 128), F32),
            pltpu.VMEM((640, 128), F32),
        ],
        compiler_params=pltpu.CompilerParams(vmem_limit_bytes=VMEM_LIMIT),
        name="conv_weights",
    )(block)


def pixel_window(x_refs, first, n):
    sides = []
    for e in range(2):
        parts = [x_refs[first + k][e, :, 64 * n : 64 * n + 80, :] for k in range(3)]
        sides.append(jnp.concatenate(parts, axis=0).reshape(960, 128))
    return jnp.concatenate(sides, axis=1)


def forward_body(
    x0, x1, x2, x3, x4, t1_ref, b1_ref, t2_ref, b2_ref, t3_ref, b3_ref, a1_ref, a2_ref, a3_ref
):
    x_refs = (x0, x1, x2, x3, x4)
    t = pl.program_id(1)
    for h in range(2):
        for n in range(5):
            window = pixel_window(x_refs, 2 * h, n)
            out = jnp.maximum(mm(t1_ref[...], window) + b1_ref[...], 0.0).astype(BF16)
            a1_ref[pl.ds(4 * t + 2 * h, 2), 4 * n : 4 * n + 4] = out.reshape(2, 4, C1, 256)

    @pl.when(t == 4)
    def _():
        def conv_two(p, carry):
            for g in range(3):
                window = a1_ref[pl.ds(2 * p, 4), 6 * g : 6 * g + 8].reshape(1024, 256)
                out = jnp.maximum(mm(t2_ref[...], window) + b2_ref[...], 0.0).astype(BF16)
                a2_ref[p, 3 * g : 3 * g + 3] = out.reshape(3, C2, 256)
            a2_ref[p, 9] = jnp.zeros((C2, 256), BF16)
            return carry

        lax.fori_loop(0, 9, conv_two, 0)

        def conv_three(p, carry):
            window = a2_ref[pl.ds(p, 3), 0:9].reshape(1728, 256)
            out = jnp.maximum(mm(t3_ref[...], window) + b3_ref[...], 0.0).astype(BF16)
            a3_ref[p] = out.reshape(7, C3, 256)
            return carry

        lax.fori_loop(0, 7, conv_three, 0)


def whole(shape):
    return pl.BlockSpec(shape, lambda *j: (0,) * len(shape), pipeline_mode=pl.Buffered(1))


def pixel_specs():
    def spec(k):
        return pl.BlockSpec((2, 4, 336, 128), lambda j, t: (j, 4 * t + k, 0, 0))

    return [spec(k) for k in range(5)]


def conv_forward(x, t1, b1, t2, b2, t3, b3):
    envs = x.shape[0]
    frames = envs * 128
    return pl.pallas_call(
        forward_body,
        grid=(envs // 2, 5),
        in_specs=pixel_specs()
        + [
            whole((256, 960)),
            whole((256, 256)),
            whole((192, 1024)),
            whole((192, 256)),
            whole((448, 1728)),
            whole((448, 256)),
        ],
        out_specs=[
            pl.BlockSpec((20, 20, C1, 256), lambda j, t: (0, 0, 0, j)),
            pl.BlockSpec((9, 10, C2, 256), lambda j, t: (0, 0, 0, j)),
            pl.BlockSpec((7, 7, C3, 256), lambda j, t: (0, 0, 0, j)),
        ],
        out_shape=[
            jax.ShapeDtypeStruct((20, 20, C1, frames), BF16),
            jax.ShapeDtypeStruct((9, 10, C2, frames), BF16),
            jax.ShapeDtypeStruct((7, 7, C3, frames), BF16),
        ],
        compiler_params=pltpu.CompilerParams(vmem_limit_bytes=VMEM_LIMIT),
        name="conv_forward",
    )(x, x, x, x, x, t1, b1, t2, b2, t3, b3)


def dense_body(
    scale,
    a3_ref,
    wd_ref,
    bd_ref,
    wh_ref,
    bh_ref,
    normed_ref,
    returns_ref,
    actions_ref,
    behavior_ref,
    packed_ref,
    dc3_ref,
    gwh_ref,
    gbh_ref,
    loss_ref,
    wide_ref,
):
    hidden_pre = mm_tn(wd_ref[...], a3_ref[...]) + bd_ref[...]
    hidden = jnp.maximum(hidden_pre, 0.0).astype(BF16)
    out = mm(wh_ref[...], hidden) + bh_ref[...]
    row = lax.broadcasted_iota(jnp.int32, out.shape, 0)
    is_logit = row < ACTIONS
    logits = jnp.where(is_logit, out, -jnp.inf)
    top = jnp.max(logits, axis=0, keepdims=True)
    shifted = out - top
    exps = jnp.where(is_logit, jnp.exp(shifted), 0.0)
    total = jnp.sum(exps, axis=0, keepdims=True)
    log_probs = jnp.where(is_logit, shifted - jnp.log(total), 0.0)
    probs = jnp.where(is_logit, jnp.exp(log_probs), 0.0)
    value = jnp.sum(jnp.where(row == ACTIONS, out, 0.0), axis=0, keepdims=True)
    normed = normed_ref[...]
    chosen = row == actions_ref[...]
    taken = jnp.sum(jnp.where(chosen, log_probs, 0.0), axis=0, keepdims=True)
    ratio = jnp.exp(taken - behavior_ref[...])
    low = 1.0 - RATIO_CLIP
    high = 1.0 + RATIO_CLIP
    clipped = jnp.clip(ratio, low, high)
    plain = ratio * normed
    cut = clipped * normed
    entropy = -jnp.sum(probs * log_probs, axis=0, keepdims=True)
    error = value - returns_ref[...]
    losses = -jnp.minimum(plain, cut) + 0.5 * VALUE_COEF * error * error - ENTROPY_COEF * entropy
    loss_ref[...] = jnp.sum(losses, axis=1, keepdims=True) * scale
    plain_share = jnp.where(plain < cut, 1.0, jnp.where(plain == cut, 0.5, 0.0))
    inside = jnp.where(
        (ratio > low) & (ratio < high), 1.0, jnp.where((ratio == low) | (ratio == high), 0.5, 0.0)
    )
    d_taken = -scale * normed * ratio * (plain_share + (1.0 - plain_share) * inside)
    d_logits = d_taken * (jnp.where(chosen, 1.0, 0.0) - probs) + (scale * ENTROPY_COEF) * probs * (
        log_probs + entropy
    )
    d_value = scale * VALUE_COEF * error
    d_out = jnp.where(is_logit, d_logits, jnp.where(row == ACTIONS, d_value, 0.0)).astype(BF16)
    gwh_ref[...] = mm_nt(d_out, hidden)
    gbh_ref[...] = jnp.sum(d_out.astype(F32), axis=1, keepdims=True)
    back = mm_tn(wh_ref[...], d_out)
    d_hidden = jnp.where(hidden_pre > 0, back, 0.0).astype(BF16)
    last = LEAD + FEATURES
    wide_ref[0:LEAD] = jnp.zeros((LEAD, HID), F32)
    wide_ref[LEAD:last] = mm_nt(a3_ref[...], d_hidden)
    wide_ref[last:] = jnp.zeros((wide_ref.shape[0] - last, HID), F32)
    ones = jnp.ones((8, d_hidden.shape[1]), BF16)
    wide_ref[last : last + 1] = mm_nt(ones, d_hidden)[0:1]
    late = lax.broadcasted_iota(jnp.int32, (1, HID), 1) >= PHASE
    shards, rows, _ = packed_ref.shape
    for k in range(shards):
        first = rows * k + LEAD - TOP - 1
        packed_ref[k] = jnp.where(
            late, wide_ref[first + 1 : first + 1 + rows], wide_ref[first : first + rows]
        )
    d_a3 = mm(wd_ref[...], d_hidden)
    dc3_ref[...] = jnp.where(a3_ref[...] > 0, d_a3, 0.0).astype(BF16)


def dense_step(scale, shards, shard_rows, a3, wd, bd, wh, bh, normed, returns, actions, behavior):
    frames = a3.shape[1]
    rows = wh.shape[0]
    return pl.pallas_call(
        lambda *refs: dense_body(scale, *refs),
        out_shape=[
            jax.ShapeDtypeStruct((shards, shard_rows, HID), F32),
            jax.ShapeDtypeStruct((FEATURES, frames), BF16),
            jax.ShapeDtypeStruct((rows, HID), F32),
            jax.ShapeDtypeStruct((rows, 1), F32),
            jax.ShapeDtypeStruct((1, 1), F32),
        ],
        scratch_shapes=[
            pltpu.VMEM((max(shards * shard_rows, TOP + 1 + FEATURES) + 2 * LEAD - TOP, HID), F32)
        ],
        compiler_params=pltpu.CompilerParams(vmem_limit_bytes=VMEM_LIMIT),
        name="dense_step",
    )(a3, wd, bd, wh, bh, normed, returns, actions, behavior)


def fold(g_ref, width, rows):
    step = HID // width
    lane = lax.broadcasted_iota(jnp.int32, (1, 128), 1)
    columns = []
    for m in range(4):
        total = 0.0
        for t in range(128 // width):
            piece = g_ref[pl.ds(m * 128 // width + t, rows, stride=step), :]
            piece = jnp.where(lane < width, piece, 0.0)
            total = total + (pltpu.roll(piece, width * t, 1) if t else piece)
        columns.append(total)
    return jnp.concatenate(columns, axis=1)


def upper_body(
    a1_hbm,
    a2_ref,
    dc3_ref,
    t3_ref,
    d2_ref,
    packed_ref,
    r2_ref,
    r3_ref,
    s2_ref,
    s3_ref,
    a1_ref,
    d3_ref,
    g2_ref,
    g3_ref,
    sems,
):
    step = pl.program_id(0)
    lanes = pl.ds(pl.multiple_of(256 * step, 256), 256)
    load_a1 = pltpu.make_async_copy(a1_hbm.at[:, :, :, lanes], a1_ref, sems.at[0])
    load_a1.start()

    @pl.when(step == 0)
    def _():
        for ref in (r2_ref, r3_ref, s2_ref, s3_ref):
            ref[...] = jnp.zeros(ref.shape, F32)
        for p in (0, 1, 9, 10):
            d3_ref[p] = jnp.zeros((8, C3, 256), BF16)

    for p in (0, 10):
        d2_ref[p] = jnp.zeros((11, C2, 256), BF16)

    def edge(p, carry):
        d2_ref[p, 0] = jnp.zeros((C2, 256), BF16)
        d2_ref[p, 10] = jnp.zeros((C2, 256), BF16)
        return carry

    lax.fori_loop(1, 10, edge, 0)

    def fill(p, carry):
        d3_ref[p + 2, 0:7] = dc3_ref[p]
        d3_ref[p + 2, 7] = jnp.zeros((C3, 256), BF16)
        s3_ref[...] += jnp.sum(dc3_ref[p].astype(F32), axis=0)
        return carry

    lax.fori_loop(0, 7, fill, 0)

    def three_weights(p, carry):
        left = mm_nt(a2_ref[pl.ds(p, 3), 0:6].reshape(1152, 256), d3_ref[p + 2, 0:4].reshape(256, 256))
        right = mm_nt(
            a2_ref[pl.ds(p, 3), 4:10].reshape(1152, 256), d3_ref[p + 2, 4:8].reshape(256, 256)
        )
        r3_ref[...] += left + right
        return carry

    lax.fori_loop(0, 7, three_weights, 0)

    def three_input(y, carry):
        back = mm(t3_ref[...], d3_ref[pl.ds(y, 3)].reshape(1536, 256)).reshape(9, C2, 256)
        masked = jnp.where(a2_ref[y, 0:9] > 0, back, 0.0).astype(BF16)
        d2_ref[y + 1, 1:10] = masked
        s2_ref[...] += jnp.sum(masked.astype(F32), axis=0)
        return carry

    lax.fori_loop(0, 9, three_input, 0)
    load_a1.wait()

    def two_weights(p, carry):
        total = 0.0
        for g in range(3):
            total = total + mm_nt(
                a1_ref[pl.ds(2 * p, 4), 6 * g : 6 * g + 8].reshape(1024, 256),
                d2_ref[p + 1, 1 + 3 * g : 4 + 3 * g].reshape(192, 256),
            )
        r2_ref[:, 0:192] += total
        return carry

    lax.fori_loop(0, 9, two_weights, 0)

    @pl.when(step == pl.num_programs(0) - 1)
    def _():
        g2_ref[...] = jnp.zeros(g2_ref.shape, F32)
        g3_ref[...] = jnp.zeros(g3_ref.shape, F32)
        for i in range(4):
            k = 256 * i
            total = r2_ref[k : k + 128, 0:128]
            total = total + pltpu.roll(r2_ref[k + 64 : k + 192, 0:128], 64, 1)
            g2_ref[128 * i : 128 * i + 128] = total + r2_ref[k + 128 : k + 256, 128:256]
        for i in range(3):
            k = 384 * i
            total = r3_ref[k : k + 192, 0:128]
            total = total + pltpu.roll(r3_ref[k + 64 : k + 256, 0:128], 64, 1)
            total = total + r3_ref[k + 128 : k + 320, 128:256]
            total = total + pltpu.roll(r3_ref[k + 192 : k + 384, 128:256], 64, 1)
            g3_ref[192 * i : 192 * i + 192] = total
        g2_ref[512:513, 0:64] = jnp.sum(s2_ref[...].T, axis=0, keepdims=True)
        g3_ref[576:577, 0:64] = jnp.sum(s3_ref[...].T, axis=0, keepdims=True)
        lane = lax.broadcasted_iota(jnp.int32, (1, HID), 1)
        packed_ref[...] = jnp.zeros(packed_ref.shape, F32)
        for ref, rows, base, phase in ((g2_ref, 72, 16, 32), (g3_ref, 80, 80, 96)):
            turned = pltpu.roll(fold(ref, 64, rows), phase, 1)
            packed_ref[base : base + rows] += jnp.where(lane >= phase, turned, 0.0)
            packed_ref[base + 1 : base + 1 + rows] += jnp.where(lane < phase, turned, 0.0)


def upper_backward(a1, a2, dc3, t3):
    frames = a1.shape[3]
    return pl.pallas_call(
        upper_body,
        grid=(frames // 256,),
        in_specs=[
            pl.BlockSpec(memory_space=pl.ANY),
            pl.BlockSpec((9, 10, C2, 256), lambda j: (0, 0, 0, j)),
            pl.BlockSpec((7, 7, C3, 256), lambda j: (0, 0, 0, j)),
            whole((576, 1536)),
        ],
        out_specs=[
            pl.BlockSpec((11, 11, C2, 256), lambda j: (0, 0, 0, j)),
            whole((BLOCK_ROWS, HID)),
        ],
        out_shape=[
            jax.ShapeDtypeStruct((11, 11, C2, frames), BF16),
            jax.ShapeDtypeStruct((BLOCK_ROWS, HID), F32),
        ],
        scratch_shapes=[
            pltpu.VMEM((1024, 256), F32),
            pltpu.VMEM((1152, 256), F32),
            pltpu.VMEM((C2, 256), F32),
            pltpu.VMEM((C3, 256), F32),
            pltpu.VMEM((20, 20, C1, 256), BF16),
            pltpu.VMEM((11, 8, C3, 256), BF16),
            pltpu.VMEM((640, 128), F32),
            pltpu.VMEM((640, 128), F32),
            pltpu.SemaphoreType.DMA((1,)),
        ],
        compiler_params=pltpu.CompilerParams(vmem_limit_bytes=VMEM_LIMIT),
        name="upper_backward",
    )(a1, a2, dc3, t3)


def lower_body(x0, x1, x2, x3, x4, a1_ref, d2_ref, t2_ref, packed_ref, r1_ref, s1_ref, g1_ref):
    x_refs = (x0, x1, x2, x3, x4)
    t = pl.program_id(1)

    @pl.when((pl.program_id(0) == 0) & (t == 0))
    def _():
        r1_ref[...] = jnp.zeros(r1_ref.shape, F32)
        s1_ref[...] = jnp.zeros(s1_ref.shape, F32)

    total = 0.0
    sums = jnp.zeros((C1, 256), F32)
    for h in range(2):
        for n in range(5):
            back = mm(
                t2_ref[...],
                d2_ref[pl.ds(2 * t + h, 2), 2 * n : 2 * n + 3].reshape(384, 256),
            )
            kept = a1_ref[2 * h : 2 * h + 2, 4 * n : 4 * n + 4].reshape(256, 256) > 0
            masked = jnp.where(kept, back, 0.0).astype(BF16)
            sums = sums + jnp.sum(masked.astype(F32).reshape(8, C1, 256), axis=0)
            total = total + mm_nt(pixel_window(x_refs, 2 * h, n), masked)
    r1_ref[...] += total
    s1_ref[...] += sums

    @pl.when((pl.program_id(0) == pl.num_programs(0) - 1) & (t == 4))
    def _():
        g1_ref[...] = jnp.zeros(g1_ref.shape, F32)
        for i in range(8):
            total = 0.0
            for p in range(2):
                for q in range(4):
                    k = (i + 4 * p) * 80 + 16 * q
                    slab = r1_ref[k : k + 32, 128 * p : 128 * p + 128]
                    total = total + (pltpu.roll(slab, 128 - 32 * q, 1) if q else slab)
            g1_ref[32 * i : 32 * i + 32] = total
        g1_ref[256:257, 0:32] = jnp.sum(s1_ref[...].T, axis=0, keepdims=True)
        packed_ref[...] = fold(g1_ref, 32, 24)


def lower_backward(x, a1, d2, t2):
    envs = x.shape[0]
    return pl.pallas_call(
        lower_body,
        grid=(envs // 2, 5),
        in_specs=pixel_specs()
        + [
            pl.BlockSpec((4, 20, C1, 256), lambda j, t: (t, 0, 0, j)),
            pl.BlockSpec((11, 11, C2, 256), lambda j, t: (0, 0, 0, j)),
            whole((256, 384)),
        ],
        out_specs=whole((24, HID)),
        out_shape=jax.ShapeDtypeStruct((24, HID), F32),
        scratch_shapes=[
            pltpu.VMEM((960, 256), F32),
            pltpu.VMEM((C1, 256), F32),
            pltpu.VMEM((384, 128), F32),
        ],
        compiler_params=pltpu.CompilerParams(vmem_limit_bytes=VMEM_LIMIT),
        name="lower_backward",
    )(x, x, x, x, x, a1, d2, t2)


def swap(value, lanes, step):
    return lax.ppermute(value, "dp", [(i, i ^ step) for i in range(lanes)])


def halving_order(lanes):
    return [1 << k for k in range(lanes.bit_length() - 1)]


def sum_everywhere(value, lanes):
    for step in halving_order(lanes):
        value = value + swap(value, lanes, step)
    return value


def scatter_sum(blocks, lanes, place):
    for step in halving_order(lanes):
        pairs = blocks.reshape((blocks.shape[0] // 2, 2) + blocks.shape[1:])
        high = (place // step) % 2 == 1
        kept = jnp.where(high, pairs[:, 1], pairs[:, 0])
        sent = jnp.where(high, pairs[:, 0], pairs[:, 1])
        blocks = kept + swap(sent, lanes, step)
    return blocks[0]


def gather_blocks(block, lanes, place):
    blocks = block[None]
    for step in reversed(halving_order(lanes)):
        other = swap(blocks, lanes, step)
        high = (place // step) % 2 == 1
        blocks = jnp.stack(
            [jnp.where(high, other, blocks), jnp.where(high, blocks, other)], axis=1
        ).reshape((2 * blocks.shape[0],) + blocks.shape[1:])
    return blocks


def first_rows_everywhere(local, lanes, place):
    rows = local.shape[0]
    owners = -(-(TOP + 1) // rows)
    if owners == 1:
        block = jnp.pad(local[: TOP + 1], ((0, BLOCK_ROWS - TOP - 1), (0, 0)))
        block = jnp.where(place == 0, block, jnp.zeros((), BF16))
        for step in reversed(halving_order(lanes)):
            pairs = [(i, i + step) for i in range(0, lanes, 2 * step)]
            block = block + lax.ppermute(block, "dp", pairs)
        return block
    block = jnp.zeros((owners, rows, HID), BF16)
    block = jnp.where(jnp.arange(owners)[:, None, None] == place, local[None], block)
    block = sum_everywhere(block, lanes).reshape(owners * rows, HID)[: TOP + 1]
    return jnp.pad(block, ((0, BLOCK_ROWS - TOP - 1), (0, 0)))


def on_device(
    frames,
    actions,
    rewards,
    old_values,
    next_values,
    terminal,
    truncated,
    behavior_logprob,
    master,
    first_moment,
    second_moment,
    outer_momentum,
    step_count,
):
    lanes = lax.axis_size("dp")
    place = lax.axis_index("dp")
    shard_len = master.shape[0]
    rows = shard_len // HID
    groups = lax.axis_size("group")
    assert groups == 2 and rows * HID == shard_len and frames.shape[2] == 128

    def other_group(value):
        return lax.ppermute(value, "group", [(0, 1), (1, 0)])

    master_rows = master.reshape(rows, HID)
    low_rows = master_rows.astype(BF16)
    block = first_rows_everywhere(low_rows, lanes, place)
    gathered = lax.all_gather(low_rows, "dp", axis=0).reshape(lanes * rows, HID)

    advantage = trajectory_advantages(
        rewards[0], old_values[0], next_values[0], terminal[0], truncated[0]
    )
    envs_here, steps_here = advantage.shape
    batch = envs_here * steps_here
    total_frames = batch * lanes
    sums = jnp.stack([jnp.sum(advantage), jnp.sum(advantage * advantage)])
    first_sum, square_sum = sum_everywhere(sums, lanes)
    mean = first_sum / total_frames
    spread = square_sum / total_frames - mean * mean
    normed = ((advantage - mean) * lax.rsqrt(spread + 1e-05)).reshape(1, batch)
    returns = (advantage + old_values[0]).reshape(1, batch)

    x = frames[0].transpose(0, 2, 3, 1)
    t1, b1, t2, b2, t3, b3, back3, back2 = conv_weights(block)
    a1, a2, a3 = conv_forward(x, t1, b1, t2, b2, t3, b3)

    column = lax.broadcasted_iota(jnp.int32, (1, HID), 1)
    late = column >= PHASE
    w_dense = jnp.where(
        late, gathered[TOP : TOP + FEATURES], gathered[TOP + 1 : TOP + 1 + FEATURES]
    )
    b_dense = jnp.where(
        late[0], gathered[TOP + FEATURES], gathered[TOP + 1 + FEATURES]
    ).astype(F32)
    tail = TOP + FEATURES + 1
    head_flat = gathered[tail:].reshape(-1)[PHASE : PHASE + HEAD_LEN]
    w_head = head_flat[: HID * (ACTIONS + 1)].reshape(HID, ACTIONS + 1)
    w_head = jnp.pad(jnp.roll(w_head, PHASE, axis=0).T, ((0, 13), (0, 0)))
    b_head = jnp.pad(head_flat[HID * (ACTIONS + 1) :], (0, 13)).astype(F32)
    packed_dense, d_c3, g_head, g_head_bias, loss_local = dense_step(
        1.0 / total_frames,
        lanes,
        rows,
        a3.reshape(FEATURES, batch),
        w_dense,
        b_dense[:, None],
        w_head,
        b_head[:, None],
        normed,
        returns,
        actions[0].reshape(1, batch),
        behavior_logprob[0].reshape(1, batch),
    )
    dense_owned = lax.psum_scatter(packed_dense, "dp", scatter_dimension=0, tiled=False)
    d2, upper = upper_backward(a1, a2, d_c3.reshape(7, 7, C3, batch), back3)
    lower = lower_backward(x, a1, d2, back2)

    tail_rows = lanes * rows - tail
    head_part = jnp.concatenate(
        [
            jnp.zeros((PHASE,), F32),
            jnp.roll(g_head[: ACTIONS + 1].T, -PHASE, axis=0).reshape(-1),
            g_head_bias[: ACTIONS + 1, 0],
            jnp.zeros((tail_rows * HID - PHASE - HEAD_LEN,), F32),
        ]
    ).reshape(tail_rows, HID)
    small = jnp.concatenate(
        [jnp.pad(lower, ((0, BLOCK_ROWS - 24), (0, 0))) + upper, head_part], axis=0
    )
    unit = lanes * 8 // math.gcd(lanes * 8, 4)
    count = -(-small.shape[0] // unit) * unit
    small = jnp.pad(small, ((0, count - small.shape[0]), (0, 0)))
    piece = scatter_sum(small.reshape(lanes, count * 4 // lanes, 128), lanes, place)
    squares = jnp.sum(dense_owned * dense_owned) + jnp.sum(piece * piece)
    facts = jnp.zeros((8, 128), F32).at[0, 0].set(squares).at[0, 1].set(loss_local[0, 0])
    message = jnp.concatenate([piece, facts], axis=0)
    message = jnp.stack([message, other_group(message)])
    messages = gather_blocks(message, lanes, place)
    own_facts = jnp.sum(messages[:, :, -8], axis=0)
    norm = jnp.sqrt(own_facts[:, 0])
    loss_total = own_facts[0, 1]
    smalls = messages[:, :, :-8].transpose(1, 0, 2, 3).reshape(2, count, HID)

    def own_rows(part, first_row):
        first = first_row // rows
        blocks = -(-(first_row + part.shape[1]) // rows) - first
        part = jnp.pad(
            part,
            (
                (0, 0),
                (first_row - first * rows, (first + blocks) * rows - first_row - part.shape[1]),
                (0, 0),
            ),
        )
        here = (place >= first) & (place < first + blocks)
        start = jnp.clip(place - first, 0, blocks - 1) * rows
        return jnp.where(here, lax.dynamic_slice_in_dim(part, start, rows, 1), 0.0)

    owned = jnp.stack([dense_owned, other_group(dense_owned)])
    owned = owned + own_rows(smalls[:, : TOP + 1], 0)
    owned = owned + own_rows(smalls[:, BLOCK_ROWS : BLOCK_ROWS + tail_rows], tail)
    firsts = jnp.stack([first_moment[0], other_group(first_moment[0])])
    seconds = jnp.stack([second_moment[0], other_group(second_moment[0])])
    factor = jnp.minimum(1.0, CLIP_NORM / (norm + 1e-06))
    clipped = owned.reshape(2, shard_len) * factor[:, None]
    moment_step = step_count[0].astype(F32)
    first_next = BETA_ONE * firsts + (1.0 - BETA_ONE) * clipped
    second_next = BETA_TWO * seconds + (1.0 - BETA_TWO) * clipped * clipped
    first_hat = first_next / (1.0 - jnp.power(BETA_ONE, moment_step))
    second_hat = second_next / (1.0 - jnp.power(BETA_TWO, moment_step))
    inner = master - LEARN_RATE * (
        first_hat / (jnp.sqrt(second_hat) + ADAM_EPSILON) + WEIGHT_DECAY * master
    )
    drift = master - inner
    moved = (drift[0] + drift[1]) / groups
    momentum_next = OUTER_MOMENTUM * outer_momentum + moved
    final = master - OUTER_RATE * (moved + OUTER_MOMENTUM * momentum_next)
    return (
        clipped[:1],
        norm[:1],
        loss_total.reshape(1),
        first_next[:1],
        second_next[:1],
        moved,
        momentum_next,
        final,
        final.astype(BF16),
    )


def solution(mesh):
    return jax.shard_map(
        on_device,
        mesh=mesh,
        in_specs=(
            P("group", "dp", None, None, None),
            P("group", "dp", None),
            P("group", "dp", None),
            P("group", "dp", None),
            P("group", "dp", None),
            P("group", "dp", None),
            P("group", "dp", None),
            P("group", "dp", None),
            P("dp"),
            P("group", "dp"),
            P("group", "dp"),
            P("dp"),
            P(),
        ),
        out_specs=(
            P("group", "dp"),
            P("group"),
            P("group"),
            P("group", "dp"),
            P("group", "dp"),
            P("dp"),
            P("dp"),
            P("dp"),
            P("dp"),
        ),
        check_vma=False,
    )
```

time: 544 us -> 299 us (0.55)
  waiting for transfers between devices: 182 us -> 60.3 us
  local copies, waits for them, and re-layouts: 109 us -> 25.1 us
  blocking collectives: 67.4 us -> 0 us
  starting transfers between devices: 0.16 us -> 25.2 us
  Pallas kernels: 128 us -> 135 us
    reduce_scatter x1, waiting for transfers between devices: 91.1 us -> 0.01 us  [on_device(): lax.psum_scatter(packed_dense, 'dp', scatter_dimension=0, tiled=False)]
    psum x2 -> x0, waiting for transfers between devices: 90.7 us -> none  [the longest x1 71.2 us: on_device(): small = lax.psum(small, 'dp')]
    psum x2 -> x0, blocking collectives: 67.4 us -> none  [the longest x1 36 us: on_device(): lax.psum((jnp.sum(advantage), jnp.sum(advantage * advantage)), 'dp')]
    ppermute x0 -> x20, waiting for transfers between devices: none -> 60.2 us  [the longest x12 30.8 us: swap(): return lax.ppermute(value, 'dp', [(i, i ^ step) for i in range(lanes)])]
    ppermute x0 -> x20, starting transfers between devices: none -> 25.1 us  [the longest x4 11 us: first_rows_everywhere(): block = block + lax.ppermute(block, 'dp', pairs)]
    reshape x10 -> x3, local copies, waits for them, and re-layouts: 22.7 us -> 2.62 us  [the longest x1 2.49 us: on_device(): gathered = lax.all_gather(low_rows, 'dp', axis=0).reshape(lanes * rows, HID)]
    unnamed x70 -> x33, local copies, waits for them, and re-layouts: 21.4 us -> 1.76 us
    another operation x15 -> x11, local copies, waits for them, and re-layouts: 23.1 us -> 3.54 us  [the longest x1 1.05 us: on_device(): seconds = jnp.stack([second_moment[0], other_group(second_moment[0])])]
  transfers between devices with their start and end apart: 4 -> 22, of which waited for: 3 -> 15; matrix products, arithmetic and copies ran while one was open for 6% -> 9% of each run, Pallas kernels for 0% -> 41%
where the time goes in v2:
time: 299 us; the launch traced here: 298 us
  Pallas kernels  135 us (45%)
  waiting for transfers between devices  60.3 us (20%)
  other arithmetic  30.6 us (10%)
  starting transfers between devices  25.2 us (8%)
  local copies, waits for them, and re-layouts  25.1 us (8%)
  between operations  19.5 us (7%)
    pallas_call x1, Pallas kernels, conv_forward(): pl.pallas_call(forward_body, grid=(envs // 2, 5), in_specs=pixel_specs()...  44.7 us
    pallas_call x1, Pallas kernels, lower_backward(): pl.pallas_call(lower_body, grid=(envs // 2, 5), in_specs=pixel_specs() +...  36.9 us
    pallas_call x1, Pallas kernels, upper_backward(): pl.pallas_call(upper_body, grid=(frames // 256,), in_specs=[pl.BlockSpec(...  36.1 us
    ppermute x12, waiting for transfers between devices, swap(): return lax.ppermute(value, 'dp', [(i, i ^ step) for i in range(lanes)])  30.8 us
    ppermute x4, waiting for transfers between devices, other_group(): return lax.ppermute(value, 'group', [(0, 1), (1, 0)])  27.5 us
    pallas_call x1, Pallas kernels, dense_step(): pl.pallas_call(lambda *refs: dense_body(scale, *refs), out_shape=[jax.Sha...  13.3 us
    ppermute x4, starting transfers between devices, first_rows_everywhere(): block = block + lax.ppermute(block, 'dp', pairs)  11 us
    ppermute x12, starting transfers between devices, swap(): return lax.ppermute(value, 'dp', [(i, i ^ step) for i in range(lanes)])  9.01 us
  transfers between devices with their start and end apart: 22, of which 15 were waited for; matrix products, arithmetic and copies ran while one was open for 9% of the time, Pallas kernels for 41%

profile of v2, /device:TPU:0, one launch (start us, length us, event | category | flops | bytes accessed | tf_op | source)
XLA Modules:
  0.0 298.2 jit_solution(551567340956197401)
XLA Ops:
  7.2 2.0 fusion.29
  10.1 6.0 %collective-permute-start = (bf16[168,512]{1,0:T(8,128)(2,1)S(1)}, bf16[168,512]{1,0:T(8,128)(2,1)S(1)}, u32[]{:S(2)}, u32[]{:S(2)}) collective-permute-start(bf16[168,512]{1,0:T(8,128)(2,1)S(1)} %select_select_fusion), channel_id=1, source_target_pairs={{0,8},{16,24}} | collective-permute-start | bytes 516104 | tf_op jit(solution)/shard_map/ppermute | solution.py:616
  19.6 9.6 %while.19 = (s32[]{:T(128)}, f32[4]{0:T(128)S(1)}, f32[128,4]{1,0:T(8,128)S(1)}, f32[128,4]{1,0:T(8,128)S(1)}, f32[128,4]{1,0:T(8,128)S(1)}, /*index=5*/s32[]{:T(128)}, s32[]{:T(128)}, s32[]{:T(128)}) while((s32[]{:T(128)}, f32[4]{0:T(128)S(1)}, f32[128,4]{1,0:T(8,128)S(1)}, f32[128,4]{1,0:T(8,128)S(1)}, f32[128,4]{1,0:T(8,128)S(1)}, ...), condition=%wide.region_1.2_spmd.clone, body=%wide.region_0.1_spmd.clone.sunk | while | flops 16 | bytes 219 | solution.py:69
  30.5 1.4 pad_maximum_fusion.5
  32.7 1.3 collective-permute-start.1
  34.0 1.4 fusion.32
  35.4 1.5 collective-permute-done.1
  36.9 2.4 collective-permute-start.2
  39.4 1.4 fusion.34
  40.8 1.3 collective-permute-start.6
  42.1 2.7 collective-permute-done.6
  45.3 4.0 %collective-permute-done.7 = f32[2]{0:T(128)S(1)} collective-permute-done((f32[2]{0:T(128)S(1)}, f32[2]{0:T(128)S(1)}, u32[]{:S(2)}, u32[]{:S(2)}) %collective-permute-start.7) | collective-permute-done | bytes 40 | tf_op jit(solution)/shard_map/ppermute | solution.py:574
  52.6 1.3 collective-permute-start.3
  55.7 4.2 %conv_weights.1 = (bf16[256,960]{1,0:T(8,128)(2,1)}, f32[256,256]{1,0:T(8,128)}, bf16[192,1024]{1,0:T(8,128)(2,1)}, f32[192,256]{1,0:T(8,128)}, bf16[448,1728]{1...) custom-call(bf16[168,512]{1,0:T(8,128)(2,1)} %add.169.conv_ref), custom_call_target="tpu_custom_call" | custom-call | tf_op jit(solution)/shard_map/conv_weights/pallas_call | solution.py:167
  59.9 44.7 %conv_forward.1 = (bf16[20,20,32,512]{3,2,1,0:T(8,128)(2,1)}, bf16[9,10,64,512]{3,2,1,0:T(8,128)(2,1)}, bf16[7,7,64,512]{3,2,1,0:T(8,128)(2,1)}) custom-call(bf16[4,84,336,128]{3,2,1,0:T(8,128)(2,1)} %bitcast.194, bf16[4,84,336,128]{3,2,1,0:T(8,128)(2,1)} %bitcast.195, bf16[4,84,336,128]{3,2,1,0:T(8,128)(2,1)} %bitcast.196, ...), custom_call_target="tpu_custom_call" | custom-call | tf_op jit(solution)/shard_map/conv_forward/pallas_call | solution.py:235
  104.6 2.5 reshape.277
  107.4 2.5 slice_select_fusion.refs_1_
  113.1 13.3 %dense_step.1 = (f32[16,207,512]{2,1,0:T(8,128)}, bf16[3136,512]{1,0:T(8,128)(2,1)}, f32[32,512]{1,0:T(8,128)}, f32[32,1]{1,0:T(8,128)}, f32[1,1]{1,0:T(1,128)}) custom-call(bf16[3136,512]{1,0:T(8,128)(2,1)} %bitcast.207, bf16[3136,512]{1,0:T(8,128)(2,1)} %slice_select_fusion.refs_1_, f32[512,1]{1,0:T(8,128)} %fusion.9.refs_2_, ...), custom_call_target="tpu_custom_call" | custom-call | tf_op jit(solution)/shard_map/dense_step/pallas_call | solution.py:340
  128.1 36.1 %upper_backward.1 = (bf16[11,11,64,512]{3,2,1,0:T(8,128)(2,1)}, f32[168,512]{1,0:T(8,128)}) custom-call(bf16[20,20,32,512]{3,2,1,0:T(8,128)(2,1)} %get-tuple-element.163.a1_hbm.a1_ref, bf16[9,10,64,512]{3,2,1,0:T(8,128)(2,1)} %get-tuple-element.164.a2_ref, bf16[7,7,64,512]{3,2,1,0:T(8,128)(2,1)} %bitcast.208, bf16[576,1536]{1,0:T(8,128)(2,1)} %get-tuple-element.166.t3_ref), custom_call_target="tpu_custom_call" | custom-call | tf_op jit(solution)/shard_map/upper_backward/pallas_call | solution.py:478
  164.2 36.9 %lower_backward.1 = f32[24,512]{1,0:T(8,128)} custom-call(bf16[4,84,336,128]{3,2,1,0:T(8,128)(2,1)} %bitcast.199, bf16[4,84,336,128]{3,2,1,0:T(8,128)(2,1)} %bitcast.200, bf16[4,84,336,128]{3,2,1,0:T(8,128)(2,1)} %bitcast.201, bf16[4,84,336,128]{3,2,1,0:T(8,128)(2,1)} %bitcast.202, bf16[4,84,336,128]{3,2,1,0:T(8,128)(2,1)} %bitcast.203, ...), custom_call_target="tpu_custom_call" | custom-call | tf_op jit(solution)/shard_map/lower_backward/pallas_call | solution.py:552
  202.6 1.1 collective-permute-done.9
  203.8 5.0 %collective-permute-done.10 = f32[4,48,128]{2,1,0:T(8,128)S(1)} collective-permute-done((f32[4,48,128]{2,1,0:T(8,128)S(1)}, f32[4,48,128]{2,1,0:T(8,128)S(1)}, u32[]{:S(2)}, u32[]{:S(2)}) %collective-permute-start.10) | collective-permute-done | bytes 98336 | tf_op jit(solution)/shard_map/ppermute | solution.py:574
  208.9 1.1 collective-permute-start.11
  210.0 3.1 %collective-permute-done.11 = f32[2,48,128]{2,1,0:T(8,128)S(1)} collective-permute-done((f32[2,48,128]{2,1,0:T(8,128)S(1)}, f32[2,48,128]{2,1,0:T(8,128)S(1)}, u32[]{:S(2)}, u32[]{:S(2)}) %collective-permute-start.11) | collective-permute-done | bytes 49184 | tf_op jit(solution)/shard_map/ppermute | solution.py:574
  213.1 1.2 collective-permute-start.12
  214.9 3.0 collective-permute-done.12
  218.5 1.7 multiply_reduce_fusion
  221.5 2.1 scatter.9
  223.6 1.5 collective-permute-start.13
  225.1 2.4 collective-permute-done.13
  227.6 1.2 collective-permute-start.14
  228.7 4.0 %collective-permute-done.14 = f32[1,2,56,128]{3,2,1,0:T(8,128)S(1)} collective-permute-done((f32[1,2,56,128]{3,2,1,0:T(8,128)S(1)}, f32[1,2,56,128]{3,2,1,0:T(8,128)S(1)}, u32[]{:S(2)}, u32[]{:S(2)}) %collective-permute-start.14) | collective-permute-done | bytes 57376 | tf_op jit(solution)/shard_map/ppermute | solution.py:574
  232.8 1.5 collective-permute-start.15
  234.3 3.3 %collective-permute-done.15 = f32[2,2,56,128]{3,2,1,0:T(8,128)S(1)} collective-permute-done((f32[2,2,56,128]{3,2,1,0:T(8,128)S(1)}, f32[2,2,56,128]{3,2,1,0:T(8,128)S(1)}, u32[]{:S(2)}, u32[]{:S(2)}) %collective-permute-start.15) | collective-permute-done | bytes 114720 | tf_op jit(solution)/shard_map/ppermute | solution.py:574
  237.7 1.5 collective-permute-start.16
  239.3 4.6 %collective-permute-done.16 = f32[4,2,56,128]{3,2,1,0:T(8,128)S(1)} collective-permute-done((f32[4,2,56,128]{3,2,1,0:T(8,128)S(1)}, f32[4,2,56,128]{3,2,1,0:T(8,128)S(1)}, u32[]{:S(2)}, u32[]{:S(2)}) %collective-permute-start.16) | collective-permute-done | bytes 229408 | tf_op jit(solution)/shard_map/ppermute | solution.py:574
  245.0 1.5 collective-permute-start.19
  249.0 8.8 %collective-permute-done.19 = f32[105984]{0:T(1024)S(1)} collective-permute-done((f32[105984]{0:T(1024)S(1)}, f32[105984]{0:T(1024)S(1)}, u32[]{:S(2)}, u32[]{:S(2)}) %collective-permute-start.19) | collective-permute-done | bytes 423968 | tf_op jit(solution)/shard_map/ppermute | solution.py:647
  257.8 1.0 stack.94
  258.8 7.6 %collective-permute-done.18 = f32[105984]{0:T(1024)S(1)} collective-permute-done((f32[105984]{0:T(1024)S(1)}, f32[105984]{0:T(1024)S(1)}, u32[]{:S(2)}, u32[]{:S(2)}) %collective-permute-start.18) | collective-permute-done | bytes 423968 | tf_op jit(solution)/shard_map/ppermute | solution.py:647
  266.4 1.0 stack.92
  267.5 1.4 collective-permute-start.8
  270.3 8.7 %collective-permute-done.8 = f32[207,512]{1,0:T(8,128)} collective-permute-done((f32[207,512]{1,0:T(8,128)S(1)}, f32[207,512]{1,0:T(8,128)}, u32[]{:S(2)}, u32[]{:S(2)}) %collective-permute-start.8) | collective-permute-done | bytes 423968 | tf_op jit(solution)/shard_map/ppermute | solution.py:647
  279.0 1.2 fusion.3
  280.9 4.3 %subtract_subtract_fusion = (f32[2,105984]{1,0:T(2,128)S(1)}, f32[2,105984]{1,0:T(2,128)S(1)}, f32[2,105984]{1,0:T(2,128)S(1)}, f32[2,105984]{1,0:T(2,128)S(1)}) fusion(f32[105984]{0:T(1024)S(1)} %copy-done.3, f32[]{:T(128)} %bitcast.69, f32[]{:T(128)} %bitcast.68, f32[105984]{0:T(1024)S(1)} %copy-done, f32[1,105984]{1,0:T(1,128)S(1)} %copy-done.8, ...), kind=kLoop, calls=%fused_computation.13 | loop fusion | flops 3815424 | bytes 6782992 | tf_op jit(solution)/shard_map/sub | solution.py:758
  285.2 1.0 slice.238
  288.8 1.4 fusion.7
  290.2 1.1 fusion.25
  (397 shorter events, 32.0 us)
Async XLA Ops:
  7.2 46.7 %copy-start.13 = (f32[1,4,128]{2,1,0:T(4,128)S(1)}, f32[1,4,128]{2,1,0:T(4,128)}, u32[]{:S(2)}) copy-start(f32[1,4,128]{2,1,0:T(4,128)} %param.22) | copy-start | bytes 6148
  7.2 97.4 %all-gather.2.cloned.1.call-start = ((), (), s32[]{:S(2)}) async-start(), calls=%async_computation.1 | async-start | bytes 3620864 | tf_op jit(solution)/shard_map/all_gather | solution.py:652
  10.1 21.8 %collective-permute-start = (bf16[168,512]{1,0:T(8,128)(2,1)S(1)}, bf16[168,512]{1,0:T(8,128)(2,1)S(1)}, u32[]{:S(2)}, u32[]{:S(2)}) collective-permute-start(bf16[168,512]{1,0:T(8,128)(2,1)S(1)} %select_select_fusion), channel_id=1, source_target_pairs={{0,8},{16,24}} | collective-permute-start | bytes 516104 | tf_op jit(solution)/shard_map/ppermute | solution.py:616
  16.9 201.5 %reduce-scatter.2.cloned.1.call-start = ((), (), s32[]{:S(2)}) async-start(), calls=%async_computation.2 | async-start | bytes 7241728 | tf_op jit(solution)/shard_map/reduce_scatter | solution.py:698
  31.9 2.1 collective-permute-start.4
  32.7 4.2 %collective-permute-start.1 = (bf16[168,512]{1,0:T(8,128)(2,1)S(1)}, bf16[168,512]{1,0:T(8,128)(2,1)S(1)}, u32[]{:S(2)}, u32[]{:S(2)}) collective-permute-start(bf16[168,512]{1,0:T(8,128)(2,1)S(1)} %fusion.33), channel_id=1, source_target_pairs={{0,4},{8,12},{16,20},{24,28}} | collective-permute-start | bytes 516104 | tf_op jit(solution)/shard_map/ppermute | solution.py:616
  35.4 4.0 %collective-permute-start.5 = (f32[2]{0:T(128)S(1)}, f32[2]{0:T(128)S(1)}, u32[]{:S(2)}, u32[]{:S(2)}) collective-permute-start(f32[2]{0:T(128)S(1)} %fusion.32), channel_id=1, source_target_pairs={{0,2},{1,3},{2,0},{3,1},{4,6},{5,7},{6,4},{7,5},{8,10},{9,11},{10,... | collective-permute-start | bytes 32 | tf_op jit(solution)/shard_map/ppermute | solution.py:574
  36.9 15.6 %collective-permute-start.2 = (bf16[168,512]{1,0:T(8,128)(2,1)S(1)}, bf16[168,512]{1,0:T(8,128)(2,1)S(1)}, u32[]{:S(2)}, u32[]{:S(2)}) collective-permute-start(bf16[168,512]{1,0:T(8,128)(2,1)S(1)} %add.167), channel_id=1, source_target_pairs={{0,2},{4,6},{8,10},{12,14},{16,18},{20,22},{24,26},{28,30}} | collective-permute-start | bytes 516104 | tf_op jit(solution)/shard_map/ppermute | solution.py:616
  40.8 4.1 %collective-permute-start.6 = (f32[2]{0:T(128)S(1)}, f32[2]{0:T(128)S(1)}, u32[]{:S(2)}, u32[]{:S(2)}) collective-permute-start(f32[2]{0:T(128)S(1)} %fusion.34), channel_id=1, source_target_pairs={{0,4},{1,5},{2,6},{3,7},{4,0},{5,1},{6,2},{7,3},{8,12},{9,13},{10,... | collective-permute-start | bytes 32 | tf_op jit(solution)/shard_map/ppermute | solution.py:574
  44.8 4.5 %collective-permute-start.7 = (f32[2]{0:T(128)S(1)}, f32[2]{0:T(128)S(1)}, u32[]{:S(2)}, u32[]{:S(2)}) collective-permute-start(f32[2]{0:T(128)S(1)} %add.174), channel_id=1, source_target_pairs={{0,8},{1,9},{2,10},{3,11},{4,12},{5,13},{6,14},{7,15},{8,0},{9,1},... | collective-permute-start | bytes 32 | tf_op jit(solution)/shard_map/ppermute | solution.py:574
  52.6 2.4 collective-permute-start.3
  126.4 0.8 copy-start.12
  126.4 1.4 copy-start.14
  164.2 36.9 %copy-start.11 = (f32[168,512]{1,0:T(8,128)S(1)}, f32[168,512]{1,0:T(8,128)}, u32[]{:S(2)}) copy-start(f32[168,512]{1,0:T(8,128)} %get-tuple-element.169) | copy-start | bytes 1032196
  202.1 1.6 collective-permute-start.9
  203.7 40.4 %copy-start.4 = (f32[1,105984]{1,0:T(1,128)S(1)}, f32[1,105984]{1,0:T(1,128)}, u32[]{:S(2)}) copy-start(f32[1,105984]{1,0:T(1,128)} %param.29) | copy-start | bytes 1271812
  203.7 5.1 %collective-permute-start.10 = (f32[4,48,128]{2,1,0:T(8,128)S(1)}, f32[4,48,128]{2,1,0:T(8,128)S(1)}, u32[]{:S(2)}, u32[]{:S(2)}) collective-permute-start(f32[4,48,128]{2,1,0:T(8,128)S(1)} %select_bitcast_fusion.7), channel_id=1, source_target_pairs={{0,2},{1,3},{2,0},{3,1},{4,6},{5,7},{6,4},{7,5},{8,10},{9,11},{10,... | collective-permute-start | bytes 294920 | tf_op jit(solution)/shard_map/ppermute | solution.py:574
  208.9 37.7 %copy-start.6 = (f32[1,105984]{1,0:T(1,128)S(1)}, f32[1,105984]{1,0:T(1,128)}, u32[]{:S(2)}) copy-start(f32[1,105984]{1,0:T(1,128)} %param.28) | copy-start | bytes 1271812
  208.9 4.2 %collective-permute-start.11 = (f32[2,48,128]{2,1,0:T(8,128)S(1)}, f32[2,48,128]{2,1,0:T(8,128)S(1)}, u32[]{:S(2)}, u32[]{:S(2)}) collective-permute-start(f32[2,48,128]{2,1,0:T(8,128)S(1)} %select_bitcast_fusion.10), channel_id=1, source_target_pairs={{0,4},{1,5},{2,6},{3,7},{4,0},{5,1},{6,2},{7,3},{8,12},{9,13},{10,... | collective-permute-start | bytes 147464 | tf_op jit(solution)/shard_map/ppermute | solution.py:574
  213.1 4.8 %collective-permute-start.12 = (f32[1,48,128]{2,1,0:T(8,128)S(1)}, f32[1,48,128]{2,1,0:T(8,128)S(1)}, u32[]{:S(2)}, u32[]{:S(2)}) collective-permute-start(f32[1,48,128]{2,1,0:T(8,128)S(1)} %select_bitcast_fusion.11), channel_id=1, source_target_pairs={{0,8},{1,9},{2,10},{3,11},{4,12},{5,13},{6,14},{7,15},{8,0},{9,1},... | collective-permute-start | bytes 73736 | tf_op jit(solution)/shard_map/ppermute | solution.py:574
  223.6 3.9 %collective-permute-start.13 = (f32[56,128]{1,0:T(8,128)S(1)}, f32[56,128]{1,0:T(8,128)S(1)}, u32[]{:S(2)}, u32[]{:S(2)}) collective-permute-start(f32[56,128]{1,0:T(8,128)S(1)} %get-tuple-element.233), channel_id=1, source_target_pairs={{0,16},{16,0},{1,17},{17,1},{2,18},{18,2},{3,19},{19,3},{4,20},{20... | collective-permute-start | bytes 86024 | tf_op jit(solution)/shard_map/ppermute | solution.py:647
  227.6 5.2 %collective-permute-start.14 = (f32[1,2,56,128]{3,2,1,0:T(8,128)S(1)}, f32[1,2,56,128]{3,2,1,0:T(8,128)S(1)}, u32[]{:S(2)}, u32[]{:S(2)}) collective-permute-start(f32[1,2,56,128]{3,2,1,0:T(8,128)S(1)} %maximum_bitcast_fusion.1), channel_id=1, source_target_pairs={{0,8},{1,9},{2,10},{3,11},{4,12},{5,13},{6,14},{7,15},{8,0},{9,1},... | collective-permute-start | bytes 172040 | tf_op jit(solution)/shard_map/ppermute | solution.py:574
  232.8 4.9 %collective-permute-start.15 = (f32[2,2,56,128]{3,2,1,0:T(8,128)S(1)}, f32[2,2,56,128]{3,2,1,0:T(8,128)S(1)}, u32[]{:S(2)}, u32[]{:S(2)}) collective-permute-start(f32[2,2,56,128]{3,2,1,0:T(8,128)S(1)} %maximum_bitcast_fusion), channel_id=1, source_target_pairs={{0,4},{1,5},{2,6},{3,7},{4,0},{5,1},{6,2},{7,3},{8,12},{9,13},{10,... | collective-permute-start | bytes 344072 | tf_op jit(solution)/shard_map/ppermute | solution.py:574
  237.7 29.8 %copy-start.2 = (f32[1,207,512]{2,1,0:T(8,128)S(1)}, f32[1,207,512]{2,1,0:T(8,128)}, u32[]{:S(2)}) copy-start(f32[1,207,512]{2,1,0:T(8,128)} %reduce-scatter.2.cloned.1.call-done) | copy-start | bytes 1271812
  237.7 6.1 %collective-permute-start.16 = (f32[4,2,56,128]{3,2,1,0:T(8,128)S(1)}, f32[4,2,56,128]{3,2,1,0:T(8,128)S(1)}, u32[]{:S(2)}, u32[]{:S(2)}) collective-permute-start(f32[4,2,56,128]{3,2,1,0:T(8,128)S(1)} %bitcast.213), channel_id=1, source_target_pairs={{0,2},{1,3},{2,0},{3,1},{4,6},{5,7},{6,4},{7,5},{8,10},{9,11},{10,... | collective-permute-start | bytes 688136 | tf_op jit(solution)/shard_map/ppermute | solution.py:574
  243.9 25.0 %collective-permute-start.17 = (f32[8,2,56,128]{3,2,1,0:T(8,128)S(1)}, f32[8,2,56,128]{3,2,1,0:T(8,128)S(1)}, u32[]{:S(2)}, u32[]{:S(2)}) collective-permute-start(f32[8,2,56,128]{3,2,1,0:T(8,128)S(1)} %bitcast.209), channel_id=1, source_target_pairs={{0,1},{1,0},{2,3},{3,2},{4,5},{5,4},{6,7},{7,6},{8,9},{9,8},{10,11... | collective-permute-start | bytes 1376264 | tf_op jit(solution)/shard_map/ppermute | solution.py:574
  245.0 12.8 %collective-permute-start.19 = (f32[105984]{0:T(1024)S(1)}, f32[105984]{0:T(1024)S(1)}, u32[]{:S(2)}, u32[]{:S(2)}) collective-permute-start(f32[105984]{0:T(1024)S(1)} %reduce.9), channel_id=1, source_target_pairs={{0,16},{16,0},{1,17},{17,1},{2,18},{18,2},{3,19},{19,3},{4,20},{20... | collective-permute-start | bytes 1271816 | tf_op jit(solution)/shard_map/ppermute | solution.py:647
  247.6 18.9 %collective-permute-start.18 = (f32[105984]{0:T(1024)S(1)}, f32[105984]{0:T(1024)S(1)}, u32[]{:S(2)}, u32[]{:S(2)}) collective-permute-start(f32[105984]{0:T(1024)S(1)} %reduce.8), channel_id=1, source_target_pairs={{0,16},{16,0},{1,17},{17,1},{2,18},{18,2},{3,19},{19,3},{4,20},{20... | collective-permute-start | bytes 1271816 | tf_op jit(solution)/shard_map/ppermute | solution.py:647
  267.5 11.5 %collective-permute-start.8 = (f32[207,512]{1,0:T(8,128)S(1)}, f32[207,512]{1,0:T(8,128)}, u32[]{:S(2)}, u32[]{:S(2)}) collective-permute-start(f32[207,512]{1,0:T(8,128)S(1)} %bitcast.212), channel_id=1, source_target_pairs={{0,16},{16,0},{1,17},{17,1},{2,18},{18,2},{3,19},{19,3},{4,20},{20... | collective-permute-start | bytes 1271816 | tf_op jit(solution)/shard_map/ppermute | solution.py:647
  269.3 11.5 %copy-start = (f32[105984]{0:T(1024)S(1)}, f32[105984]{0:T(1024)}, u32[]{:S(2)}) copy-start(f32[105984]{0:T(1024)} %param.27) | copy-start | bytes 1271812
  269.4 11.4 %copy-start.3 = (f32[105984]{0:T(1024)S(1)}, f32[105984]{0:T(1024)}, u32[]{:S(2)}) copy-start(f32[105984]{0:T(1024)} %get-tuple-element.227) | copy-start | bytes 1271812
  269.4 11.4 %copy-start.5 = (f32[1,105984]{1,0:T(1,128)S(1)}, f32[1,105984]{1,0:T(1,128)}, u32[]{:S(2)}) copy-start(f32[1,105984]{1,0:T(1,128)} %param.29) | copy-start | bytes 1271812
  269.5 11.4 %copy-start.7 = (f32[1,105984]{1,0:T(1,128)S(1)}, f32[1,105984]{1,0:T(1,128)}, u32[]{:S(2)}) copy-start(f32[1,105984]{1,0:T(1,128)} %param.28) | copy-start | bytes 1271812
  269.5 11.4 %copy-start.8 = (f32[1,105984]{1,0:T(1,128)S(1)}, f32[1,105984]{1,0:T(1,128)}, u32[]{:S(2)}) copy-start(f32[1,105984]{1,0:T(1,128)} %stack.94) | copy-start | bytes 1271812
  269.5 11.4 %copy-start.9 = (f32[1,105984]{1,0:T(1,128)S(1)}, f32[1,105984]{1,0:T(1,128)}, u32[]{:S(2)}) copy-start(f32[1,105984]{1,0:T(1,128)} %stack.92) | copy-start | bytes 1271812
  285.2 5.1 %copy-start.10 = (f32[105984]{0:T(1024)S(1)}, f32[105984]{0:T(1024)}, u32[]{:S(2)}) copy-start(f32[105984]{0:T(1024)} %param.30) | copy-start | bytes 1271812
  290.2 1.1 copy-start.1
Sparse Core Ops, SparseCore 0:
  17.0 44.0 all-gather.1
  126.6 86.3 reduce-scatter.1

commit v3 on v2

--- a/solution.py
+++ b/solution.py
@@ -52,22 +52,38 @@
     return lax.dot_general(a, b, (((0,), (0,)), ((), ())), preferred_element_type=F32)
 
 
+def advantage_body(rewards_ref, values_ref, next_ref, terminal_ref, truncated_ref, out_ref, sums_ref):
+    values = values_ref[...]
+    steps = values.shape[1]
+    lane = lax.broadcasted_iota(jnp.int32, values.shape, 1)
+    alive = 1.0 - terminal_ref[...].astype(F32)
+    cutoff = truncated_ref[...].astype(F32)
+    following = jnp.where(lane < steps - 1, pltpu.roll(values, steps - 1, 1), next_ref[...])
+    following = cutoff * next_ref[...] + (1.0 - cutoff) * following
+    series = rewards_ref[...] + DISCOUNT * alive * following - values
+    keeping = DISCOUNT * TRACE_DECAY * alive * (1.0 - cutoff)
+    step = 1
+    while step < steps:
+        inside = lane < steps - step
+        series = series + keeping * jnp.where(inside, pltpu.roll(series, steps - step, 1), 0.0)
+        keeping = keeping * jnp.where(inside, pltpu.roll(keeping, steps - step, 1), 0.0)
+        step *= 2
+    out_ref[...] = series
+    first = jnp.sum(jnp.sum(series, axis=0, keepdims=True), axis=1, keepdims=True)
+    square = jnp.sum(jnp.sum(series * series, axis=0, keepdims=True), axis=1, keepdims=True)
+    place = lax.broadcasted_iota(jnp.int32, (8, 128), 0)
+    sums_ref[...] = jnp.where(place == 0, first, square)
+
+
 def trajectory_advantages(rewards, values, next_values, terminal, truncated):
-    alive = 1.0 - terminal.astype(F32)
-    cutoff = truncated.astype(F32)
-    following = jnp.concatenate([values[:, 1:], next_values[:, -1:]], axis=1)
-    following = cutoff * next_values + (1.0 - cutoff) * following
-    deltas = rewards + DISCOUNT * alive * following - values
-    keeping = DISCOUNT * TRACE_DECAY * alive * (1.0 - cutoff)
-
-    def backward_step(carry, item):
-        delta, keep = item
-        result = delta + keep * carry
-        return (result, result)
-
-    start = jnp.zeros((rewards.shape[0],), F32)
-    _, series = lax.scan(backward_step, start, (deltas.T, keeping.T), reverse=True)
-    return series.T
+    return pl.pallas_call(
+        advantage_body,
+        out_shape=[
+            jax.ShapeDtypeStruct(rewards.shape, F32),
+            jax.ShapeDtypeStruct((8, 128), F32),
+        ],
+        name="advantages",
+    )(rewards, values, next_values, terminal, truncated)
 
 
 def unfold(block, phase, width, rows):
@@ -112,57 +128,49 @@
     w1_low = w1.astype(BF16)
     w2_low = w2.astype(BF16)
     w3_low = w3.astype(BF16)
-    for ref in (t1_ref, t2_ref, t3_ref, back3_ref, back2_ref):
-        ref[...] = jnp.zeros(ref.shape, BF16)
+    t1_ref[...] = jnp.zeros(t1_ref.shape, BF16)
+    for q in range(2):
+        for p in range(2):
+            row = 64 * q + 32 * p
+            for i in range(8):
+                lane = (i + 4 * p) * 16
+                k = 32 * i + 16 * q
+                t1_ref[row : row + 32, lane : lane + 16] = w1_low[0:32, k : k + 16]
     for p in range(2):
-        for q in range(4):
-            d = 4 * p + q
-            for i in range(8):
-                lane = (i + 4 * p) * 80 + 16 * q
-                t1_ref[32 * d : 32 * d + 32, lane : lane + 32] = w1_low[0:32, 32 * i : 32 * i + 32]
-            b1_ref[32 * d : 32 * d + 32] = jnp.broadcast_to(w1[0:32, 256:257], (32, 256))
-    for q in range(3):
+        b1_ref[32 * p : 32 * p + 32] = jnp.broadcast_to(w1[0:32, 256:257], (32, 256))
+    b2_ref[...] = jnp.broadcast_to(w2[0:64, 512:513], (64, 256))
+    b3_ref[...] = jnp.broadcast_to(w3[0:64, 576:577], (64, 256))
+    for q in range(2):
         for i in range(4):
-            lane = 256 * i + 64 * q
-            t2_ref[64 * q : 64 * q + 64, lane : lane + 128] = w2_low[0:64, 128 * i : 128 * i + 128]
-        b2_ref[64 * q : 64 * q + 64] = jnp.broadcast_to(w2[0:64, 512:513], (64, 256))
-    for q in range(7):
+            k = 128 * i + 64 * q
+            t2_ref[64 * q : 64 * q + 64, 64 * i : 64 * i + 64] = w2_low[0:64, k : k + 64]
+    for j in range(3):
         for i in range(3):
-            lane = 576 * i + 64 * q
-            t3_ref[64 * q : 64 * q + 64, lane : lane + 192] = w3_low[0:64, 192 * i : 192 * i + 192]
-        b3_ref[64 * q : 64 * q + 64] = jnp.broadcast_to(w3[0:64, 576:577], (64, 256))
-    for x in range(9):
-        for r in range(3):
-            for q in range(max(0, x - 2), min(6, x) + 1):
-                k = ((2 - r) * 3 + x - q) * 64
-                lane = 512 * r + 64 * q
-                back3_ref[64 * x : 64 * x + 64, lane : lane + 64] = w3_ref[k : k + 64, 0:64].astype(
+            here = (slice(64 * j, 64 * j + 64), slice(64 * i, 64 * i + 64))
+            k = (3 * i + j) * 64
+            t3_ref[here] = w3_low[0:64, k : k + 64]
+            k = (3 * (2 - i) + j) * 64
+            back3_ref[here] = w3_ref[k : k + 64, 0:64].astype(BF16)
+    for x in range(4):
+        for y in range(2):
+            for r in range(2):
+                k = ((y + 2 - 2 * r) * 4 + x) * 32
+                row = 32 * (2 * x + y)
+                back2_ref[row : row + 32, 64 * r : 64 * r + 64] = w2_ref[k : k + 32, 0:64].astype(
                     BF16
                 )
-    for y in range(2):
-        for x in range(4):
-            for r in range(2):
-                for q in range(3):
-                    j = x + 2 - 2 * q
-                    if 0 <= j < 4:
-                        k = ((y + 2 - 2 * r) * 4 + j) * 32
-                        row = 32 * (4 * y + x)
-                        lane = 64 * (3 * r + q)
-                        back2_ref[row : row + 32, lane : lane + 64] = w2_ref[
-                            k : k + 32, 0:64
-                        ].astype(BF16)
 
 
 def conv_weights(block):
     shapes = [
-        ((256, 960), BF16),
-        ((256, 256), F32),
-        ((192, 1024), BF16),
-        ((192, 256), F32),
-        ((448, 1728), BF16),
-        ((448, 256), F32),
-        ((576, 1536), BF16),
-        ((256, 384), BF16),
+        ((128, 192), BF16),
+        ((64, 256), F32),
+        ((128, 256), BF16),
+        ((64, 256), F32),
+        ((192, 192), BF16),
+        ((64, 256), F32),
+        ((192, 192), BF16),
+        ((256, 128), BF16),
     ]
     return pl.pallas_call(
         weights_body,
@@ -178,11 +186,11 @@
     )(block)
 
 
-def pixel_window(x_refs, first, n):
+def pixel_window(x_refs, first, start, width):
     sides = []
     for e in range(2):
-        parts = [x_refs[first + k][e, :, 64 * n : 64 * n + 80, :] for k in range(3)]
-        sides.append(jnp.concatenate(parts, axis=0).reshape(960, 128))
+        parts = [x_refs[first + k][e, :, start : start + width, :] for k in range(3)]
+        sides.append(jnp.concatenate(parts, axis=0).reshape(12 * width, 128))
     return jnp.concatenate(sides, axis=1)
 
 
@@ -191,31 +199,45 @@
 ):
     x_refs = (x0, x1, x2, x3, x4)
     t = pl.program_id(1)
+
+    def low(value, bias_ref):
+        return jnp.maximum(value + bias_ref[...], 0.0).astype(BF16)
+
     for h in range(2):
-        for n in range(5):
-            window = pixel_window(x_refs, 2 * h, n)
-            out = jnp.maximum(mm(t1_ref[...], window) + b1_ref[...], 0.0).astype(BF16)
-            a1_ref[pl.ds(4 * t + 2 * h, 2), 4 * n : 4 * n + 4] = out.reshape(2, 4, C1, 256)
+        held = None
+        for n in range(21):
+            got = mm(t1_ref[...], pixel_window(x_refs, 2 * h, 16 * n, 16))
+            if n > 0:
+                out = low(held + got[64:128], b1_ref)
+                a1_ref[pl.ds(4 * t + 2 * h, 2), n - 1] = out.reshape(2, C1, 256)
+            held = got[0:64]
 
     @pl.when(t == 4)
     def _():
         def conv_two(p, carry):
-            for g in range(3):
-                window = a1_ref[pl.ds(2 * p, 4), 6 * g : 6 * g + 8].reshape(1024, 256)
-                out = jnp.maximum(mm(t2_ref[...], window) + b2_ref[...], 0.0).astype(BF16)
-                a2_ref[p, 3 * g : 3 * g + 3] = out.reshape(3, C2, 256)
+            held = None
+            for n in range(10):
+                window = a1_ref[pl.ds(2 * p, 4), 2 * n : 2 * n + 2].reshape(256, 256)
+                got = mm(t2_ref[...], window)
+                if n > 0:
+                    a2_ref[p, n - 1] = low(held + got[64:128], b2_ref)
+                held = got[0:64]
             a2_ref[p, 9] = jnp.zeros((C2, 256), BF16)
             return carry
 
-        lax.fori_loop(0, 9, conv_two, 0)
+        lax.fori_loop(0, 9, conv_two, 0, unroll=3)
 
         def conv_three(p, carry):
-            window = a2_ref[pl.ds(p, 3), 0:9].reshape(1728, 256)
-            out = jnp.maximum(mm(t3_ref[...], window) + b3_ref[...], 0.0).astype(BF16)
-            a3_ref[p] = out.reshape(7, C3, 256)
+            held, older = None, None
+            for x in range(9):
+                got = mm(t3_ref[...], a2_ref[pl.ds(p, 3), x].reshape(192, 256))
+                if x > 1:
+                    a3_ref[p, x - 2] = low(older + got[128:192], b3_ref)
+                older = held + got[64:128] if x > 0 else None
+                held = got[0:64]
             return carry
 
-        lax.fori_loop(0, 7, conv_three, 0)
+        lax.fori_loop(0, 7, conv_three, 0, unroll=7)
 
 
 def whole(shape):
@@ -237,12 +259,12 @@
         grid=(envs // 2, 5),
         in_specs=pixel_specs()
         + [
-            whole((256, 960)),
-            whole((256, 256)),
-            whole((192, 1024)),
-            whole((192, 256)),
-            whole((448, 1728)),
-            whole((448, 256)),
+            whole((128, 192)),
+            whole((64, 256)),
+            whole((128, 256)),
+            whole((64, 256)),
+            whole((192, 192)),
+            whole((64, 256)),
         ],
         out_specs=[
             pl.BlockSpec((20, 20, C1, 256), lambda j, t: (0, 0, 0, j)),
@@ -262,8 +284,7 @@
 def dense_body(
     scale,
     a3_ref,
-    wd_ref,
-    bd_ref,
+    gathered_ref,
     wh_ref,
     bh_ref,
     normed_ref,
@@ -276,8 +297,24 @@
     gbh_ref,
     loss_ref,
     wide_ref,
+    wd_ref,
 ):
-    hidden_pre = mm_tn(wd_ref[...], a3_ref[...]) + bd_ref[...]
+    late = lax.broadcasted_iota(jnp.int32, (1, HID), 1) >= PHASE
+    shards, rows, _ = gathered_ref.shape
+    for k in range(shards):
+        if rows * k <= TOP + 1 + FEATURES and rows * (k + 1) > TOP:
+            wide_ref[rows * k : rows * k + rows] = gathered_ref[k].astype(F32)
+    for i in range(0, FEATURES, 448):
+        wd_ref[i : i + 448] = jnp.where(
+            late, wide_ref[TOP + i : TOP + i + 448], wide_ref[TOP + 1 + i : TOP + 449 + i]
+        ).astype(BF16)
+    bias = jnp.where(
+        late,
+        wide_ref[TOP + FEATURES : TOP + 1 + FEATURES],
+        wide_ref[TOP + 1 + FEATURES : TOP + 2 + FEATURES],
+    )
+    bias = jnp.broadcast_to(bias, (8, HID)).T[:, 0:1]
+    hidden_pre = mm_tn(wd_ref[...], a3_ref[...]) + bias
     hidden = jnp.maximum(hidden_pre, 0.0).astype(BF16)
     out = mm(wh_ref[...], hidden) + bh_ref[...]
     row = lax.broadcasted_iota(jnp.int32, out.shape, 0)
@@ -323,35 +360,44 @@
     wide_ref[last:] = jnp.zeros((wide_ref.shape[0] - last, HID), F32)
     ones = jnp.ones((8, d_hidden.shape[1]), BF16)
     wide_ref[last : last + 1] = mm_nt(ones, d_hidden)[0:1]
-    late = lax.broadcasted_iota(jnp.int32, (1, HID), 1) >= PHASE
-    shards, rows, _ = packed_ref.shape
     for k in range(shards):
         first = rows * k + LEAD - TOP - 1
-        packed_ref[k] = jnp.where(
-            late, wide_ref[first + 1 : first + 1 + rows], wide_ref[first : first + rows]
-        )
+        for j in range(4):
+            cols = slice(128 * j, 128 * j + 128)
+            early_part = wide_ref[first : first + rows, cols]
+            if 128 * j + 128 <= PHASE:
+                part = early_part
+            elif 128 * j >= PHASE:
+                part = wide_ref[first + 1 : first + 1 + rows, cols]
+            else:
+                part = jnp.where(
+                    late[:, cols], wide_ref[first + 1 : first + 1 + rows, cols], early_part
+                )
+            packed_ref[k, pl.ds(j, rows, stride=4), :] = part
     d_a3 = mm(wd_ref[...], d_hidden)
     dc3_ref[...] = jnp.where(a3_ref[...] > 0, d_a3, 0.0).astype(BF16)
 
 
-def dense_step(scale, shards, shard_rows, a3, wd, bd, wh, bh, normed, returns, actions, behavior):
+def dense_step(scale, a3, gathered, wh, bh, normed, returns, actions, behavior):
     frames = a3.shape[1]
+    shards, shard_rows, _ = gathered.shape
     rows = wh.shape[0]
     return pl.pallas_call(
         lambda *refs: dense_body(scale, *refs),
         out_shape=[
-            jax.ShapeDtypeStruct((shards, shard_rows, HID), F32),
+            jax.ShapeDtypeStruct((shards, 4 * shard_rows, 128), F32),
             jax.ShapeDtypeStruct((FEATURES, frames), BF16),
             jax.ShapeDtypeStruct((rows, HID), F32),
             jax.ShapeDtypeStruct((rows, 1), F32),
             jax.ShapeDtypeStruct((1, 1), F32),
         ],
         scratch_shapes=[
-            pltpu.VMEM((max(shards * shard_rows, TOP + 1 + FEATURES) + 2 * LEAD - TOP, HID), F32)
+            pltpu.VMEM((max(shards * shard_rows, TOP + 1 + FEATURES) + 2 * LEAD - TOP, HID), F32),
+            pltpu.VMEM((FEATURES, HID), BF16),
         ],
         compiler_params=pltpu.CompilerParams(vmem_limit_bytes=VMEM_LIMIT),
         name="dense_step",
-    )(a3, wd, bd, wh, bh, normed, returns, actions, behavior)
+    )(a3, gathered, wh, bh, normed, returns, actions, behavior)
 
 
 def fold(g_ref, width, rows):
@@ -365,7 +411,7 @@
             piece = jnp.where(lane < width, piece, 0.0)
             total = total + (pltpu.roll(piece, width * t, 1) if t else piece)
         columns.append(total)
-    return jnp.concatenate(columns, axis=1)
+    return columns
 
 
 def upper_body(
@@ -415,37 +461,40 @@
 
     lax.fori_loop(0, 7, fill, 0)
 
-    def three_weights(p, carry):
-        left = mm_nt(a2_ref[pl.ds(p, 3), 0:6].reshape(1152, 256), d3_ref[p + 2, 0:4].reshape(256, 256))
-        right = mm_nt(
-            a2_ref[pl.ds(p, 3), 4:10].reshape(1152, 256), d3_ref[p + 2, 4:8].reshape(256, 256)
-        )
-        r3_ref[...] += left + right
+    left = [a2_ref[p : p + 3, 4 * g : 4 * g + 6].reshape(1152, 256) for p in range(7) for g in range(2)]
+    right = [d3_ref[p + 2, 4 * g : 4 * g + 4].reshape(256, 256) for p in range(7) for g in range(2)]
+    r3_ref[...] += mm_nt(jnp.concatenate(left, axis=1), jnp.concatenate(right, axis=1))
+
+    def three_input(y, carry):
+        total = jnp.zeros((C2, 256), F32)
+        parts = []
+        for x in range(9):
+            if x < 7:
+                parts.append(mm(t3_ref[...], d3_ref[pl.ds(y, 3), x].reshape(192, 256)))
+            back = 0.0
+            for j in range(3):
+                if 0 <= x - j < 7:
+                    back = back + parts[x - j][64 * j : 64 * j + 64]
+            masked = jnp.where(a2_ref[y, x] > 0, back, 0.0).astype(BF16)
+            d2_ref[y + 1, x + 1] = masked
+            total = total + masked.astype(F32)
+        s2_ref[...] += total
         return carry
 
-    lax.fori_loop(0, 7, three_weights, 0)
-
-    def three_input(y, carry):
-        back = mm(t3_ref[...], d3_ref[pl.ds(y, 3)].reshape(1536, 256)).reshape(9, C2, 256)
-        masked = jnp.where(a2_ref[y, 0:9] > 0, back, 0.0).astype(BF16)
-        d2_ref[y + 1, 1:10] = masked
-        s2_ref[...] += jnp.sum(masked.astype(F32), axis=0)
+    lax.fori_loop(0, 9, three_input, 0, unroll=3)
+    load_a1.wait()
+
+    def two_weights(r, carry):
+        left, right = [], []
+        for k in range(3):
+            p = 3 * r + k
+            for g in range(3):
+                left.append(a1_ref[pl.ds(2 * p, 4), 6 * g : 6 * g + 8].reshape(1024, 256))
+                right.append(d2_ref[p + 1, 1 + 3 * g : 4 + 3 * g].reshape(192, 256))
+        r2_ref[:, 0:192] += mm_nt(jnp.concatenate(left, axis=1), jnp.concatenate(right, axis=1))
         return carry
 
-    lax.fori_loop(0, 9, three_input, 0)
-    load_a1.wait()
-
-    def two_weights(p, carry):
-        total = 0.0
-        for g in range(3):
-            total = total + mm_nt(
-                a1_ref[pl.ds(2 * p, 4), 6 * g : 6 * g + 8].reshape(1024, 256),
-                d2_ref[p + 1, 1 + 3 * g : 4 + 3 * g].reshape(192, 256),
-            )
-        r2_ref[:, 0:192] += total
-        return carry
-
-    lax.fori_loop(0, 9, two_weights, 0)
+    lax.fori_loop(0, 3, two_weights, 0)
 
     @pl.when(step == pl.num_programs(0) - 1)
     def _():
@@ -468,9 +517,14 @@
         lane = lax.broadcasted_iota(jnp.int32, (1, HID), 1)
         packed_ref[...] = jnp.zeros(packed_ref.shape, F32)
         for ref, rows, base, phase in ((g2_ref, 72, 16, 32), (g3_ref, 80, 80, 96)):
-            turned = pltpu.roll(fold(ref, 64, rows), phase, 1)
-            packed_ref[base : base + rows] += jnp.where(lane >= phase, turned, 0.0)
-            packed_ref[base + 1 : base + 1 + rows] += jnp.where(lane < phase, turned, 0.0)
+            turned = pltpu.roll(jnp.concatenate(fold(ref, 64, rows), axis=1), phase, 1)
+            for j in range(4):
+                cols = slice(128 * j, 128 * j + 128)
+                here = pl.ds(4 * base + j, rows, stride=4)
+                packed_ref[here, :] += jnp.where(lane >= phase, turned, 0.0)[:, cols]
+                if j == 0:
+                    below = pl.ds(4 * base + 4, rows, stride=4)
+                    packed_ref[below, :] += jnp.where(lane < phase, turned, 0.0)[:, cols]
 
 
 def upper_backward(a1, a2, dc3, t3):
@@ -482,15 +536,15 @@
             pl.BlockSpec(memory_space=pl.ANY),
             pl.BlockSpec((9, 10, C2, 256), lambda j: (0, 0, 0, j)),
             pl.BlockSpec((7, 7, C3, 256), lambda j: (0, 0, 0, j)),
-            whole((576, 1536)),
+            whole((192, 192)),
         ],
         out_specs=[
             pl.BlockSpec((11, 11, C2, 256), lambda j: (0, 0, 0, j)),
-            whole((BLOCK_ROWS, HID)),
+            whole((4 * BLOCK_ROWS, 128)),
         ],
         out_shape=[
             jax.ShapeDtypeStruct((11, 11, C2, frames), BF16),
-            jax.ShapeDtypeStruct((BLOCK_ROWS, HID), F32),
+            jax.ShapeDtypeStruct((4 * BLOCK_ROWS, 128), F32),
         ],
         scratch_shapes=[
             pltpu.VMEM((1024, 256), F32),
@@ -508,7 +562,9 @@
     )(a1, a2, dc3, t3)
 
 
-def lower_body(x0, x1, x2, x3, x4, a1_ref, d2_ref, t2_ref, packed_ref, r1_ref, s1_ref, g1_ref):
+def lower_body(
+    x0, x1, x2, x3, x4, a1_ref, d2_ref, t2_ref, packed_ref, r1_ref, s1_ref, g1_ref, d1_ref
+):
     x_refs = (x0, x1, x2, x3, x4)
     t = pl.program_id(1)
 
@@ -517,19 +573,27 @@
         r1_ref[...] = jnp.zeros(r1_ref.shape, F32)
         s1_ref[...] = jnp.zeros(s1_ref.shape, F32)
 
-    total = 0.0
     sums = jnp.zeros((C1, 256), F32)
     for h in range(2):
-        for n in range(5):
-            back = mm(
-                t2_ref[...],
-                d2_ref[pl.ds(2 * t + h, 2), 2 * n : 2 * n + 3].reshape(384, 256),
-            )
-            kept = a1_ref[2 * h : 2 * h + 2, 4 * n : 4 * n + 4].reshape(256, 256) > 0
-            masked = jnp.where(kept, back, 0.0).astype(BF16)
-            sums = sums + jnp.sum(masked.astype(F32).reshape(8, C1, 256), axis=0)
-            total = total + mm_nt(pixel_window(x_refs, 2 * h, n), masked)
-    r1_ref[...] += total
+        held = None
+        for n in range(10):
+            back = held
+            if n < 9:
+                got = mm(t2_ref[...], d2_ref[pl.ds(2 * t + h, 2), n + 1].reshape(128, 256))
+                back = got[0:128] if n == 0 else held + got[0:128]
+                held = got[128:256]
+            for x in range(2):
+                for y in range(2):
+                    k = 32 * (2 * x + y)
+                    kept = a1_ref[2 * h + y, 2 * n + x] > 0
+                    masked = jnp.where(kept, back[k : k + 32], 0.0).astype(BF16)
+                    sums = sums + masked.astype(F32)
+                    row = 128 * (n % 2) + k
+                    d1_ref[row : row + 32, 256 * (n // 2) : 256 * (n // 2) + 256] = masked
+        window = jnp.concatenate(
+            [pixel_window(x_refs, 2 * h, 64 * n, 80) for n in range(5)], axis=1
+        )
+        r1_ref[...] += mm_nt(window, d1_ref[...])
     s1_ref[...] += sums
 
     @pl.when((pl.program_id(0) == pl.num_programs(0) - 1) & (t == 4))
@@ -540,11 +604,15 @@
             for p in range(2):
                 for q in range(4):
                     k = (i + 4 * p) * 80 + 16 * q
-                    slab = r1_ref[k : k + 32, 128 * p : 128 * p + 128]
-                    total = total + (pltpu.roll(slab, 128 - 32 * q, 1) if q else slab)
+                    col = 128 * (q // 2)
+                    turn = 64 * (q % 2) + 32 * p
+                    slab = r1_ref[k : k + 32, col : col + 128]
+                    total = total + (pltpu.roll(slab, 128 - turn, 1) if turn else slab)
             g1_ref[32 * i : 32 * i + 32] = total
         g1_ref[256:257, 0:32] = jnp.sum(s1_ref[...].T, axis=0, keepdims=True)
-        packed_ref[...] = fold(g1_ref, 32, 24)
+        packed_ref[...] = jnp.zeros(packed_ref.shape, F32)
+        for j, part in enumerate(fold(g1_ref, 32, 24)):
+            packed_ref[pl.ds(j, 24, stride=4), :] = part
 
 
 def lower_backward(x, a1, d2, t2):
@@ -556,14 +624,15 @@
         + [
             pl.BlockSpec((4, 20, C1, 256), lambda j, t: (t, 0, 0, j)),
             pl.BlockSpec((11, 11, C2, 256), lambda j, t: (0, 0, 0, j)),
-            whole((256, 384)),
-        ],
-        out_specs=whole((24, HID)),
-        out_shape=jax.ShapeDtypeStruct((24, HID), F32),
+            whole((256, 128)),
+        ],
+        out_specs=whole((4 * BLOCK_ROWS, 128)),
+        out_shape=jax.ShapeDtypeStruct((4 * BLOCK_ROWS, 128), F32),
         scratch_shapes=[
             pltpu.VMEM((960, 256), F32),
             pltpu.VMEM((C1, 256), F32),
             pltpu.VMEM((384, 128), F32),
+            pltpu.VMEM((256, 1280), BF16),
         ],
         compiler_params=pltpu.CompilerParams(vmem_limit_bytes=VMEM_LIMIT),
         name="lower_backward",
@@ -605,20 +674,84 @@
     return blocks
 
 
-def first_rows_everywhere(local, lanes, place):
+def first_rows_everywhere(local, sums, lanes, place):
     rows = local.shape[0]
     owners = -(-(TOP + 1) // rows)
+    order = halving_order(lanes)
     if owners == 1:
         block = jnp.pad(local[: TOP + 1], ((0, BLOCK_ROWS - TOP - 1), (0, 0)))
         block = jnp.where(place == 0, block, jnp.zeros((), BF16))
-        for step in reversed(halving_order(lanes)):
+        for step in reversed(order):
             pairs = [(i, i + step) for i in range(0, lanes, 2 * step)]
-            block = block + lax.ppermute(block, "dp", pairs)
-        return block
+            came = lax.ppermute(block, "dp", pairs)
+            block, sums = lax.optimization_barrier((block + came, sums + swap(sums, lanes, step)))
+        return block, sums
     block = jnp.zeros((owners, rows, HID), BF16)
     block = jnp.where(jnp.arange(owners)[:, None, None] == place, local[None], block)
     block = sum_everywhere(block, lanes).reshape(owners * rows, HID)[: TOP + 1]
-    return jnp.pad(block, ((0, BLOCK_ROWS - TOP - 1), (0, 0)))
+    return jnp.pad(block, ((0, BLOCK_ROWS - TOP - 1), (0, 0))), sum_everywhere(sums, lanes)
+
+
+def finish_body(
+    scalars_ref,
+    mine_ref,
+    other_ref,
+    mine_extra_ref,
+    other_extra_ref,
+    first_ref,
+    other_first_ref,
+    second_ref,
+    other_second_ref,
+    master_ref,
+    momentum_ref,
+    clipped_ref,
+    first_out,
+    second_out,
+    moved_ref,
+    momentum_out,
+    final_ref,
+    low_ref,
+):
+    master = master_ref[...]
+
+    def inner_step(factor, dense_ref, extra_ref, one_ref, two_ref):
+        clipped = (dense_ref[...] + extra_ref[...]) * factor
+        first_next = BETA_ONE * one_ref[...] + (1.0 - BETA_ONE) * clipped
+        second_next = BETA_TWO * two_ref[...] + (1.0 - BETA_TWO) * clipped * clipped
+        first_hat = first_next / scalars_ref[2]
+        second_hat = second_next / scalars_ref[3]
+        inner = master - LEARN_RATE * (
+            first_hat / (jnp.sqrt(second_hat) + ADAM_EPSILON) + WEIGHT_DECAY * master
+        )
+        return clipped, first_next, second_next, master - inner
+
+    clipped, first_next, second_next, drift = inner_step(
+        scalars_ref[0], mine_ref, mine_extra_ref, first_ref, second_ref
+    )
+    clipped_ref[...] = clipped
+    first_out[...] = first_next
+    second_out[...] = second_next
+    _, _, _, other_drift = inner_step(
+        scalars_ref[1], other_ref, other_extra_ref, other_first_ref, other_second_ref
+    )
+    moved = (drift + other_drift) / 2.0
+    moved_ref[...] = moved
+    momentum_next = OUTER_MOMENTUM * momentum_ref[...] + moved
+    momentum_out[...] = momentum_next
+    final = master - OUTER_RATE * (moved + OUTER_MOMENTUM * momentum_next)
+    final_ref[...] = final
+    low_ref[...] = final.astype(BF16)
+
+
+def finish(scalars, *arrays):
+    shape = arrays[0].shape
+    return pl.pallas_call(
+        finish_body,
+        in_specs=[pl.BlockSpec(memory_space=pltpu.SMEM)]
+        + [pl.BlockSpec(memory_space=pltpu.VMEM)] * len(arrays),
+        out_shape=[jax.ShapeDtypeStruct(shape, F32)] * 6 + [jax.ShapeDtypeStruct(shape, BF16)],
+        name="finish",
+    )(scalars, *arrays)
 
 
 def on_device(
@@ -648,46 +781,39 @@
 
     master_rows = master.reshape(rows, HID)
     low_rows = master_rows.astype(BF16)
-    block = first_rows_everywhere(low_rows, lanes, place)
-    gathered = lax.all_gather(low_rows, "dp", axis=0).reshape(lanes * rows, HID)
-
-    advantage = trajectory_advantages(
+    gathered = lax.all_gather(low_rows, "dp", axis=0)
+
+    advantage, sums = trajectory_advantages(
         rewards[0], old_values[0], next_values[0], terminal[0], truncated[0]
     )
     envs_here, steps_here = advantage.shape
     batch = envs_here * steps_here
     total_frames = batch * lanes
-    sums = jnp.stack([jnp.sum(advantage), jnp.sum(advantage * advantage)])
-    first_sum, square_sum = sum_everywhere(sums, lanes)
-    mean = first_sum / total_frames
-    spread = square_sum / total_frames - mean * mean
+    block, sums = first_rows_everywhere(low_rows, sums, lanes, place)
+    mean = sums[0, 0] / total_frames
+    spread = sums[1, 0] / total_frames - mean * mean
     normed = ((advantage - mean) * lax.rsqrt(spread + 1e-05)).reshape(1, batch)
     returns = (advantage + old_values[0]).reshape(1, batch)
 
     x = frames[0].transpose(0, 2, 3, 1)
     t1, b1, t2, b2, t3, b3, back3, back2 = conv_weights(block)
     a1, a2, a3 = conv_forward(x, t1, b1, t2, b2, t3, b3)
-
-    column = lax.broadcasted_iota(jnp.int32, (1, HID), 1)
-    late = column >= PHASE
-    w_dense = jnp.where(
-        late, gathered[TOP : TOP + FEATURES], gathered[TOP + 1 : TOP + 1 + FEATURES]
-    )
-    b_dense = jnp.where(
-        late[0], gathered[TOP + FEATURES], gathered[TOP + 1 + FEATURES]
-    ).astype(F32)
+    _, first_sent, second_sent = lax.optimization_barrier((block, first_moment[0], second_moment[0]))
+    a3, other_first, other_second = lax.optimization_barrier(
+        (a3, other_group(first_sent), other_group(second_sent))
+    )
+
     tail = TOP + FEATURES + 1
-    head_flat = gathered[tail:].reshape(-1)[PHASE : PHASE + HEAD_LEN]
+    head_owner = tail // rows
+    head_flat = gathered[head_owner:].reshape((lanes - head_owner) * rows, HID)
+    head_flat = head_flat[tail - head_owner * rows :].reshape(-1)[PHASE : PHASE + HEAD_LEN]
     w_head = head_flat[: HID * (ACTIONS + 1)].reshape(HID, ACTIONS + 1)
     w_head = jnp.pad(jnp.roll(w_head, PHASE, axis=0).T, ((0, 13), (0, 0)))
     b_head = jnp.pad(head_flat[HID * (ACTIONS + 1) :], (0, 13)).astype(F32)
     packed_dense, d_c3, g_head, g_head_bias, loss_local = dense_step(
         1.0 / total_frames,
-        lanes,
-        rows,
         a3.reshape(FEATURES, batch),
-        w_dense,
-        b_dense[:, None],
+        gathered,
         w_head,
         b_head[:, None],
         normed,
@@ -707,68 +833,74 @@
             g_head_bias[: ACTIONS + 1, 0],
             jnp.zeros((tail_rows * HID - PHASE - HEAD_LEN,), F32),
         ]
-    ).reshape(tail_rows, HID)
-    small = jnp.concatenate(
-        [jnp.pad(lower, ((0, BLOCK_ROWS - 24), (0, 0))) + upper, head_part], axis=0
-    )
-    unit = lanes * 8 // math.gcd(lanes * 8, 4)
-    count = -(-small.shape[0] // unit) * unit
-    small = jnp.pad(small, ((0, count - small.shape[0]), (0, 0)))
-    piece = scatter_sum(small.reshape(lanes, count * 4 // lanes, 128), lanes, place)
+    ).reshape(4 * tail_rows, 128)
+    real = 4 * (BLOCK_ROWS + tail_rows)
+    count = -(-real // (8 * lanes)) * 8 * lanes
+    head_part = jnp.pad(head_part, ((0, count - real), (0, 0)))
+    small = jnp.concatenate([lower + upper, head_part], axis=0)
+    piece = scatter_sum(small.reshape(lanes, count // lanes, 128), lanes, place)
     squares = jnp.sum(dense_owned * dense_owned) + jnp.sum(piece * piece)
-    facts = jnp.zeros((8, 128), F32).at[0, 0].set(squares).at[0, 1].set(loss_local[0, 0])
-    message = jnp.concatenate([piece, facts], axis=0)
-    message = jnp.stack([message, other_group(message)])
-    messages = gather_blocks(message, lanes, place)
-    own_facts = jnp.sum(messages[:, :, -8], axis=0)
-    norm = jnp.sqrt(own_facts[:, 0])
-    loss_total = own_facts[0, 1]
-    smalls = messages[:, :, :-8].transpose(1, 0, 2, 3).reshape(2, count, HID)
+    row = lax.broadcasted_iota(jnp.int32, (8, 128), 0)
+    message = jnp.concatenate([piece, jnp.where(row == 0, squares, loss_local)], axis=0)
+    messages = gather_blocks(jnp.stack([message, other_group(message)]), lanes, place)
+    facts = jnp.sum(messages[:, :, -8:-6, 0], axis=0)
+    norm = jnp.sqrt(facts[:, 0])
+    loss_total = facts[0, 1]
+    smalls = messages[:, :, :-8].transpose(1, 0, 2, 3).reshape(2, count, 128)
+
+    own_len = 4 * rows
 
     def own_rows(part, first_row):
-        first = first_row // rows
-        blocks = -(-(first_row + part.shape[1]) // rows) - first
+        first = first_row // own_len
+        blocks = -(-(first_row + part.shape[1]) // own_len) - first
+        before = first_row - first * own_len
         part = jnp.pad(
-            part,
-            (
-                (0, 0),
-                (first_row - first * rows, (first + blocks) * rows - first_row - part.shape[1]),
-                (0, 0),
-            ),
+            part, ((0, 0), (before, blocks * own_len - before - part.shape[1]), (0, 0))
         )
         here = (place >= first) & (place < first + blocks)
-        start = jnp.clip(place - first, 0, blocks - 1) * rows
-        return jnp.where(here, lax.dynamic_slice_in_dim(part, start, rows, 1), 0.0)
-
-    owned = jnp.stack([dense_owned, other_group(dense_owned)])
-    owned = owned + own_rows(smalls[:, : TOP + 1], 0)
-    owned = owned + own_rows(smalls[:, BLOCK_ROWS : BLOCK_ROWS + tail_rows], tail)
-    firsts = jnp.stack([first_moment[0], other_group(first_moment[0])])
-    seconds = jnp.stack([second_moment[0], other_group(second_moment[0])])
+        start = jnp.clip(place - first, 0, blocks - 1) * own_len
+        return jnp.where(here, lax.dynamic_slice_in_dim(part, start, own_len, 1), 0.0)
+
+    extra = own_rows(smalls[:, : 4 * (TOP + 1)], 0)
+    extra = extra + own_rows(smalls[:, 4 * BLOCK_ROWS : real], 4 * tail)
     factor = jnp.minimum(1.0, CLIP_NORM / (norm + 1e-06))
-    clipped = owned.reshape(2, shard_len) * factor[:, None]
     moment_step = step_count[0].astype(F32)
-    first_next = BETA_ONE * firsts + (1.0 - BETA_ONE) * clipped
-    second_next = BETA_TWO * seconds + (1.0 - BETA_TWO) * clipped * clipped
-    first_hat = first_next / (1.0 - jnp.power(BETA_ONE, moment_step))
-    second_hat = second_next / (1.0 - jnp.power(BETA_TWO, moment_step))
-    inner = master - LEARN_RATE * (
-        first_hat / (jnp.sqrt(second_hat) + ADAM_EPSILON) + WEIGHT_DECAY * master
-    )
-    drift = master - inner
-    moved = (drift[0] + drift[1]) / groups
-    momentum_next = OUTER_MOMENTUM * outer_momentum + moved
-    final = master - OUTER_RATE * (moved + OUTER_MOMENTUM * momentum_next)
+    scalars = jnp.stack(
+        [
+            factor[0],
+            factor[1],
+            1.0 - jnp.power(BETA_ONE, moment_step),
+            1.0 - jnp.power(BETA_TWO, moment_step),
+        ]
+    )
+
+    def view(value):
+        return value.reshape(own_len, 128)
+
+    results = finish(
+        scalars,
+        dense_owned,
+        other_group(dense_owned),
+        extra[0],
+        extra[1],
+        view(first_moment),
+        view(other_first),
+        view(second_moment),
+        view(other_second),
+        view(master),
+        view(outer_momentum),
+    )
+    clipped, first_next, second_next, moved, momentum_next, final, final_low = results
     return (
-        clipped[:1],
+        clipped.reshape(1, shard_len),
         norm[:1],
         loss_total.reshape(1),
-        first_next[:1],
-        second_next[:1],
-        moved,
-        momentum_next,
-        final,
-        final.astype(BF16),
+        first_next.reshape(1, shard_len),
+        second_next.reshape(1, shard_len),
+        moved.reshape(shard_len),
+        momentum_next.reshape(shard_len),
+        final.reshape(shard_len),
+        final_low.reshape(shard_len),
     )
 
 

time: 299 us -> 247 us (0.83)
  Pallas kernels: 135 us -> 115 us
  other arithmetic: 30.6 us -> 14.4 us
  local copies, waits for them, and re-layouts: 25.1 us -> 14.1 us
    ppermute x4, waiting for transfers between devices: 27.5 us -> 10.8 us  [other_group(): return lax.ppermute(value, 'group', [(0, 1), (1, 0)])]
    pallas_call x1, Pallas kernels: 44.7 us -> 31.7 us  [conv_forward(): pl.pallas_call(forward_body, grid=(envs // 2, 5), in_specs=pixel_specs()...]
    pallas_call x1, Pallas kernels: 36.1 us -> 24.7 us  [upper_backward(): pl.pallas_call(upper_body, grid=(frames // 256,), in_specs=[pl.BlockSpec(...]
    reduce_scatter x1, waiting for transfers between devices: 0.01 us -> 9.16 us  [on_device(): lax.psum_scatter(packed_dense, 'dp', scatter_dimension=0, tiled=False)]
    ppermute x12, waiting for transfers between devices: 30.8 us -> 38 us  [swap(): return lax.ppermute(value, 'dp', [(i, i ^ step) for i in range(lanes)])]
    pallas_call x0 -> x2, Pallas kernels: none -> 6.33 us  [the longest x1 4.34 us: finish(): pl.pallas_call(finish_body, in_specs=[pl.BlockSpec(memory_space=pltpu.SME...]
    dynamic_update_slice x128 -> x0, local copies, waits for them, and re-layouts: 4.99 us -> none  [trajectory_advantages(): lax.scan(backward_step, start, (deltas.T, keeping.T), reverse=True)]
    sub x1 -> x0, other arithmetic: 4.29 us -> none  [on_device(): drift = master - inner]
  transfers between devices with their start and end apart: 22 -> 22, of which waited for: 15 -> 13; matrix products, arithmetic and copies ran while one was open for 9% -> 6% of each run, Pallas kernels for 41% -> 39%
where the time goes in v3:
time: 247 us; the launch traced here: 246 us
  Pallas kernels  115 us (47%)
  waiting for transfers between devices  58 us (23%)
  starting transfers between devices  25.8 us (10%)
  between operations  19.2 us (8%)
  other arithmetic  14.4 us (6%)
  local copies, waits for them, and re-layouts  14.1 us (6%)
    ppermute x12, waiting for transfers between devices, swap(): return lax.ppermute(value, 'dp', [(i, i ^ step) for i in range(lanes)])  38 us
    pallas_call x1, Pallas kernels, lower_backward(): pl.pallas_call(lower_body, grid=(envs // 2, 5), in_specs=pixel_specs() +...  36 us
    pallas_call x1, Pallas kernels, conv_forward(): pl.pallas_call(forward_body, grid=(envs // 2, 5), in_specs=pixel_specs()...  31.7 us
    pallas_call x1, Pallas kernels, upper_backward(): pl.pallas_call(upper_body, grid=(frames // 256,), in_specs=[pl.BlockSpec(...  24.7 us
    pallas_call x1, Pallas kernels, dense_step(): pl.pallas_call(lambda *refs: dense_body(scale, *refs), out_shape=[jax.Sha...  13.5 us
    ppermute x12, starting transfers between devices, swap(): return lax.ppermute(value, 'dp', [(i, i ^ step) for i in range(lanes)])  11 us
    ppermute x4, waiting for transfers between devices, other_group(): return lax.ppermute(value, 'group', [(0, 1), (1, 0)])  10.8 us
    ppermute x4, starting transfers between devices, first_rows_everywhere(): came = lax.ppermute(block, 'dp', pairs)  9.88 us
  transfers between devices with their start and end apart: 22, of which 13 were waited for; matrix products, arithmetic and copies ran while one was open for 6% of the time, Pallas kernels for 39%

profile of v3, /device:TPU:0, one launch (start us, length us, event | category | flops | bytes accessed | tf_op | source)
XLA Modules:
  0.0 246.1 jit_solution(12707302722774181995)
XLA Ops:
  7.2 1.0 convert_element_type.31
  8.3 0.8 convert_element_type.32
  9.3 0.8 select_select_fusion
  10.1 6.0 %collective-permute-start = (bf16[168,512]{1,0:T(8,128)(2,1)S(1)}, bf16[168,512]{1,0:T(8,128)(2,1)S(1)}, u32[]{:S(2)}, u32[]{:S(2)}) collective-permute-start(bf16[168,512]{1,0:T(8,128)(2,1)S(1)} %select_select_fusion), channel_id=1, source_target_pairs={{0,8},{16,24}} | collective-permute-start | bytes 516104 | tf_op jit(solution)/shard_map/ppermute | solution.py:686
  16.0 2.0 advantages.1
  18.0 4.7 %collective-permute-done.1 = f32[8,128]{1,0:T(8,128)S(1)} collective-permute-done((f32[8,128]{1,0:T(8,128)}, f32[8,128]{1,0:T(8,128)S(1)}, u32[]{:S(2)}, u32[]{:S(2)}) %collective-permute-start.1) | collective-permute-done | bytes 4128 | tf_op jit(solution)/shard_map/ppermute | solution.py:643
  23.5 0.8 fusion.11
  24.2 1.3 collective-permute-start.2
  25.6 5.4 %collective-permute-done.3 = f32[8,128]{1,0:T(8,128)S(1)} collective-permute-done((f32[8,128]{1,0:T(8,128)S(1)}, f32[8,128]{1,0:T(8,128)S(1)}, u32[]{:S(2)}, u32[]{:S(2)}) %collective-permute-start.3) | collective-permute-done | bytes 4128 | tf_op jit(solution)/shard_map/ppermute | solution.py:643
  31.1 1.3 collective-permute-start.4
  32.5 3.6 %collective-permute-done.5 = f32[8,128]{1,0:T(8,128)S(1)} collective-permute-done((f32[8,128]{1,0:T(8,128)S(1)}, f32[8,128]{1,0:T(8,128)S(1)}, u32[]{:S(2)}, u32[]{:S(2)}) %collective-permute-start.5) | collective-permute-done | bytes 4128 | tf_op jit(solution)/shard_map/ppermute | solution.py:643
  36.1 1.3 collective-permute-start.6
  37.5 2.0 reduce.1
  39.5 2.2 reduce.2
  41.8 0.8 add.104.conv_ref
  42.5 1.6 collective-permute-start.8
  44.5 2.3 conv_weights.1
  50.0 31.7 %conv_forward.1 = (bf16[20,20,32,512]{3,2,1,0:T(8,128)(2,1)}, bf16[9,10,64,512]{3,2,1,0:T(8,128)(2,1)}, bf16[7,7,64,512]{3,2,1,0:T(8,128)(2,1)}) custom-call(bf16[4,84,336,128]{3,2,1,0:T(8,128)(2,1)} %bitcast.171, bf16[4,84,336,128]{3,2,1,0:T(8,128)(2,1)} %bitcast.172, bf16[4,84,336,128]{3,2,1,0:T(8,128)(2,1)} %bitcast.173, ...), custom_call_target="tpu_custom_call" | custom-call | tf_op jit(solution)/shard_map/conv_forward/pallas_call | solution.py:257
  82.3 0.7 slice.155
  84.0 0.7 copy.78.refs_3_
  85.4 13.5 %dense_step.1 = (f32[16,828,128]{2,1,0:T(8,128)}, bf16[3136,512]{1,0:T(8,128)(2,1)}, f32[32,512]{1,0:T(8,128)}, f32[32,1]{1,0:T(8,128)}, f32[1,1]{1,0:T(1,128)}) custom-call(bf16[3136,512]{1,0:T(8,128)(2,1)} %bitcast.185, bf16[16,207,512]{2,1,0:T(8,128)(2,1)} %all-gather.2.cloned.1.call-done.refs_1_, bf16[32,512]{1,0:T(8,128)(2,1)} %pad.25.refs_2_, ...), custom_call_target="tpu_custom_call" | custom-call | tf_op jit(solution)/shard_map/dense_step/pallas_call | solution.py:385
  99.0 0.8 copy-done.4
  100.3 24.7 %upper_backward.1 = (bf16[11,11,64,512]{3,2,1,0:T(8,128)(2,1)}, f32[672,128]{1,0:T(8,128)}) custom-call(bf16[20,20,32,512]{3,2,1,0:T(8,128)(2,1)} %get-tuple-element.63.a1_hbm.a1_ref, bf16[9,10,64,512]{3,2,1,0:T(8,128)(2,1)} %get-tuple-element.64.a2_ref, bf16[7,7,64,512]{3,2,1,0:T(8,128)(2,1)} %bitcast.186, bf16[192,192]{1,0:T(8,128)(2,1)} %get-tuple-element.72.t3_ref), custom_call_target="tpu_custom_call" | custom-call | tf_op jit(solution)/shard_map/upper_backward/pallas_call | solution.py:532
  125.1 36.0 %lower_backward.1 = f32[672,128]{1,0:T(8,128)} custom-call(bf16[4,84,336,128]{3,2,1,0:T(8,128)(2,1)} %bitcast.176, bf16[4,84,336,128]{3,2,1,0:T(8,128)(2,1)} %bitcast.177, bf16[4,84,336,128]{3,2,1,0:T(8,128)(2,1)} %bitcast.178, bf16[4,84,336,128]{3,2,1,0:T(8,128)(2,1)} %bitcast.179, bf16[4,84,336,128]{3,2,1,0:T(8,128)(2,1)} %bitcast.180, ...), custom_call_target="tpu_custom_call" | custom-call | tf_op jit(solution)/shard_map/lower_backward/pallas_call | solution.py:620
  161.1 1.0 add.109
  162.5 1.4 collective-permute-done.10
  164.0 1.9 collective-permute-start.11
  165.8 3.1 %collective-permute-done.11 = f32[4,48,128]{2,1,0:T(8,128)S(1)} collective-permute-done((f32[4,48,128]{2,1,0:T(8,128)S(1)}, f32[4,48,128]{2,1,0:T(8,128)S(1)}, u32[]{:S(2)}, u32[]{:S(2)}) %collective-permute-start.11) | collective-permute-done | bytes 98336 | tf_op jit(solution)/shard_map/ppermute | solution.py:643
  169.0 2.6 %collective-permute-start.12 = (f32[2,48,128]{2,1,0:T(8,128)S(1)}, f32[2,48,128]{2,1,0:T(8,128)S(1)}, u32[]{:S(2)}, u32[]{:S(2)}) collective-permute-start(f32[2,48,128]{2,1,0:T(8,128)S(1)} %select_bitcast_fusion.10), channel_id=1, source_target_pairs={{0,4},{1,5},{2,6},{3,7},{4,0},{5,1},{6,2},{7,3},{8,12},{9,13},{10,... | collective-permute-start | bytes 147464 | tf_op jit(solution)/shard_map/ppermute | solution.py:643
  171.5 2.5 %collective-permute-done.12 = f32[2,48,128]{2,1,0:T(8,128)S(1)} collective-permute-done((f32[2,48,128]{2,1,0:T(8,128)S(1)}, f32[2,48,128]{2,1,0:T(8,128)S(1)}, u32[]{:S(2)}, u32[]{:S(2)}) %collective-permute-start.12) | collective-permute-done | bytes 49184 | tf_op jit(solution)/shard_map/ppermute | solution.py:643
  174.1 3.5 %collective-permute-start.13 = (f32[1,48,128]{2,1,0:T(8,128)S(1)}, f32[1,48,128]{2,1,0:T(8,128)S(1)}, u32[]{:S(2)}, u32[]{:S(2)}) collective-permute-start(f32[1,48,128]{2,1,0:T(8,128)S(1)} %select_bitcast_fusion.11), channel_id=1, source_target_pairs={{0,8},{1,9},{2,10},{3,11},{4,12},{5,13},{6,14},{7,15},{8,0},{9,1},... | collective-permute-start | bytes 73736 | tf_op jit(solution)/shard_map/ppermute | solution.py:643
  177.6 3.3 %collective-permute-done.13 = f32[1,48,128]{2,1,0:T(8,128)S(1)} collective-permute-done((f32[1,48,128]{2,1,0:T(8,128)S(1)}, f32[1,48,128]{2,1,0:T(8,128)S(1)}, u32[]{:S(2)}, u32[]{:S(2)}) %collective-permute-start.13) | collective-permute-done | bytes 24608 | tf_op jit(solution)/shard_map/ppermute | solution.py:643
  181.5 9.2 %reduce-scatter.2.cloned.1.call-done = f32[1,828,128]{2,1,0:T(8,128)} async-done(((f32[16,828,128]{2,1,0:T(8,128)}), f32[1,828,128]{2,1,0:T(8,128)}) %reduce-scatter.2.cloned.1.call-update) | async-done | bytes 423952 | tf_op jit(solution)/shard_map/reduce_scatter | solution.py:824
  190.7 1.7 multiply_reduce_fusion
  194.5 1.4 collective-permute-start.14
  195.9 2.5 %collective-permute-done.14 = f32[56,128]{1,0:T(8,128)S(1)} collective-permute-done((f32[56,128]{1,0:T(8,128)S(1)}, f32[56,128]{1,0:T(8,128)S(1)}, u32[]{:S(2)}, u32[]{:S(2)}) %collective-permute-start.14) | collective-permute-done | bytes 28704 | tf_op jit(solution)/shard_map/ppermute | solution.py:780
  198.4 1.1 collective-permute-start.15
  199.4 4.7 %collective-permute-done.15 = f32[1,2,56,128]{3,2,1,0:T(8,128)S(1)} collective-permute-done((f32[1,2,56,128]{3,2,1,0:T(8,128)S(1)}, f32[1,2,56,128]{3,2,1,0:T(8,128)S(1)}, u32[]{:S(2)}, u32[]{:S(2)}) %collective-permute-start.15) | collective-permute-done | bytes 57376 | tf_op jit(solution)/shard_map/ppermute | solution.py:643
  204.3 4.7 %collective-permute-done.16 = f32[2,2,56,128]{3,2,1,0:T(8,128)S(1)} collective-permute-done((f32[2,2,56,128]{3,2,1,0:T(8,128)S(1)}, f32[2,2,56,128]{3,2,1,0:T(8,128)S(1)}, u32[]{:S(2)}, u32[]{:S(2)}) %collective-permute-start.16) | collective-permute-done | bytes 114720 | tf_op jit(solution)/shard_map/ppermute | solution.py:643
  209.1 1.5 collective-permute-start.17
  210.5 4.6 %collective-permute-done.17 = f32[4,2,56,128]{3,2,0,1:T(8,128)S(1)} collective-permute-done((f32[4,2,56,128]{3,2,0,1:T(8,128)S(1)}, f32[4,2,56,128]{3,2,0,1:T(8,128)S(1)}, u32[]{:S(2)}, u32[]{:S(2)}) %collective-permute-start.17) | collective-permute-done | bytes 229408 | tf_op jit(solution)/shard_map/ppermute | solution.py:643
  216.0 1.4 collective-permute-start.19
  219.2 1.0 slice_bitcast_fusion
  220.2 8.3 %collective-permute-done.19.other_ref = f32[828,128]{1,0:T(8,128)S(1)} collective-permute-done((f32[828,128]{1,0:T(8,128)}, f32[828,128]{1,0:T(8,128)S(1)}, u32[]{:S(2)}, u32[]{:S(2)}) %collective-permute-start.19) | collective-permute-done | bytes 423968 | tf_op jit(solution)/shard_map/ppermute | solution.py:780
  228.5 0.8 copy-done.2
  229.3 4.3 %finish.1 = (f32[828,128]{1,0:T(8,128)}, f32[828,128]{1,0:T(8,128)}, f32[828,128]{1,0:T(8,128)}, f32[828,128]{1,0:T(8,128)}, f32[828,128]{1,0:T(8,128)}, /*index=5*/f32[828,128]{1,0:T(8,128)}, bf16[828,128]{1,0:T(8,128)(2,1)}) custom-call(f32[4]{0:T(128)} %pad_maximum_fusion.5.scalars_ref, f32[828,128]{1,0:T(8,128)} %bitcast.197, f32[828,128]{1,0:T(8,128)} %copy-done.2, ...), custom_call_target="tpu_custom_call" | custom-call | tf_op jit(solution)/shard_map/finish/pallas_call | solution.py:748
  233.6 2.2 copy.104
  236.3 2.9 %copy_bitcast_fusion = (f32[1,105984]{1,0:T(1,128)}, f32[1,105984]{1,0:T(1,128)}) fusion(f32[1,1,828,128]{3,2,1,0:T(8,128)} %bitcast.205, f32[1,1,828,128]{3,2,1,0:T(8,128)} %bitcast.204), kind=kLoop, calls=%fused_computation.8 | loop fusion | bytes 1695744 | tf_op jit(solution)/shard_map/reshape | solution.py:899
  (97 shorter events, 9.4 us)
Async XLA Ops:
  7.2 75.1 %all-gather.2.cloned.1.call-start = ((), (), s32[]{:S(2)}) async-start(), calls=%async_computation.1 | async-start | bytes 3620864 | tf_op jit(solution)/shard_map/all_gather | solution.py:784
  9.1 181.5 %reduce-scatter.2.cloned.1.call-start = ((), (), s32[]{:S(2)}) async-start(), calls=%async_computation.2 | async-start | bytes 7241728 | tf_op jit(solution)/shard_map/reduce_scatter | solution.py:824
  10.1 13.4 %collective-permute-start = (bf16[168,512]{1,0:T(8,128)(2,1)S(1)}, bf16[168,512]{1,0:T(8,128)(2,1)S(1)}, u32[]{:S(2)}, u32[]{:S(2)}) collective-permute-start(bf16[168,512]{1,0:T(8,128)(2,1)S(1)} %select_select_fusion), channel_id=1, source_target_pairs={{0,8},{16,24}} | collective-permute-start | bytes 516104 | tf_op jit(solution)/shard_map/ppermute | solution.py:686
  18.0 4.7 %collective-permute-start.1 = (f32[8,128]{1,0:T(8,128)}, f32[8,128]{1,0:T(8,128)S(1)}, u32[]{:S(2)}, u32[]{:S(2)}) collective-permute-start(f32[8,128]{1,0:T(8,128)} %get-tuple-element.49), channel_id=1, source_target_pairs={{0,8},{1,9},{2,10},{3,11},{4,12},{5,13},{6,14},{7,15},{8,0},{9,1},... | collective-permute-start | bytes 12296 | tf_op jit(solution)/shard_map/ppermute | solution.py:643
  24.2 6.8 %collective-permute-start.2 = (bf16[168,512]{1,0:T(8,128)(2,1)S(1)}, bf16[168,512]{1,0:T(8,128)(2,1)S(1)}, u32[]{:S(2)}, u32[]{:S(2)}) collective-permute-start(bf16[168,512]{1,0:T(8,128)(2,1)S(1)} %fusion.11), channel_id=1, source_target_pairs={{0,4},{8,12},{16,20},{24,28}} | collective-permute-start | bytes 516104 | tf_op jit(solution)/shard_map/ppermute | solution.py:686
  25.5 5.5 %collective-permute-start.3 = (f32[8,128]{1,0:T(8,128)S(1)}, f32[8,128]{1,0:T(8,128)S(1)}, u32[]{:S(2)}, u32[]{:S(2)}) collective-permute-start(f32[8,128]{1,0:T(8,128)S(1)} %add.99), channel_id=1, source_target_pairs={{0,4},{1,5},{2,6},{3,7},{4,0},{5,1},{6,2},{7,3},{8,12},{9,13},{10,... | collective-permute-start | bytes 12296 | tf_op jit(solution)/shard_map/ppermute | solution.py:643
  31.1 5.0 %collective-permute-start.4 = (bf16[168,512]{1,0:T(8,128)(2,1)S(1)}, bf16[168,512]{1,0:T(8,128)(2,1)S(1)}, u32[]{:S(2)}, u32[]{:S(2)}) collective-permute-start(bf16[168,512]{1,0:T(8,128)(2,1)S(1)} %add.100), channel_id=1, source_target_pairs={{0,2},{4,6},{8,10},{12,14},{16,18},{20,22},{24,26},{28,30}} | collective-permute-start | bytes 516104 | tf_op jit(solution)/shard_map/ppermute | solution.py:686
  32.4 3.7 %collective-permute-start.5 = (f32[8,128]{1,0:T(8,128)S(1)}, f32[8,128]{1,0:T(8,128)S(1)}, u32[]{:S(2)}, u32[]{:S(2)}) collective-permute-start(f32[8,128]{1,0:T(8,128)S(1)} %add.101), channel_id=1, source_target_pairs={{0,2},{1,3},{2,0},{3,1},{4,6},{5,7},{6,4},{7,5},{8,10},{9,11},{10,... | collective-permute-start | bytes 12296 | tf_op jit(solution)/shard_map/ppermute | solution.py:643
  36.1 5.6 %collective-permute-start.6 = (bf16[168,512]{1,0:T(8,128)(2,1)S(1)}, bf16[168,512]{1,0:T(8,128)(2,1)S(1)}, u32[]{:S(2)}, u32[]{:S(2)}) collective-permute-start(bf16[168,512]{1,0:T(8,128)(2,1)S(1)} %add.102), channel_id=1, source_target_pairs={{0,1},{2,3},{4,5},{6,7},{8,9},{10,11},{12,13},{14,15},{16,17},{18,... | collective-permute-start | bytes 516104 | tf_op jit(solution)/shard_map/ppermute | solution.py:686
  37.4 4.3 %collective-permute-start.7 = (f32[8,128]{1,0:T(8,128)S(1)}, f32[8,128]{1,0:T(8,128)S(1)}, u32[]{:S(2)}, u32[]{:S(2)}) collective-permute-start(f32[8,128]{1,0:T(8,128)S(1)} %add.103), channel_id=1, source_target_pairs={{0,1},{1,0},{2,3},{3,2},{4,5},{5,4},{6,7},{7,6},{8,9},{9,8},{10,11... | collective-permute-start | bytes 12296 | tf_op jit(solution)/shard_map/ppermute | solution.py:643
  39.5 42.1 %copy-start = (f32[105984]{0:T(1024)}, f32[105984]{0:T(1024)S(1)}, u32[]{:S(2)}) copy-start(f32[105984]{0:T(1024)S(1)} %reduce.1) | copy-start | bytes 1271812
  41.7 40.0 %copy-start.1 = (f32[105984]{0:T(1024)}, f32[105984]{0:T(1024)S(1)}, u32[]{:S(2)}) copy-start(f32[105984]{0:T(1024)S(1)} %reduce.2) | copy-start | bytes 1271812
  42.5 39.8 %collective-permute-start.8 = (f32[105984]{0:T(1024)S(1)}, f32[105984]{0:T(1024)}, u32[]{:S(2)}, u32[]{:S(2)}) collective-permute-start(f32[105984]{0:T(1024)S(1)} %reduce.1), channel_id=1, source_target_pairs={{0,16},{16,0},{1,17},{17,1},{2,18},{18,2},{3,19},{19,3},{4,20},{20... | collective-permute-start | bytes 1271816 | tf_op jit(solution)/shard_map/ppermute | solution.py:780
  44.1 38.2 %collective-permute-start.9 = (f32[105984]{0:T(1024)S(1)}, f32[105984]{0:T(1024)}, u32[]{:S(2)}, u32[]{:S(2)}) collective-permute-start(f32[105984]{0:T(1024)S(1)} %reduce.2), channel_id=1, source_target_pairs={{0,16},{16,0},{1,17},{17,1},{2,18},{18,2},{3,19},{19,3},{4,20},{20... | collective-permute-start | bytes 1271816 | tf_op jit(solution)/shard_map/ppermute | solution.py:780
  50.0 31.7 %copy-start.6 = (f32[1,4,128]{2,1,0:T(4,128)S(1)}, f32[1,4,128]{2,1,0:T(4,128)}, u32[]{:S(2)}) copy-start(f32[1,4,128]{2,1,0:T(4,128)} %param.16) | copy-start | bytes 6148
  50.0 31.7 %copy-start.7 = (f32[4,128]{1,0:T(4,128)S(1)}, f32[4,128]{1,0:T(4,128)}, u32[]{:S(2)}) copy-start(f32[4,128]{1,0:T(4,128)} %get-tuple-element.69) | copy-start | bytes 6148
  99.0 0.8 copy-start.4
  125.0 36.0 %copy-start.3 = (f32[672,128]{1,0:T(8,128)S(1)}, f32[672,128]{1,0:T(8,128)}, u32[]{:S(2)}) copy-start(f32[672,128]{1,0:T(8,128)} %get-tuple-element.75) | copy-start | bytes 1032196
  125.1 37.0 %copy-start.5 = (f32[32,1]{1,0:T(8,128)S(1)}, f32[32,1]{1,0:T(8,128)}, u32[]{:S(2)}) copy-start(f32[32,1]{1,0:T(8,128)} %get-tuple-element.77) | copy-start | bytes 388
  162.4 1.5 collective-permute-start.10
  164.0 5.0 %collective-permute-start.11 = (f32[4,48,128]{2,1,0:T(8,128)S(1)}, f32[4,48,128]{2,1,0:T(8,128)S(1)}, u32[]{:S(2)}, u32[]{:S(2)}) collective-permute-start(f32[4,48,128]{2,1,0:T(8,128)S(1)} %select_bitcast_fusion.7), channel_id=1, source_target_pairs={{0,2},{1,3},{2,0},{3,1},{4,6},{5,7},{6,4},{7,5},{8,10},{9,11},{10,... | collective-permute-start | bytes 294920 | tf_op jit(solution)/shard_map/ppermute | solution.py:643
  169.0 5.1 %collective-permute-start.12 = (f32[2,48,128]{2,1,0:T(8,128)S(1)}, f32[2,48,128]{2,1,0:T(8,128)S(1)}, u32[]{:S(2)}, u32[]{:S(2)}) collective-permute-start(f32[2,48,128]{2,1,0:T(8,128)S(1)} %select_bitcast_fusion.10), channel_id=1, source_target_pairs={{0,4},{1,5},{2,6},{3,7},{4,0},{5,1},{6,2},{7,3},{8,12},{9,13},{10,... | collective-permute-start | bytes 147464 | tf_op jit(solution)/shard_map/ppermute | solution.py:643
  174.1 6.8 %collective-permute-start.13 = (f32[1,48,128]{2,1,0:T(8,128)S(1)}, f32[1,48,128]{2,1,0:T(8,128)S(1)}, u32[]{:S(2)}, u32[]{:S(2)}) collective-permute-start(f32[1,48,128]{2,1,0:T(8,128)S(1)} %select_bitcast_fusion.11), channel_id=1, source_target_pairs={{0,8},{1,9},{2,10},{3,11},{4,12},{5,13},{6,14},{7,15},{8,0},{9,1},... | collective-permute-start | bytes 73736 | tf_op jit(solution)/shard_map/ppermute | solution.py:643
  194.5 3.9 %collective-permute-start.14 = (f32[56,128]{1,0:T(8,128)S(1)}, f32[56,128]{1,0:T(8,128)S(1)}, u32[]{:S(2)}, u32[]{:S(2)}) collective-permute-start(f32[56,128]{1,0:T(8,128)S(1)} %get-tuple-element.102), channel_id=1, source_target_pairs={{0,16},{16,0},{1,17},{17,1},{2,18},{18,2},{3,19},{19,3},{4,20},{20... | collective-permute-start | bytes 86024 | tf_op jit(solution)/shard_map/ppermute | solution.py:780
  198.4 5.7 %collective-permute-start.15 = (f32[1,2,56,128]{3,2,1,0:T(8,128)S(1)}, f32[1,2,56,128]{3,2,1,0:T(8,128)S(1)}, u32[]{:S(2)}, u32[]{:S(2)}) collective-permute-start(f32[1,2,56,128]{3,2,1,0:T(8,128)S(1)} %maximum_bitcast_fusion.1), channel_id=1, source_target_pairs={{0,8},{1,9},{2,10},{3,11},{4,12},{5,13},{6,14},{7,15},{8,0},{9,1},... | collective-permute-start | bytes 172040 | tf_op jit(solution)/shard_map/ppermute | solution.py:643
  204.1 4.9 %collective-permute-start.16 = (f32[2,2,56,128]{3,2,1,0:T(8,128)S(1)}, f32[2,2,56,128]{3,2,1,0:T(8,128)S(1)}, u32[]{:S(2)}, u32[]{:S(2)}) collective-permute-start(f32[2,2,56,128]{3,2,1,0:T(8,128)S(1)} %maximum_bitcast_fusion), channel_id=1, source_target_pairs={{0,4},{1,5},{2,6},{3,7},{4,0},{5,1},{6,2},{7,3},{8,12},{9,13},{10,... | collective-permute-start | bytes 344072 | tf_op jit(solution)/shard_map/ppermute | solution.py:643
  209.1 6.1 %collective-permute-start.17 = (f32[4,2,56,128]{3,2,0,1:T(8,128)S(1)}, f32[4,2,56,128]{3,2,0,1:T(8,128)S(1)}, u32[]{:S(2)}, u32[]{:S(2)}) collective-permute-start(f32[4,2,56,128]{3,2,0,1:T(8,128)S(1)} %bitcast.198), channel_id=1, source_target_pairs={{0,2},{1,3},{2,0},{3,1},{4,6},{5,7},{6,4},{7,5},{8,10},{9,11},{10,... | collective-permute-start | bytes 688136 | tf_op jit(solution)/shard_map/ppermute | solution.py:643
  215.2 2.3 collective-permute-start.18
  216.0 12.5 %collective-permute-start.19 = (f32[828,128]{1,0:T(8,128)}, f32[828,128]{1,0:T(8,128)S(1)}, u32[]{:S(2)}, u32[]{:S(2)}) collective-permute-start(f32[828,128]{1,0:T(8,128)} %bitcast.196), channel_id=1, source_target_pairs={{0,16},{16,0},{1,17},{17,1},{2,18},{18,2},{3,19},{19,3},{4,20},{20... | collective-permute-start | bytes 1271816 | tf_op jit(solution)/shard_map/ppermute | solution.py:780
  228.5 0.8 copy-start.2
Sparse Core Ops, SparseCore 0:
  10.8 49.4 all-gather.1
  99.1 91.5 reduce-scatter.1

commit v4 on v3

--- a/solution.py
+++ b/solution.py
@@ -195,49 +195,84 @@
 
 
 def forward_body(
-    x0, x1, x2, x3, x4, t1_ref, b1_ref, t2_ref, b2_ref, t3_ref, b3_ref, a1_ref, a2_ref, a3_ref
+    x_hbm,
+    t1_ref,
+    b1_ref,
+    t2_ref,
+    b2_ref,
+    t3_ref,
+    b3_ref,
+    a1_hbm,
+    a2_ref,
+    a3_ref,
+    x_ref,
+    a1_ref,
+    x_sems,
+    sem,
 ):
-    x_refs = (x0, x1, x2, x3, x4)
-    t = pl.program_id(1)
+    pair = pl.program_id(0)
+    lanes = pl.ds(pl.multiple_of(256 * pair, 256), 256)
+
+    def load(j, c):
+        part = pl.ds(12 * c, 12)
+        return pltpu.make_async_copy(
+            x_hbm.at[pl.ds(2 * j, 2), part], x_ref.at[j, :, part], x_sems.at[7 * j + c]
+        )
+
+    @pl.when(pair == 0)
+    def _():
+        for j in range(x_ref.shape[0]):
+            for c in range(7):
+                load(j, c).start()
 
     def low(value, bias_ref):
         return jnp.maximum(value + bias_ref[...], 0.0).astype(BF16)
 
-    for h in range(2):
+    ready = 0
+    for m in range(10):
+        while m % 2 == 0 and 12 * ready < 8 * m + 20:
+            load(pair, ready).wait()
+            ready += 1
         held = None
         for n in range(21):
-            got = mm(t1_ref[...], pixel_window(x_refs, 2 * h, 16 * n, 16))
+            window = jnp.concatenate(
+                [
+                    x_ref[pair, e, 8 * m : 8 * m + 12, 16 * n : 16 * n + 16, :].reshape(192, 128)
+                    for e in range(2)
+                ],
+                axis=1,
+            )
+            got = mm(t1_ref[...], window)
             if n > 0:
                 out = low(held + got[64:128], b1_ref)
-                a1_ref[pl.ds(4 * t + 2 * h, 2), n - 1] = out.reshape(2, C1, 256)
+                a1_ref[2 * m : 2 * m + 2, n - 1] = out.reshape(2, C1, 256)
             held = got[0:64]
-
-    @pl.when(t == 4)
-    def _():
-        def conv_two(p, carry):
-            held = None
-            for n in range(10):
-                window = a1_ref[pl.ds(2 * p, 4), 2 * n : 2 * n + 2].reshape(256, 256)
-                got = mm(t2_ref[...], window)
-                if n > 0:
-                    a2_ref[p, n - 1] = low(held + got[64:128], b2_ref)
-                held = got[0:64]
-            a2_ref[p, 9] = jnp.zeros((C2, 256), BF16)
-            return carry
-
-        lax.fori_loop(0, 9, conv_two, 0, unroll=3)
-
-        def conv_three(p, carry):
-            held, older = None, None
-            for x in range(9):
-                got = mm(t3_ref[...], a2_ref[pl.ds(p, 3), x].reshape(192, 256))
-                if x > 1:
-                    a3_ref[p, x - 2] = low(older + got[128:192], b3_ref)
-                older = held + got[64:128] if x > 0 else None
-                held = got[0:64]
-            return carry
-
-        lax.fori_loop(0, 7, conv_three, 0, unroll=7)
+        if m % 2 == 1:
+            here = pl.ds(2 * m - 2, 4)
+            pltpu.make_async_copy(a1_ref.at[here], a1_hbm.at[here, :, :, lanes], sem.at[0]).start()
+
+    def conv_two(p, carry):
+        held = None
+        for n in range(10):
+            window = a1_ref[pl.ds(2 * p, 4), 2 * n : 2 * n + 2].reshape(256, 256)
+            got = mm(t2_ref[...], window)
+            if n > 0:
+                a2_ref[p, n - 1] = low(held + got[64:128], b2_ref)
+            held = got[0:64]
+        a2_ref[p, 9] = jnp.zeros((C2, 256), BF16)
+        return carry
+
+    lax.fori_loop(0, 9, conv_two, 0, unroll=3)
+
+    for p in range(7):
+        held, older = None, None
+        for x in range(9):
+            got = mm(t3_ref[...], a2_ref[p : p + 3, x].reshape(192, 256))
+            if x > 1:
+                a3_ref[p, x - 2] = low(older + got[128:192], b3_ref)
+            older = held + got[64:128] if x > 0 else None
+            held = got[0:64]
+    pltpu.make_async_copy(a1_ref, a1_hbm.at[:, :, :, lanes], sem.at[0]).wait()
 
 
 def whole(shape):
@@ -256,9 +291,9 @@
     frames = envs * 128
     return pl.pallas_call(
         forward_body,
-        grid=(envs // 2, 5),
-        in_specs=pixel_specs()
-        + [
+        grid=(envs // 2,),
+        in_specs=[
+            pl.BlockSpec(memory_space=pl.ANY),
             whole((128, 192)),
             whole((64, 256)),
             whole((128, 256)),
@@ -267,56 +302,83 @@
             whole((64, 256)),
         ],
         out_specs=[
-            pl.BlockSpec((20, 20, C1, 256), lambda j, t: (0, 0, 0, j)),
-            pl.BlockSpec((9, 10, C2, 256), lambda j, t: (0, 0, 0, j)),
-            pl.BlockSpec((7, 7, C3, 256), lambda j, t: (0, 0, 0, j)),
+            pl.BlockSpec(memory_space=pl.ANY),
+            pl.BlockSpec((9, 10, C2, 256), lambda j: (0, 0, 0, j)),
+            pl.BlockSpec((7, 7, C3, 256), lambda j: (0, 0, 0, j)),
         ],
         out_shape=[
             jax.ShapeDtypeStruct((20, 20, C1, frames), BF16),
             jax.ShapeDtypeStruct((9, 10, C2, frames), BF16),
             jax.ShapeDtypeStruct((7, 7, C3, frames), BF16),
         ],
+        scratch_shapes=[
+            pltpu.VMEM((envs // 2, 2, 84, 336, 128), BF16),
+            pltpu.VMEM((20, 20, C1, 256), BF16),
+            pltpu.SemaphoreType.DMA((7 * envs // 2,)),
+            pltpu.SemaphoreType.DMA((1,)),
+        ],
         compiler_params=pltpu.CompilerParams(vmem_limit_bytes=VMEM_LIMIT),
         name="conv_forward",
-    )(x, x, x, x, x, t1, b1, t2, b2, t3, b3)
+    )(x, t1, b1, t2, b2, t3, b3)
 
 
 def dense_body(
     scale,
-    a3_ref,
-    gathered_ref,
-    wh_ref,
-    bh_ref,
-    normed_ref,
-    returns_ref,
+    a3_hbm,
+    gathered_hbm,
+    head_ref,
+    sums_ref,
+    advantage_ref,
+    values_ref,
     actions_ref,
     behavior_ref,
-    packed_ref,
-    dc3_ref,
+    packed_hbm,
+    wd_hbm,
+    d_hidden_ref,
     gwh_ref,
     gbh_ref,
     loss_ref,
     wide_ref,
+    a3_ref,
+    gathered_ref,
     wd_ref,
+    packed_ref,
+    sems,
 ):
+    shards, rows, _ = gathered_ref.shape
+    halves = [slice(0, shards // 2), slice(shards // 2, shards)]
+    loads = []
+    for h, part in enumerate(halves):
+        loads.append(
+            pltpu.make_async_copy(gathered_hbm.at[part], gathered_ref.at[part], sems.at[h])
+        )
+        loads[h].start()
+    load_a3 = pltpu.make_async_copy(a3_hbm, a3_ref, sems.at[2])
+    load_a3.start()
     late = lax.broadcasted_iota(jnp.int32, (1, HID), 1) >= PHASE
-    shards, rows, _ = gathered_ref.shape
-    for k in range(shards):
-        if rows * k <= TOP + 1 + FEATURES and rows * (k + 1) > TOP:
-            wide_ref[rows * k : rows * k + rows] = gathered_ref[k].astype(F32)
+    for h, part in enumerate(halves):
+        loads[h].wait()
+        for k in range(part.start, part.stop):
+            if rows * k <= TOP + 1 + FEATURES and rows * (k + 1) > TOP:
+                wide_ref[rows * k : rows * k + rows] = gathered_ref[k].astype(F32)
     for i in range(0, FEATURES, 448):
         wd_ref[i : i + 448] = jnp.where(
             late, wide_ref[TOP + i : TOP + i + 448], wide_ref[TOP + 1 + i : TOP + 449 + i]
         ).astype(BF16)
+    store_wd = pltpu.make_async_copy(wd_ref, wd_hbm, sems.at[3])
+    store_wd.start()
     bias = jnp.where(
         late,
         wide_ref[TOP + FEATURES : TOP + 1 + FEATURES],
         wide_ref[TOP + 1 + FEATURES : TOP + 2 + FEATURES],
     )
     bias = jnp.broadcast_to(bias, (8, HID)).T[:, 0:1]
+    load_a3.wait()
     hidden_pre = mm_tn(wd_ref[...], a3_ref[...]) + bias
     hidden = jnp.maximum(hidden_pre, 0.0).astype(BF16)
-    out = mm(wh_ref[...], hidden) + bh_ref[...]
+    head = head_ref[...].astype(F32).T
+    weights = pltpu.roll(head[0:32, 0:HID], PHASE, 1).astype(BF16)
+    out = mm(weights, hidden) + head[0:32, HID : HID + 1]
     row = lax.broadcasted_iota(jnp.int32, out.shape, 0)
     is_logit = row < ACTIONS
     logits = jnp.where(is_logit, out, -jnp.inf)
@@ -327,17 +389,26 @@
     log_probs = jnp.where(is_logit, shifted - jnp.log(total), 0.0)
     probs = jnp.where(is_logit, jnp.exp(log_probs), 0.0)
     value = jnp.sum(jnp.where(row == ACTIONS, out, 0.0), axis=0, keepdims=True)
-    normed = normed_ref[...]
-    chosen = row == actions_ref[...]
+
+    def flat(array):
+        return jnp.concatenate([array[e : e + 1] for e in range(array.shape[0])], axis=1)
+
+    advantage = flat(advantage_ref[...])
+    sums = sums_ref[...]
+    mean = sums[0:1, 0:1] * scale
+    spread = sums[1:2, 0:1] * scale - mean * mean
+    normed = (advantage - mean) * lax.rsqrt(spread + 1e-05)
+    returns = advantage + flat(values_ref[...])
+    chosen = row == flat(actions_ref[...])
     taken = jnp.sum(jnp.where(chosen, log_probs, 0.0), axis=0, keepdims=True)
-    ratio = jnp.exp(taken - behavior_ref[...])
+    ratio = jnp.exp(taken - flat(behavior_ref[...]))
     low = 1.0 - RATIO_CLIP
     high = 1.0 + RATIO_CLIP
     clipped = jnp.clip(ratio, low, high)
     plain = ratio * normed
     cut = clipped * normed
     entropy = -jnp.sum(probs * log_probs, axis=0, keepdims=True)
-    error = value - returns_ref[...]
+    error = value - returns
     losses = -jnp.minimum(plain, cut) + 0.5 * VALUE_COEF * error * error - ENTROPY_COEF * entropy
     loss_ref[...] = jnp.sum(losses, axis=1, keepdims=True) * scale
     plain_share = jnp.where(plain < cut, 1.0, jnp.where(plain == cut, 0.5, 0.0))
@@ -352,52 +423,68 @@
     d_out = jnp.where(is_logit, d_logits, jnp.where(row == ACTIONS, d_value, 0.0)).astype(BF16)
     gwh_ref[...] = mm_nt(d_out, hidden)
     gbh_ref[...] = jnp.sum(d_out.astype(F32), axis=1, keepdims=True)
-    back = mm_tn(wh_ref[...], d_out)
-    d_hidden = jnp.where(hidden_pre > 0, back, 0.0).astype(BF16)
+    back = mm_tn(weights, d_out)
+    d_hidden = jnp.where(hidden > 0, back, 0.0).astype(BF16)
+    d_hidden_ref[...] = d_hidden
     last = LEAD + FEATURES
     wide_ref[0:LEAD] = jnp.zeros((LEAD, HID), F32)
-    wide_ref[LEAD:last] = mm_nt(a3_ref[...], d_hidden)
     wide_ref[last:] = jnp.zeros((wide_ref.shape[0] - last, HID), F32)
     ones = jnp.ones((8, d_hidden.shape[1]), BF16)
     wide_ref[last : last + 1] = mm_nt(ones, d_hidden)[0:1]
-    for k in range(shards):
-        first = rows * k + LEAD - TOP - 1
-        for j in range(4):
-            cols = slice(128 * j, 128 * j + 128)
-            early_part = wide_ref[first : first + rows, cols]
-            if 128 * j + 128 <= PHASE:
-                part = early_part
-            elif 128 * j >= PHASE:
-                part = wide_ref[first + 1 : first + 1 + rows, cols]
-            else:
-                part = jnp.where(
-                    late[:, cols], wide_ref[first + 1 : first + 1 + rows, cols], early_part
-                )
-            packed_ref[k, pl.ds(j, rows, stride=4), :] = part
-    d_a3 = mm(wd_ref[...], d_hidden)
-    dc3_ref[...] = jnp.where(a3_ref[...] > 0, d_a3, 0.0).astype(BF16)
-
-
-def dense_step(scale, a3, gathered, wh, bh, normed, returns, actions, behavior):
+    done = 0
+    for i in range(0, FEATURES, 448):
+        wide_ref[LEAD + i : LEAD + i + 448] = mm_nt(a3_ref[i : i + 448], d_hidden)
+        for k in range(done, shards):
+            first = rows * k + LEAD - TOP - 1
+            if first + rows >= LEAD + i + 448 and i + 448 < FEATURES:
+                break
+            done = k + 1
+            for j in range(4):
+                cols = slice(128 * j, 128 * j + 128)
+                early_part = wide_ref[first : first + rows, cols]
+                if 128 * j + 128 <= PHASE:
+                    part = early_part
+                elif 128 * j >= PHASE:
+                    part = wide_ref[first + 1 : first + 1 + rows, cols]
+                else:
+                    part = jnp.where(
+                        late[:, cols], wide_ref[first + 1 : first + 1 + rows, cols], early_part
+                    )
+                packed_ref[k, pl.ds(j, rows, stride=4), :] = part
+            pltpu.make_async_copy(packed_ref.at[k], packed_hbm.at[k], sems.at[4]).start()
+    store_wd.wait()
+    pltpu.make_async_copy(packed_ref, packed_hbm, sems.at[4]).wait()
+
+
+def dense_step(scale, a3, gathered, head, sums, advantage, values, actions, behavior):
     frames = a3.shape[1]
     shards, shard_rows, _ = gathered.shape
-    rows = wh.shape[0]
+    rows = 32
+    here = pl.BlockSpec(memory_space=pltpu.VMEM)
+    away = pl.BlockSpec(memory_space=pl.ANY)
     return pl.pallas_call(
         lambda *refs: dense_body(scale, *refs),
+        in_specs=[away, away] + [here] * 6,
+        out_specs=[away, away] + [here] * 4,
         out_shape=[
             jax.ShapeDtypeStruct((shards, 4 * shard_rows, 128), F32),
-            jax.ShapeDtypeStruct((FEATURES, frames), BF16),
+            jax.ShapeDtypeStruct((FEATURES, HID), BF16),
+            jax.ShapeDtypeStruct((HID, frames), BF16),
             jax.ShapeDtypeStruct((rows, HID), F32),
             jax.ShapeDtypeStruct((rows, 1), F32),
             jax.ShapeDtypeStruct((1, 1), F32),
         ],
         scratch_shapes=[
             pltpu.VMEM((max(shards * shard_rows, TOP + 1 + FEATURES) + 2 * LEAD - TOP, HID), F32),
+            pltpu.VMEM(a3.shape, BF16),
+            pltpu.VMEM(gathered.shape, BF16),
             pltpu.VMEM((FEATURES, HID), BF16),
+            pltpu.VMEM((shards, 4 * shard_rows, 128), F32),
+            pltpu.SemaphoreType.DMA((5,)),
         ],
         compiler_params=pltpu.CompilerParams(vmem_limit_bytes=VMEM_LIMIT),
         name="dense_step",
-    )(a3, gathered, wh, bh, normed, returns, actions, behavior)
+    )(a3, gathered, head, sums, advantage, values, actions, behavior)
 
 
 def fold(g_ref, width, rows):
@@ -417,7 +504,9 @@
 def upper_body(
     a1_hbm,
     a2_ref,
-    dc3_ref,
+    a3_ref,
+    wd_ref,
+    d_hidden_ref,
     t3_ref,
     d2_ref,
     packed_ref,
@@ -453,13 +542,14 @@
 
     lax.fori_loop(1, 10, edge, 0)
 
-    def fill(p, carry):
-        d3_ref[p + 2, 0:7] = dc3_ref[p]
+    sums = jnp.zeros((C3, 256), F32)
+    for p in range(7):
+        back = mm(wd_ref[448 * p : 448 * p + 448], d_hidden_ref[...]).reshape(7, C3, 256)
+        masked = jnp.where(a3_ref[p] > 0, back, 0.0).astype(BF16)
+        d3_ref[p + 2, 0:7] = masked
         d3_ref[p + 2, 7] = jnp.zeros((C3, 256), BF16)
-        s3_ref[...] += jnp.sum(dc3_ref[p].astype(F32), axis=0)
-        return carry
-
-    lax.fori_loop(0, 7, fill, 0)
+        sums = sums + jnp.sum(masked.astype(F32), axis=0)
+    s3_ref[...] += sums
 
     left = [a2_ref[p : p + 3, 4 * g : 4 * g + 6].reshape(1152, 256) for p in range(7) for g in range(2)]
     right = [d3_ref[p + 2, 4 * g : 4 * g + 4].reshape(256, 256) for p in range(7) for g in range(2)]
@@ -527,7 +617,7 @@
                     packed_ref[below, :] += jnp.where(lane < phase, turned, 0.0)[:, cols]
 
 
-def upper_backward(a1, a2, dc3, t3):
+def upper_backward(a1, a2, a3, w_dense, d_hidden, t3):
     frames = a1.shape[3]
     return pl.pallas_call(
         upper_body,
@@ -536,6 +626,8 @@
             pl.BlockSpec(memory_space=pl.ANY),
             pl.BlockSpec((9, 10, C2, 256), lambda j: (0, 0, 0, j)),
             pl.BlockSpec((7, 7, C3, 256), lambda j: (0, 0, 0, j)),
+            whole((FEATURES, HID)),
+            pl.BlockSpec((HID, 256), lambda j: (0, j)),
             whole((192, 192)),
         ],
         out_specs=[
@@ -559,7 +651,7 @@
         ],
         compiler_params=pltpu.CompilerParams(vmem_limit_bytes=VMEM_LIMIT),
         name="upper_backward",
-    )(a1, a2, dc3, t3)
+    )(a1, a2, a3, w_dense, d_hidden, t3)
 
 
 def lower_body(
@@ -663,15 +755,17 @@
     return blocks[0]
 
 
-def gather_blocks(block, lanes, place):
+def gather_blocks(block, beside, lanes, place):
     blocks = block[None]
     for step in reversed(halving_order(lanes)):
+        if step == 1:
+            blocks, beside = lax.optimization_barrier((blocks, beside))
         other = swap(blocks, lanes, step)
         high = (place // step) % 2 == 1
         blocks = jnp.stack(
             [jnp.where(high, other, blocks), jnp.where(high, blocks, other)], axis=1
         ).reshape((2 * blocks.shape[0],) + blocks.shape[1:])
-    return blocks
+    return blocks, beside
 
 
 def first_rows_everywhere(local, sums, lanes, place):
@@ -692,12 +786,34 @@
     return jnp.pad(block, ((0, BLOCK_ROWS - TOP - 1), (0, 0))), sum_everywhere(sums, lanes)
 
 
+def facts_body(dense_ref, piece_ref, loss_ref, message_ref):
+    dense = dense_ref[...]
+    piece = piece_ref[...]
+    squares = jnp.sum(dense * dense, axis=0, keepdims=True)
+    squares = squares + jnp.sum(piece * piece, axis=0, keepdims=True)
+    squares = jnp.sum(squares, axis=1, keepdims=True)
+    height = piece.shape[0]
+    message_ref[0:height] = piece
+    row = lax.broadcasted_iota(jnp.int32, (8, 128), 0)
+    message_ref[height : height + 8] = jnp.where(row == 0, squares, loss_ref[...])
+
+
+def facts_message(dense, piece, loss):
+    return pl.pallas_call(
+        facts_body,
+        out_shape=jax.ShapeDtypeStruct((piece.shape[0] + 8, 128), F32),
+        name="facts_message",
+    )(dense, piece, loss)
+
+
 def finish_body(
+    parts,
+    own_len,
+    place_ref,
     scalars_ref,
+    messages_ref,
     mine_ref,
     other_ref,
-    mine_extra_ref,
-    other_extra_ref,
     first_ref,
     other_first_ref,
     second_ref,
@@ -711,29 +827,63 @@
     momentum_out,
     final_ref,
     low_ref,
+    norm_ref,
+    loss_ref,
+    extra_ref,
 ):
+    height = messages_ref.shape[2] - 8
+    place = place_ref[0]
+    first_step = pl.program_id(0) == 0
+
+    @pl.when(first_step)
+    def _():
+        extra_ref[...] = jnp.zeros(extra_ref.shape, F32)
+
+    for start, stop, target in parts:
+        for owner in range(target // own_len, (target + stop - start - 1) // own_len + 1):
+            shift = target - start - owner * own_len
+            low = max(start, -shift)
+            high = min(stop, own_len - shift)
+
+            @pl.when(first_step & (place == owner))
+            def _(shift=shift, low=low, high=high):
+                for k in range(low // height, (high - 1) // height + 1):
+                    a = max(low, k * height)
+                    b = min(high, (k + 1) * height)
+                    for g in range(2):
+                        extra_ref[g, a + shift : b + shift] = messages_ref[
+                            k, g, a - k * height : b - k * height
+                        ]
+
+    block = master_ref.shape[0]
+    here = pl.ds(pl.multiple_of(block * pl.program_id(0), 8), block)
+
+    factors = []
+    for g in range(2):
+        facts = jnp.sum(messages_ref[:, g, height : height + 8, :], axis=0)
+        norm = jnp.sqrt(facts[0:1, 0:1])
+        factors.append(jnp.minimum(1.0, CLIP_NORM / (norm + 1e-06)))
+        if g == 0:
+            norm_ref[...] = norm
+            loss_ref[...] = facts[1:2, 0:1]
     master = master_ref[...]
 
-    def inner_step(factor, dense_ref, extra_ref, one_ref, two_ref):
-        clipped = (dense_ref[...] + extra_ref[...]) * factor
+    def inner_step(g, dense_ref, one_ref, two_ref):
+        clipped = (dense_ref[...] + extra_ref[g, here]) * factors[g]
         first_next = BETA_ONE * one_ref[...] + (1.0 - BETA_ONE) * clipped
         second_next = BETA_TWO * two_ref[...] + (1.0 - BETA_TWO) * clipped * clipped
-        first_hat = first_next / scalars_ref[2]
-        second_hat = second_next / scalars_ref[3]
+        first_hat = first_next / scalars_ref[0]
+        second_hat = second_next / scalars_ref[1]
         inner = master - LEARN_RATE * (
             first_hat / (jnp.sqrt(second_hat) + ADAM_EPSILON) + WEIGHT_DECAY * master
         )
         return clipped, first_next, second_next, master - inner
 
-    clipped, first_next, second_next, drift = inner_step(
-        scalars_ref[0], mine_ref, mine_extra_ref, first_ref, second_ref
-    )
-    clipped_ref[...] = clipped
-    first_out[...] = first_next
-    second_out[...] = second_next
-    _, _, _, other_drift = inner_step(
-        scalars_ref[1], other_ref, other_extra_ref, other_first_ref, other_second_ref
-    )
+    clipped, first_next, second_next, drift = inner_step(0, mine_ref, first_ref, second_ref)
+    clipped_ref[:, 0, :] = clipped
+    first_out[:, 0, :] = first_next
+    second_out[:, 0, :] = second_next
+    _, _, _, other_drift = inner_step(1, other_ref, other_first_ref, other_second_ref)
     moved = (drift + other_drift) / 2.0
     moved_ref[...] = moved
     momentum_next = OUTER_MOMENTUM * momentum_ref[...] + moved
@@ -743,15 +893,29 @@
     low_ref[...] = final.astype(BF16)
 
 
-def finish(scalars, *arrays):
-    shape = arrays[0].shape
+def finish(parts, place, scalars, messages, *arrays):
+    own_len = arrays[0].shape[0]
+    block = min(208, -(-own_len // 8) * 8)
+    steps = -(-own_len // block)
+    scalar = pl.BlockSpec(memory_space=pltpu.SMEM)
+
+    def spec(array):
+        if len(array.shape) == 3:
+            return pl.BlockSpec((block, 1, 128), lambda k: (k, 0, 0))
+        return pl.BlockSpec((block, 128), lambda k: (k, 0))
+
+    outs = [jax.ShapeDtypeStruct((own_len, 1, 128), F32)] * 3
+    outs += [jax.ShapeDtypeStruct((own_len, 128), F32)] * 3
+    outs += [jax.ShapeDtypeStruct((own_len, 128), BF16)]
     return pl.pallas_call(
-        finish_body,
-        in_specs=[pl.BlockSpec(memory_space=pltpu.SMEM)]
-        + [pl.BlockSpec(memory_space=pltpu.VMEM)] * len(arrays),
-        out_shape=[jax.ShapeDtypeStruct(shape, F32)] * 6 + [jax.ShapeDtypeStruct(shape, BF16)],
+        lambda *refs: finish_body(parts, own_len, *refs),
+        grid=(steps,),
+        in_specs=[scalar, scalar, whole(messages.shape)] + [spec(array) for array in arrays],
+        out_specs=[spec(array) for array in outs] + [whole((1, 1))] * 2,
+        out_shape=outs + [jax.ShapeDtypeStruct((1, 1), F32)] * 2,
+        scratch_shapes=[pltpu.VMEM((2, block * steps, 128), F32)],
         name="finish",
-    )(scalars, *arrays)
+    )(place, scalars, messages, *arrays)
 
 
 def on_device(
@@ -790,39 +954,35 @@
     batch = envs_here * steps_here
     total_frames = batch * lanes
     block, sums = first_rows_everywhere(low_rows, sums, lanes, place)
-    mean = sums[0, 0] / total_frames
-    spread = sums[1, 0] / total_frames - mean * mean
-    normed = ((advantage - mean) * lax.rsqrt(spread + 1e-05)).reshape(1, batch)
-    returns = (advantage + old_values[0]).reshape(1, batch)
-
     x = frames[0].transpose(0, 2, 3, 1)
     t1, b1, t2, b2, t3, b3, back3, back2 = conv_weights(block)
     a1, a2, a3 = conv_forward(x, t1, b1, t2, b2, t3, b3)
-    _, first_sent, second_sent = lax.optimization_barrier((block, first_moment[0], second_moment[0]))
-    a3, other_first, other_second = lax.optimization_barrier(
-        (a3, other_group(first_sent), other_group(second_sent))
-    )
-
     tail = TOP + FEATURES + 1
     head_owner = tail // rows
     head_flat = gathered[head_owner:].reshape((lanes - head_owner) * rows, HID)
     head_flat = head_flat[tail - head_owner * rows :].reshape(-1)[PHASE : PHASE + HEAD_LEN]
-    w_head = head_flat[: HID * (ACTIONS + 1)].reshape(HID, ACTIONS + 1)
-    w_head = jnp.pad(jnp.roll(w_head, PHASE, axis=0).T, ((0, 13), (0, 0)))
-    b_head = jnp.pad(head_flat[HID * (ACTIONS + 1) :], (0, 13)).astype(F32)
-    packed_dense, d_c3, g_head, g_head_bias, loss_local = dense_step(
+    head = jnp.pad(head_flat.reshape(HID + 1, ACTIONS + 1), ((0, 7), (0, 127 - ACTIONS)))
+    packed_dense, w_dense, d_hidden, g_head, g_head_bias, loss_local = dense_step(
         1.0 / total_frames,
         a3.reshape(FEATURES, batch),
         gathered,
-        w_head,
-        b_head[:, None],
-        normed,
-        returns,
-        actions[0].reshape(1, batch),
-        behavior_logprob[0].reshape(1, batch),
+        head,
+        sums,
+        advantage,
+        old_values[0],
+        actions[0],
+        behavior_logprob[0],
     )
     dense_owned = lax.psum_scatter(packed_dense, "dp", scatter_dimension=0, tiled=False)
-    d2, upper = upper_backward(a1, a2, d_c3.reshape(7, 7, C3, batch), back3)
+    d_hidden, first_sent, second_sent = lax.optimization_barrier(
+        (d_hidden, first_moment, second_moment)
+    )
+    d2, upper = upper_backward(a1, a2, a3, w_dense, d_hidden, back3)
+    first_flat = first_sent.reshape(shard_len)
+    second_flat = second_sent.reshape(shard_len)
+    d2, other_first, other_second = lax.optimization_barrier(
+        (d2, other_group(first_flat), other_group(second_flat))
+    )
     lower = lower_backward(x, a1, d2, back2)
 
     tail_rows = lanes * rows - tail
@@ -839,62 +999,40 @@
     head_part = jnp.pad(head_part, ((0, count - real), (0, 0)))
     small = jnp.concatenate([lower + upper, head_part], axis=0)
     piece = scatter_sum(small.reshape(lanes, count // lanes, 128), lanes, place)
-    squares = jnp.sum(dense_owned * dense_owned) + jnp.sum(piece * piece)
-    row = lax.broadcasted_iota(jnp.int32, (8, 128), 0)
-    message = jnp.concatenate([piece, jnp.where(row == 0, squares, loss_local)], axis=0)
-    messages = gather_blocks(jnp.stack([message, other_group(message)]), lanes, place)
-    facts = jnp.sum(messages[:, :, -8:-6, 0], axis=0)
-    norm = jnp.sqrt(facts[:, 0])
-    loss_total = facts[0, 1]
-    smalls = messages[:, :, :-8].transpose(1, 0, 2, 3).reshape(2, count, 128)
+    message = facts_message(dense_owned, piece, loss_local)
+    messages, dense_other = gather_blocks(
+        jnp.stack([message, other_group(message)]), other_group(dense_owned), lanes, place
+    )
 
     own_len = 4 * rows
-
-    def own_rows(part, first_row):
-        first = first_row // own_len
-        blocks = -(-(first_row + part.shape[1]) // own_len) - first
-        before = first_row - first * own_len
-        part = jnp.pad(
-            part, ((0, 0), (before, blocks * own_len - before - part.shape[1]), (0, 0))
-        )
-        here = (place >= first) & (place < first + blocks)
-        start = jnp.clip(place - first, 0, blocks - 1) * own_len
-        return jnp.where(here, lax.dynamic_slice_in_dim(part, start, own_len, 1), 0.0)
-
-    extra = own_rows(smalls[:, : 4 * (TOP + 1)], 0)
-    extra = extra + own_rows(smalls[:, 4 * BLOCK_ROWS : real], 4 * tail)
-    factor = jnp.minimum(1.0, CLIP_NORM / (norm + 1e-06))
     moment_step = step_count[0].astype(F32)
     scalars = jnp.stack(
-        [
-            factor[0],
-            factor[1],
-            1.0 - jnp.power(BETA_ONE, moment_step),
-            1.0 - jnp.power(BETA_TWO, moment_step),
-        ]
-    )
+        [1.0 - jnp.power(BETA_ONE, moment_step), 1.0 - jnp.power(BETA_TWO, moment_step)]
+    )
+    parts = ((0, 4 * (TOP + 1), 0), (4 * BLOCK_ROWS, real, 4 * tail))
 
     def view(value):
         return value.reshape(own_len, 128)
 
     results = finish(
+        parts,
+        place.reshape(1),
         scalars,
+        messages,
         dense_owned,
-        other_group(dense_owned),
-        extra[0],
-        extra[1],
-        view(first_moment),
+        dense_other,
+        view(first_flat),
         view(other_first),
-        view(second_moment),
+        view(second_flat),
         view(other_second),
         view(master),
         view(outer_momentum),
     )
-    clipped, first_next, second_next, moved, momentum_next, final, final_low = results
+    clipped, first_next, second_next, moved, momentum_next, final, final_low, norm, loss = results
     return (
         clipped.reshape(1, shard_len),
-        norm[:1],
-        loss_total.reshape(1),
+        norm.reshape(1),
+        loss.reshape(1),
         first_next.reshape(1, shard_len),
         second_next.reshape(1, shard_len),
         moved.reshape(shard_len),

time: 247 us -> 216 us (0.87)
  local copies, waits for them, and re-layouts: 14.1 us -> 4.51 us
  waiting for transfers between devices: 58 us -> 48.5 us
  Pallas kernels: 115 us -> 110 us
  between operations: 19.2 us -> 15.3 us
  other arithmetic: 14.4 us -> 10.9 us
    reduce_scatter x1, waiting for transfers between devices: 9.16 us -> 0.67 us  [on_device(): lax.psum_scatter(packed_dense, 'dp', scatter_dimension=0, tiled=False)]
    pallas_call x3 -> x4, Pallas kernels: 49.6 us -> 42.2 us  [the longest x1 23.1 us: conv_forward(): pl.pallas_call(forward_body, grid=(envs // 2,), in_specs=[pl.BlockSpec(me...]
    unnamed x2 -> x0, other arithmetic: 4.18 us -> none
    ppermute x4, waiting for transfers between devices: 10.8 us -> 6.65 us  [other_group(): return lax.ppermute(value, 'group', [(0, 1), (1, 0)])]
    unnamed x17 -> x16, local copies, waits for them, and re-layouts: 3.79 us -> 0.04 us
    ppermute x12, waiting for transfers between devices: 38 us -> 41.1 us  [swap(): return lax.ppermute(value, 'dp', [(i, i ^ step) for i in range(lanes)])]
    reshape x1, local copies, waits for them, and re-layouts: 2.9 us -> 0.25 us  [on_device(): head_flat.reshape(HID + 1, ACTIONS + 1)]
    slice x13 -> x0, local copies, waits for them, and re-layouts: 2.59 us -> none  [the longest x6 0.8 us: on_device(): w_head = jnp.pad(jnp.roll(w_head, PHASE, axis=0).T, ((0, 13), (0, 0)))]
  transfers between devices with their start and end apart: 22 -> 22, of which waited for: 13 -> 15; matrix products, arithmetic and copies ran while one was open for 6% -> 4% of each run, Pallas kernels for 39% -> 42%
where the time goes in v4:
time: 216 us; the launch traced here: 215 us
  Pallas kernels  110 us (51%)
  waiting for transfers between devices  48.5 us (22%)
  starting transfers between devices  25.9 us (12%)
  between operations  15.3 us (7%)
  other arithmetic  10.9 us (5%)
  local copies, waits for them, and re-layouts  4.51 us (2%)
    ppermute x12, waiting for transfers between devices, swap(): return lax.ppermute(value, 'dp', [(i, i ^ step) for i in range(lanes)])  41.1 us
    pallas_call x1, Pallas kernels, lower_backward(): pl.pallas_call(lower_body, grid=(envs // 2, 5), in_specs=pixel_specs() +...  36.7 us
    pallas_call x1, Pallas kernels, upper_backward(): pl.pallas_call(upper_body, grid=(frames // 256,), in_specs=[pl.BlockSpec(...  27 us
    pallas_call x1, Pallas kernels, conv_forward(): pl.pallas_call(forward_body, grid=(envs // 2,), in_specs=[pl.BlockSpec(me...  23.1 us
    pallas_call x1, Pallas kernels, dense_step(): pl.pallas_call(lambda *refs: dense_body(scale, *refs), in_specs=[away, aw...  10.9 us
    ppermute x12, starting transfers between devices, swap(): return lax.ppermute(value, 'dp', [(i, i ^ step) for i in range(lanes)])  10.8 us
    ppermute x4, starting transfers between devices, first_rows_everywhere(): came = lax.ppermute(block, 'dp', pairs)  9.88 us
    ppermute x4, waiting for transfers between devices, other_group(): return lax.ppermute(value, 'group', [(0, 1), (1, 0)])  6.65 us
  transfers between devices with their start and end apart: 22, of which 15 were waited for; matrix products, arithmetic and copies ran while one was open for 4% of the time, Pallas kernels for 42%

profile of v4, /device:TPU:0, one launch (start us, length us, event | category | flops | bytes accessed | tf_op | source)
XLA Modules:
  0.0 215.2 jit_solution(7777037699581084734)
XLA Ops:
  7.2 1.0 convert_element_type.25
  8.3 0.8 convert_element_type.26
  9.3 0.8 select_select_fusion
  10.1 6.0 %collective-permute-start = (bf16[168,512]{1,0:T(8,128)(2,1)S(1)}, bf16[168,512]{1,0:T(8,128)(2,1)S(1)}, u32[]{:S(2)}, u32[]{:S(2)}) collective-permute-start(bf16[168,512]{1,0:T(8,128)(2,1)S(1)} %select_select_fusion), channel_id=1, source_target_pairs={{0,8},{16,24}} | collective-permute-start | bytes 516104 | tf_op jit(solution)/shard_map/ppermute | solution.py:780
  16.1 2.0 advantages.1
  18.0 4.7 %collective-permute-done.1 = f32[8,128]{1,0:T(8,128)S(1)} collective-permute-done((f32[8,128]{1,0:T(8,128)}, f32[8,128]{1,0:T(8,128)S(1)}, u32[]{:S(2)}, u32[]{:S(2)}) %collective-permute-start.1) | collective-permute-done | bytes 4128 | tf_op jit(solution)/shard_map/ppermute | solution.py:735
  22.8 0.7 add.71
  23.5 0.8 fusion.4
  24.2 1.3 collective-permute-start.2
  25.6 5.4 %collective-permute-done.3 = f32[8,128]{1,0:T(8,128)S(1)} collective-permute-done((f32[8,128]{1,0:T(8,128)S(1)}, f32[8,128]{1,0:T(8,128)S(1)}, u32[]{:S(2)}, u32[]{:S(2)}) %collective-permute-start.3) | collective-permute-done | bytes 4128 | tf_op jit(solution)/shard_map/ppermute | solution.py:735
  31.1 1.3 collective-permute-start.4
  32.5 3.6 %collective-permute-done.5 = f32[8,128]{1,0:T(8,128)S(1)} collective-permute-done((f32[8,128]{1,0:T(8,128)S(1)}, f32[8,128]{1,0:T(8,128)S(1)}, u32[]{:S(2)}, u32[]{:S(2)}) %collective-permute-start.5) | collective-permute-done | bytes 4128 | tf_op jit(solution)/shard_map/ppermute | solution.py:735
  36.1 1.3 collective-permute-start.6
  37.5 1.2 collective-permute-done.7
  39.3 0.7 add.76.conv_ref
  40.0 2.3 %conv_weights.1 = (bf16[128,192]{1,0:T(8,128)(2,1)}, f32[64,256]{1,0:T(8,128)}, bf16[128,256]{1,0:T(8,128)(2,1)}, f32[64,256]{1,0:T(8,128)}, bf16[192,192]{1,0:T...) custom-call(bf16[168,512]{1,0:T(8,128)(2,1)} %add.76.conv_ref), custom_call_target="tpu_custom_call" | custom-call | tf_op jit(solution)/shard_map/conv_weights/pallas_call | solution.py:175
  42.2 23.1 %conv_forward.1 = (bf16[20,20,32,512]{3,2,1,0:T(8,128)(2,1)}, bf16[9,10,64,512]{3,2,1,0:T(8,128)(2,1)}, bf16[7,7,64,512]{3,2,1,0:T(8,128)(2,1)}) custom-call(bf16[4,84,336,128]{3,2,1,0:T(8,128)(2,1)} %bitcast.131, bf16[128,192]{1,0:T(8,128)(2,1)} %get-tuple-element.63.t1_ref, f32[64,256]{1,0:T(8,128)} %get-tuple-element.64.b1_ref, ...), custom_call_target="tpu_custom_call" | custom-call | tf_op jit(solution)/shard_map/conv_forward/pallas_call | solution.py:292
  65.4 0.7 slice.76
  67.2 10.9 %dense_step.1 = (f32[16,828,128]{2,1,0:T(8,128)}, bf16[3136,512]{1,0:T(8,128)(2,1)}, bf16[512,512]{1,0:T(8,128)(2,1)}, f32[32,512]{1,0:T(8,128)}, f32[32,1]{1,0:T(8,128)}, /*index=5*/f32[1,1]{1,0:T(1,128)}) custom-call(bf16[3136,512]{1,0:T(8,128)(2,1)} %bitcast.137, bf16[16,207,512]{2,1,0:T(8,128)(2,1)} %all-gather.2.cloned.1.call-done.refs_1_, ...), custom_call_target="tpu_custom_call" | custom-call | tf_op jit(solution)/shard_map/dense_step/pallas_call | solution.py:465
  78.1 1.0 reduce
  79.2 1.4 collective-permute-start.8
  80.5 1.0 reduce.1
  81.6 0.8 collective-permute-start.9
  83.1 27.0 %upper_backward.1 = (bf16[11,11,64,512]{3,2,1,0:T(8,128)(2,1)}, f32[672,128]{1,0:T(8,128)}) custom-call(bf16[20,20,32,512]{3,2,1,0:T(8,128)(2,1)} %get-tuple-element.73.a1_hbm.a1_ref, bf16[9,10,64,512]{3,2,1,0:T(8,128)(2,1)} %get-tuple-element.74.a2_ref, bf16[7,7,64,512]{3,2,1,0:T(8,128)(2,1)} %get-tuple-element.69.a3_ref, ...), custom_call_target="tpu_custom_call" | custom-call | tf_op jit(solution)/shard_map/upper_backward/pallas_call | solution.py:622
  110.2 36.7 %lower_backward.1 = f32[672,128]{1,0:T(8,128)} custom-call(bf16[4,84,336,128]{3,2,1,0:T(8,128)(2,1)} %bitcast.132, bf16[4,84,336,128]{3,2,1,0:T(8,128)(2,1)} %bitcast.133, bf16[4,84,336,128]{3,2,1,0:T(8,128)(2,1)} %bitcast.134, bf16[4,84,336,128]{3,2,1,0:T(8,128)(2,1)} %bitcast.135, bf16[4,84,336,128]{3,2,1,0:T(8,128)(2,1)} %bitcast.136, ...), custom_call_target="tpu_custom_call" | custom-call | tf_op jit(solution)/shard_map/lower_backward/pallas_call | solution.py:712
  146.9 1.0 add.78
  148.1 1.4 collective-permute-done.10
  149.6 1.9 collective-permute-start.11
  151.4 5.1 %collective-permute-done.11 = f32[4,48,128]{2,1,0:T(8,128)S(1)} collective-permute-done((f32[4,48,128]{2,1,0:T(8,128)S(1)}, f32[4,48,128]{2,1,0:T(8,128)S(1)}, u32[]{:S(2)}, u32[]{:S(2)}) %collective-permute-start.11) | collective-permute-done | bytes 98336 | tf_op jit(solution)/shard_map/ppermute | solution.py:735
  156.6 2.7 %collective-permute-start.12 = (f32[2,48,128]{2,1,0:T(8,128)S(1)}, f32[2,48,128]{2,1,0:T(8,128)S(1)}, u32[]{:S(2)}, u32[]{:S(2)}) collective-permute-start(f32[2,48,128]{2,1,0:T(8,128)S(1)} %select_bitcast_fusion.10), channel_id=1, source_target_pairs={{0,4},{1,5},{2,6},{3,7},{4,0},{5,1},{6,2},{7,3},{8,12},{9,13},{10,... | collective-permute-start | bytes 147464 | tf_op jit(solution)/shard_map/ppermute | solution.py:735
  159.3 4.1 %collective-permute-done.12 = f32[2,48,128]{2,1,0:T(8,128)S(1)} collective-permute-done((f32[2,48,128]{2,1,0:T(8,128)S(1)}, f32[2,48,128]{2,1,0:T(8,128)S(1)}, u32[]{:S(2)}, u32[]{:S(2)}) %collective-permute-start.12) | collective-permute-done | bytes 49184 | tf_op jit(solution)/shard_map/ppermute | solution.py:735
  163.4 1.3 collective-permute-start.13
  164.7 5.1 %collective-permute-done.13 = f32[1,48,128]{2,1,0:T(8,128)S(1)} collective-permute-done((f32[1,48,128]{2,1,0:T(8,128)S(1)}, f32[1,48,128]{2,1,0:T(8,128)S(1)}, u32[]{:S(2)}, u32[]{:S(2)}) %collective-permute-start.13) | collective-permute-done | bytes 24608 | tf_op jit(solution)/shard_map/ppermute | solution.py:735
  171.1 2.5 %facts_message.1 = f32[56,128]{1,0:T(8,128)} custom-call(f32[828,128]{1,0:T(8,128)} %bitcast.146, f32[48,128]{1,0:T(8,128)} %fusion.3.piece_ref, f32[1,1]{1,0:T(1,128)} %get-tuple-element.87.loss_ref), custom_call_target="tpu_custom_call" | custom-call | tf_op jit(solution)/shard_map/facts_message/pallas_call | solution.py:802
  173.5 1.6 collective-permute-start.14
  175.1 2.5 %collective-permute-done.14 = f32[56,128]{1,0:T(8,128)S(1)} collective-permute-done((f32[56,128]{1,0:T(8,128)}, f32[56,128]{1,0:T(8,128)S(1)}, u32[]{:S(2)}, u32[]{:S(2)}) %collective-permute-start.14) | collective-permute-done | bytes 28704 | tf_op jit(solution)/shard_map/ppermute | solution.py:944
  177.6 0.8 maximum_bitcast_fusion.1
  178.4 1.4 collective-permute-start.15
  179.8 3.7 %collective-permute-done.15 = f32[1,2,56,128]{3,2,1,0:T(8,128)S(1)} collective-permute-done((f32[1,2,56,128]{3,2,1,0:T(8,128)S(1)}, f32[1,2,56,128]{3,2,1,0:T(8,128)S(1)}, u32[]{:S(2)}, u32[]{:S(2)}) %collective-permute-start.15) | collective-permute-done | bytes 57376 | tf_op jit(solution)/shard_map/ppermute | solution.py:735
  183.5 0.8 select_bitcast_fusion.9
  184.3 1.2 collective-permute-start.16
  185.5 3.6 %collective-permute-done.16 = f32[2,2,56,128]{3,2,1,0:T(8,128)S(1)} collective-permute-done((f32[2,2,56,128]{3,2,1,0:T(8,128)S(1)}, f32[2,2,56,128]{3,2,1,0:T(8,128)S(1)}, u32[]{:S(2)}, u32[]{:S(2)}) %collective-permute-start.16) | collective-permute-done | bytes 114720 | tf_op jit(solution)/shard_map/ppermute | solution.py:735
  189.2 2.0 collective-permute-start.17
  191.2 1.3 collective-permute-start.18
  192.6 2.7 %collective-permute-done.17 = f32[4,2,56,128]{3,2,1,0:T(8,128)S(1)} collective-permute-done((f32[4,2,56,128]{3,2,1,0:T(8,128)S(1)}, f32[4,2,56,128]{3,2,1,0:T(8,128)S(1)}, u32[]{:S(2)}, u32[]{:S(2)}) %collective-permute-start.17) | collective-permute-done | bytes 229408 | tf_op jit(solution)/shard_map/ppermute | solution.py:735
  195.4 4.2 %collective-permute-done.18.refs_4_ = f32[828,128]{1,0:T(8,128)S(1)} collective-permute-done((f32[828,128]{1,0:T(8,128)}, f32[828,128]{1,0:T(8,128)S(1)}, u32[]{:S(2)}, u32[]{:S(2)}) %collective-permute-start.18) | collective-permute-done | bytes 423968 | tf_op jit(solution)/shard_map/ppermute | solution.py:944
  201.5 1.0 copy.64
  202.5 5.8 %finish.1 = (f32[828,1,128]{2,1,0:T(1,128)}, f32[828,1,128]{2,1,0:T(1,128)}, f32[828,1,128]{2,1,0:T(1,128)}, f32[828,128]{1,0:T(8,128)}, f32[828,128]{1,0:T(8,12...) custom-call(s32[1]{0:T(128)} %bitcast.refs_0_, ...), custom_call_target="tpu_custom_call" | custom-call | tf_op jit(solution)/shard_map/finish/pallas_call | solution.py:910
  (75 shorter events, 5.9 us)
Async XLA Ops:
  7.2 58.2 %all-gather.2.cloned.1.call-start = ((), (), s32[]{:S(2)}) async-start(), calls=%async_computation.1 | async-start | bytes 3620864 | tf_op jit(solution)/shard_map/all_gather | solution.py:948
  9.1 162.0 %reduce-scatter.2.cloned.1.call-start = ((), (), s32[]{:S(2)}) async-start(), calls=%async_computation.2 | async-start | bytes 7241728 | tf_op jit(solution)/shard_map/reduce_scatter | solution.py:976
  10.1 13.4 %collective-permute-start = (bf16[168,512]{1,0:T(8,128)(2,1)S(1)}, bf16[168,512]{1,0:T(8,128)(2,1)S(1)}, u32[]{:S(2)}, u32[]{:S(2)}) collective-permute-start(bf16[168,512]{1,0:T(8,128)(2,1)S(1)} %select_select_fusion), channel_id=1, source_target_pairs={{0,8},{16,24}} | collective-permute-start | bytes 516104 | tf_op jit(solution)/shard_map/ppermute | solution.py:780
  18.0 4.7 %collective-permute-start.1 = (f32[8,128]{1,0:T(8,128)}, f32[8,128]{1,0:T(8,128)S(1)}, u32[]{:S(2)}, u32[]{:S(2)}) collective-permute-start(f32[8,128]{1,0:T(8,128)} %get-tuple-element.55), channel_id=1, source_target_pairs={{0,8},{1,9},{2,10},{3,11},{4,12},{5,13},{6,14},{7,15},{8,0},{9,1},... | collective-permute-start | bytes 12296 | tf_op jit(solution)/shard_map/ppermute | solution.py:735
  24.2 6.8 %collective-permute-start.2 = (bf16[168,512]{1,0:T(8,128)(2,1)S(1)}, bf16[168,512]{1,0:T(8,128)(2,1)S(1)}, u32[]{:S(2)}, u32[]{:S(2)}) collective-permute-start(bf16[168,512]{1,0:T(8,128)(2,1)S(1)} %fusion.4), channel_id=1, source_target_pairs={{0,4},{8,12},{16,20},{24,28}} | collective-permute-start | bytes 516104 | tf_op jit(solution)/shard_map/ppermute | solution.py:780
  25.5 5.5 %collective-permute-start.3 = (f32[8,128]{1,0:T(8,128)S(1)}, f32[8,128]{1,0:T(8,128)S(1)}, u32[]{:S(2)}, u32[]{:S(2)}) collective-permute-start(f32[8,128]{1,0:T(8,128)S(1)} %add.71), channel_id=1, source_target_pairs={{0,4},{1,5},{2,6},{3,7},{4,0},{5,1},{6,2},{7,3},{8,12},{9,13},{10,... | collective-permute-start | bytes 12296 | tf_op jit(solution)/shard_map/ppermute | solution.py:735
  31.1 5.0 %collective-permute-start.4 = (bf16[168,512]{1,0:T(8,128)(2,1)S(1)}, bf16[168,512]{1,0:T(8,128)(2,1)S(1)}, u32[]{:S(2)}, u32[]{:S(2)}) collective-permute-start(bf16[168,512]{1,0:T(8,128)(2,1)S(1)} %add.72), channel_id=1, source_target_pairs={{0,2},{4,6},{8,10},{12,14},{16,18},{20,22},{24,26},{28,30}} | collective-permute-start | bytes 516104 | tf_op jit(solution)/shard_map/ppermute | solution.py:780
  32.4 3.7 %collective-permute-start.5 = (f32[8,128]{1,0:T(8,128)S(1)}, f32[8,128]{1,0:T(8,128)S(1)}, u32[]{:S(2)}, u32[]{:S(2)}) collective-permute-start(f32[8,128]{1,0:T(8,128)S(1)} %add.73), channel_id=1, source_target_pairs={{0,2},{1,3},{2,0},{3,1},{4,6},{5,7},{6,4},{7,5},{8,10},{9,11},{10,... | collective-permute-start | bytes 12296 | tf_op jit(solution)/shard_map/ppermute | solution.py:735
  36.1 3.1 %collective-permute-start.6 = (bf16[168,512]{1,0:T(8,128)(2,1)S(1)}, bf16[168,512]{1,0:T(8,128)(2,1)S(1)}, u32[]{:S(2)}, u32[]{:S(2)}) collective-permute-start(bf16[168,512]{1,0:T(8,128)(2,1)S(1)} %add.74), channel_id=1, source_target_pairs={{0,1},{2,3},{4,5},{6,7},{8,9},{10,11},{12,13},{14,15},{16,17},{18,... | collective-permute-start | bytes 516104 | tf_op jit(solution)/shard_map/ppermute | solution.py:780
  37.4 1.2 collective-permute-start.7
  67.2 11.0 %copy-start.3 = (f32[1,105984]{1,0:T(1,128)S(1)}, f32[1,105984]{1,0:T(1,128)}, u32[]{:S(2)}) copy-start(f32[1,105984]{1,0:T(1,128)} %param.22) | copy-start | bytes 1271812
  78.1 2.5 %copy-start.4 = (f32[1,105984]{1,0:T(1,128)S(1)}, f32[1,105984]{1,0:T(1,128)}, u32[]{:S(2)}) copy-start(f32[1,105984]{1,0:T(1,128)} %param.23) | copy-start | bytes 1271812
  78.1 4.3 %copy-start.6 = (f32[32,512]{1,0:T(8,128)S(1)}, f32[32,512]{1,0:T(8,128)}, u32[]{:S(2)}) copy-start(f32[32,512]{1,0:T(8,128)} %get-tuple-element.85) | copy-start | bytes 196612
  78.1 4.8 %copy-start.7 = (f32[32,1]{1,0:T(8,128)S(1)}, f32[32,1]{1,0:T(8,128)}, u32[]{:S(2)}) copy-start(f32[32,1]{1,0:T(8,128)} %get-tuple-element.86) | copy-start | bytes 388
  79.2 31.0 %copy-start = (f32[105984]{0:T(1024)}, f32[105984]{0:T(1024)S(1)}, u32[]{:S(2)}) copy-start(f32[105984]{0:T(1024)S(1)} %reduce) | copy-start | bytes 1271812
  79.2 31.0 %collective-permute-start.8 = (f32[105984]{0:T(1024)S(1)}, f32[105984]{0:T(1024)}, u32[]{:S(2)}, u32[]{:S(2)}) collective-permute-start(f32[105984]{0:T(1024)S(1)} %reduce), channel_id=1, source_target_pairs={{0,16},{16,0},{1,17},{17,1},{2,18},{18,2},{3,19},{19,3},{4,20},{20... | collective-permute-start | bytes 1271816 | tf_op jit(solution)/shard_map/ppermute | solution.py:944
  81.6 28.6 %copy-start.1 = (f32[105984]{0:T(1024)}, f32[105984]{0:T(1024)S(1)}, u32[]{:S(2)}) copy-start(f32[105984]{0:T(1024)S(1)} %reduce.1) | copy-start | bytes 1271812
  81.6 28.6 %collective-permute-start.9 = (f32[105984]{0:T(1024)S(1)}, f32[105984]{0:T(1024)}, u32[]{:S(2)}, u32[]{:S(2)}) collective-permute-start(f32[105984]{0:T(1024)S(1)} %reduce.1), channel_id=1, source_target_pairs={{0,16},{16,0},{1,17},{17,1},{2,18},{18,2},{3,19},{19,3},{4,20},{20... | collective-permute-start | bytes 1271816 | tf_op jit(solution)/shard_map/ppermute | solution.py:944
  110.2 36.7 %copy-start.5 = (f32[672,128]{1,0:T(8,128)S(1)}, f32[672,128]{1,0:T(8,128)}, u32[]{:S(2)}) copy-start(f32[672,128]{1,0:T(8,128)} %get-tuple-element.84) | copy-start | bytes 1032196
  148.0 1.5 collective-permute-start.10
  149.6 7.0 %collective-permute-start.11 = (f32[4,48,128]{2,1,0:T(8,128)S(1)}, f32[4,48,128]{2,1,0:T(8,128)S(1)}, u32[]{:S(2)}, u32[]{:S(2)}) collective-permute-start(f32[4,48,128]{2,1,0:T(8,128)S(1)} %select_bitcast_fusion.7), channel_id=1, source_target_pairs={{0,2},{1,3},{2,0},{3,1},{4,6},{5,7},{6,4},{7,5},{8,10},{9,11},{10,... | collective-permute-start | bytes 294920 | tf_op jit(solution)/shard_map/ppermute | solution.py:735
  156.6 6.8 %collective-permute-start.12 = (f32[2,48,128]{2,1,0:T(8,128)S(1)}, f32[2,48,128]{2,1,0:T(8,128)S(1)}, u32[]{:S(2)}, u32[]{:S(2)}) collective-permute-start(f32[2,48,128]{2,1,0:T(8,128)S(1)} %select_bitcast_fusion.10), channel_id=1, source_target_pairs={{0,4},{1,5},{2,6},{3,7},{4,0},{5,1},{6,2},{7,3},{8,12},{9,13},{10,... | collective-permute-start | bytes 147464 | tf_op jit(solution)/shard_map/ppermute | solution.py:735
  163.4 6.4 %collective-permute-start.13 = (f32[1,48,128]{2,1,0:T(8,128)S(1)}, f32[1,48,128]{2,1,0:T(8,128)S(1)}, u32[]{:S(2)}, u32[]{:S(2)}) collective-permute-start(f32[1,48,128]{2,1,0:T(8,128)S(1)} %select_bitcast_fusion.11), channel_id=1, source_target_pairs={{0,8},{1,9},{2,10},{3,11},{4,12},{5,13},{6,14},{7,15},{8,0},{9,1},... | collective-permute-start | bytes 73736 | tf_op jit(solution)/shard_map/ppermute | solution.py:735
  173.5 4.1 %collective-permute-start.14 = (f32[56,128]{1,0:T(8,128)}, f32[56,128]{1,0:T(8,128)S(1)}, u32[]{:S(2)}, u32[]{:S(2)}) collective-permute-start(f32[56,128]{1,0:T(8,128)} %facts_message.1), channel_id=1, source_target_pairs={{0,16},{16,0},{1,17},{17,1},{2,18},{18,2},{3,19},{19,3},{4,20},{20... | collective-permute-start | bytes 86024 | tf_op jit(solution)/shard_map/ppermute | solution.py:944
  178.4 5.1 %collective-permute-start.15 = (f32[1,2,56,128]{3,2,1,0:T(8,128)S(1)}, f32[1,2,56,128]{3,2,1,0:T(8,128)S(1)}, u32[]{:S(2)}, u32[]{:S(2)}) collective-permute-start(f32[1,2,56,128]{3,2,1,0:T(8,128)S(1)} %maximum_bitcast_fusion.1), channel_id=1, source_target_pairs={{0,8},{1,9},{2,10},{3,11},{4,12},{5,13},{6,14},{7,15},{8,0},{9,1},... | collective-permute-start | bytes 172040 | tf_op jit(solution)/shard_map/ppermute | solution.py:735
  184.3 4.9 %collective-permute-start.16 = (f32[2,2,56,128]{3,2,1,0:T(8,128)S(1)}, f32[2,2,56,128]{3,2,1,0:T(8,128)S(1)}, u32[]{:S(2)}, u32[]{:S(2)}) collective-permute-start(f32[2,2,56,128]{3,2,1,0:T(8,128)S(1)} %maximum_bitcast_fusion), channel_id=1, source_target_pairs={{0,4},{1,5},{2,6},{3,7},{4,0},{5,1},{6,2},{7,3},{8,12},{9,13},{10,... | collective-permute-start | bytes 344072 | tf_op jit(solution)/shard_map/ppermute | solution.py:735
  189.2 6.1 %collective-permute-start.17 = (f32[4,2,56,128]{3,2,1,0:T(8,128)S(1)}, f32[4,2,56,128]{3,2,1,0:T(8,128)S(1)}, u32[]{:S(2)}, u32[]{:S(2)}) collective-permute-start(f32[4,2,56,128]{3,2,1,0:T(8,128)S(1)} %bitcast.151), channel_id=1, source_target_pairs={{0,2},{1,3},{2,0},{3,1},{4,6},{5,7},{6,4},{7,5},{8,10},{9,11},{10,... | collective-permute-start | bytes 688136 | tf_op jit(solution)/shard_map/ppermute | solution.py:735
  191.2 8.3 %collective-permute-start.18 = (f32[828,128]{1,0:T(8,128)}, f32[828,128]{1,0:T(8,128)S(1)}, u32[]{:S(2)}, u32[]{:S(2)}) collective-permute-start(f32[828,128]{1,0:T(8,128)} %bitcast.147), channel_id=1, source_target_pairs={{0,16},{16,0},{1,17},{17,1},{2,18},{18,2},{3,19},{19,3},{4,20},{20... | collective-permute-start | bytes 1271816 | tf_op jit(solution)/shard_map/ppermute | solution.py:944
  199.6 3.0 %copy-start.2 = (f32[828,128]{1,0:T(8,128)}, f32[828,128]{1,0:T(8,128)S(1)}, u32[]{:S(2)}) copy-start(f32[828,128]{1,0:T(8,128)S(1)} %collective-permute-done.18.refs_4_) | copy-start | bytes 1271812
  199.6 1.8 collective-permute-start.19
Sparse Core Ops, SparseCore 0:
  10.8 49.4 all-gather.1
  78.2 92.7 reduce-scatter.1

commit v5 on v4

--- a/solution.py
+++ b/solution.py
@@ -512,8 +512,6 @@
     packed_ref,
     r2_ref,
     r3_ref,
-    s2_ref,
-    s3_ref,
     a1_ref,
     d3_ref,
     g2_ref,
@@ -527,7 +525,7 @@
 
     @pl.when(step == 0)
     def _():
-        for ref in (r2_ref, r3_ref, s2_ref, s3_ref):
+        for ref in (r2_ref, r3_ref):
             ref[...] = jnp.zeros(ref.shape, F32)
         for p in (0, 1, 9, 10):
             d3_ref[p] = jnp.zeros((8, C3, 256), BF16)
@@ -542,21 +540,19 @@
 
     lax.fori_loop(1, 10, edge, 0)
 
-    sums = jnp.zeros((C3, 256), F32)
+    zero = jnp.zeros((), BF16)
     for p in range(7):
         back = mm(wd_ref[448 * p : 448 * p + 448], d_hidden_ref[...]).reshape(7, C3, 256)
-        masked = jnp.where(a3_ref[p] > 0, back, 0.0).astype(BF16)
-        d3_ref[p + 2, 0:7] = masked
+        d3_ref[p + 2, 0:7] = jnp.where(a3_ref[p] > 0, back.astype(BF16), zero)
         d3_ref[p + 2, 7] = jnp.zeros((C3, 256), BF16)
-        sums = sums + jnp.sum(masked.astype(F32), axis=0)
-    s3_ref[...] += sums
 
     left = [a2_ref[p : p + 3, 4 * g : 4 * g + 6].reshape(1152, 256) for p in range(7) for g in range(2)]
     right = [d3_ref[p + 2, 4 * g : 4 * g + 4].reshape(256, 256) for p in range(7) for g in range(2)]
-    r3_ref[...] += mm_nt(jnp.concatenate(left, axis=1), jnp.concatenate(right, axis=1))
+    left = jnp.concatenate(left, axis=1)
+    left = jnp.concatenate([left, jnp.ones((16, left.shape[1]), BF16)], axis=0)
+    r3_ref[...] += mm_nt(left, jnp.concatenate(right, axis=1))
 
     def three_input(y, carry):
-        total = jnp.zeros((C2, 256), F32)
         parts = []
         for x in range(9):
             if x < 7:
@@ -565,10 +561,7 @@
             for j in range(3):
                 if 0 <= x - j < 7:
                     back = back + parts[x - j][64 * j : 64 * j + 64]
-            masked = jnp.where(a2_ref[y, x] > 0, back, 0.0).astype(BF16)
-            d2_ref[y + 1, x + 1] = masked
-            total = total + masked.astype(F32)
-        s2_ref[...] += total
+            d2_ref[y + 1, x + 1] = jnp.where(a2_ref[y, x] > 0, back.astype(BF16), zero)
         return carry
 
     lax.fori_loop(0, 9, three_input, 0, unroll=3)
@@ -581,7 +574,9 @@
             for g in range(3):
                 left.append(a1_ref[pl.ds(2 * p, 4), 6 * g : 6 * g + 8].reshape(1024, 256))
                 right.append(d2_ref[p + 1, 1 + 3 * g : 4 + 3 * g].reshape(192, 256))
-        r2_ref[:, 0:192] += mm_nt(jnp.concatenate(left, axis=1), jnp.concatenate(right, axis=1))
+        left = jnp.concatenate(left, axis=1)
+        left = jnp.concatenate([left, jnp.ones((16, left.shape[1]), BF16)], axis=0)
+        r2_ref[:, 0:192] += mm_nt(left, jnp.concatenate(right, axis=1))
         return carry
 
     lax.fori_loop(0, 3, two_weights, 0)
@@ -602,8 +597,12 @@
             total = total + r3_ref[k + 128 : k + 320, 128:256]
             total = total + pltpu.roll(r3_ref[k + 192 : k + 384, 128:256], 64, 1)
             g3_ref[192 * i : 192 * i + 192] = total
-        g2_ref[512:513, 0:64] = jnp.sum(s2_ref[...].T, axis=0, keepdims=True)
-        g3_ref[576:577, 0:64] = jnp.sum(s3_ref[...].T, axis=0, keepdims=True)
+        row = r2_ref[1024:1032]
+        row = row[:, 0:128] + pltpu.roll(row[:, 0:128], 64, 1) + row[:, 128:256]
+        g2_ref[512:513] = row[0:1]
+        row = r3_ref[1152:1160]
+        row = row[:, 0:128] + row[:, 128:256]
+        g3_ref[576:577] = (row + pltpu.roll(row, 64, 1))[0:1]
         lane = lax.broadcasted_iota(jnp.int32, (1, HID), 1)
         packed_ref[...] = jnp.zeros(packed_ref.shape, F32)
         for ref, rows, base, phase in ((g2_ref, 72, 16, 32), (g3_ref, 80, 80, 96)):
@@ -639,10 +638,8 @@
             jax.ShapeDtypeStruct((4 * BLOCK_ROWS, 128), F32),
         ],
         scratch_shapes=[
-            pltpu.VMEM((1024, 256), F32),
-            pltpu.VMEM((1152, 256), F32),
-            pltpu.VMEM((C2, 256), F32),
-            pltpu.VMEM((C3, 256), F32),
+            pltpu.VMEM((1040, 256), F32),
+            pltpu.VMEM((1168, 256), F32),
             pltpu.VMEM((20, 20, C1, 256), BF16),
             pltpu.VMEM((11, 8, C3, 256), BF16),
             pltpu.VMEM((640, 128), F32),
@@ -655,7 +652,7 @@
 
 
 def lower_body(
-    x0, x1, x2, x3, x4, a1_ref, d2_ref, t2_ref, packed_ref, r1_ref, s1_ref, g1_ref, d1_ref
+    x0, x1, x2, x3, x4, a1_ref, d2_ref, t2_ref, packed_ref, r1_ref, g1_ref, d1_ref
 ):
     x_refs = (x0, x1, x2, x3, x4)
     t = pl.program_id(1)
@@ -663,9 +660,8 @@
     @pl.when((pl.program_id(0) == 0) & (t == 0))
     def _():
         r1_ref[...] = jnp.zeros(r1_ref.shape, F32)
-        s1_ref[...] = jnp.zeros(s1_ref.shape, F32)
-
-    sums = jnp.zeros((C1, 256), F32)
+
+    zero = jnp.zeros((), BF16)
     for h in range(2):
         held = None
         for n in range(10):
@@ -678,15 +674,14 @@
                 for y in range(2):
                     k = 32 * (2 * x + y)
                     kept = a1_ref[2 * h + y, 2 * n + x] > 0
-                    masked = jnp.where(kept, back[k : k + 32], 0.0).astype(BF16)
-                    sums = sums + masked.astype(F32)
+                    masked = jnp.where(kept, back[k : k + 32].astype(BF16), zero)
                     row = 128 * (n % 2) + k
-                    d1_ref[row : row + 32, 256 * (n // 2) : 256 * (n // 2) + 256] = masked
+                    d1_ref[h, row : row + 32, 256 * (n // 2) : 256 * (n // 2) + 256] = masked
         window = jnp.concatenate(
             [pixel_window(x_refs, 2 * h, 64 * n, 80) for n in range(5)], axis=1
         )
-        r1_ref[...] += mm_nt(window, d1_ref[...])
-    s1_ref[...] += sums
+        window = jnp.concatenate([window, jnp.ones((16, window.shape[1]), BF16)], axis=0)
+        r1_ref[...] += mm_nt(window, d1_ref[h])
 
     @pl.when((pl.program_id(0) == pl.num_programs(0) - 1) & (t == 4))
     def _():
@@ -701,7 +696,9 @@
                     slab = r1_ref[k : k + 32, col : col + 128]
                     total = total + (pltpu.roll(slab, 128 - turn, 1) if turn else slab)
             g1_ref[32 * i : 32 * i + 32] = total
-        g1_ref[256:257, 0:32] = jnp.sum(s1_ref[...].T, axis=0, keepdims=True)
+        row = r1_ref[960:968, 0:128] + r1_ref[960:968, 128:256]
+        row = row + pltpu.roll(row, 64, 1)
+        g1_ref[256:257] = (row + pltpu.roll(row, 96, 1))[0:1]
         packed_ref[...] = jnp.zeros(packed_ref.shape, F32)
         for j, part in enumerate(fold(g1_ref, 32, 24)):
             packed_ref[pl.ds(j, 24, stride=4), :] = part
@@ -721,10 +718,9 @@
         out_specs=whole((4 * BLOCK_ROWS, 128)),
         out_shape=jax.ShapeDtypeStruct((4 * BLOCK_ROWS, 128), F32),
         scratch_shapes=[
-            pltpu.VMEM((960, 256), F32),
-            pltpu.VMEM((C1, 256), F32),
+            pltpu.VMEM((976, 256), F32),
             pltpu.VMEM((384, 128), F32),
-            pltpu.VMEM((256, 1280), BF16),
+            pltpu.VMEM((2, 256, 1280), BF16),
         ],
         compiler_params=pltpu.CompilerParams(vmem_limit_bytes=VMEM_LIMIT),
         name="lower_backward",
@@ -757,38 +753,59 @@
 
 def gather_blocks(block, beside, lanes, place):
     blocks = block[None]
-    for step in reversed(halving_order(lanes)):
+    arrived = []
+    for k, step in enumerate(reversed(halving_order(lanes))):
+        other = swap(blocks, lanes, step)
+        if k < len(beside):
+            other, part = lax.optimization_barrier((other, beside[k]))
+            arrived.append(part)
         if step == 1:
-            blocks, beside = lax.optimization_barrier((blocks, beside))
-        other = swap(blocks, lanes, step)
+            return blocks, other, arrived
         high = (place // step) % 2 == 1
         blocks = jnp.stack(
             [jnp.where(high, other, blocks), jnp.where(high, blocks, other)], axis=1
         ).reshape((2 * blocks.shape[0],) + blocks.shape[1:])
-    return blocks, beside
-
-
-def first_rows_everywhere(local, sums, lanes, place):
-    rows = local.shape[0]
+
+
+def first_rows_everywhere(master, sums, lanes, place):
+    rows = master.shape[0] // HID
     owners = -(-(TOP + 1) // rows)
     order = halving_order(lanes)
     if owners == 1:
-        block = jnp.pad(local[: TOP + 1], ((0, BLOCK_ROWS - TOP - 1), (0, 0)))
-        block = jnp.where(place == 0, block, jnp.zeros((), BF16))
-        for step in reversed(order):
-            pairs = [(i, i + step) for i in range(0, lanes, 2 * step)]
-            came = lax.ppermute(block, "dp", pairs)
-            block, sums = lax.optimization_barrier((block + came, sums + swap(sums, lanes, step)))
-        return block, sums
+        block = master[: BLOCK_ROWS * HID].reshape(BLOCK_ROWS, HID).astype(BF16)
+        row = lax.broadcasted_iota(jnp.int32, (BLOCK_ROWS, 1), 0)
+        block = jnp.where((place == 0) & (row <= TOP), block, jnp.zeros((), BF16))
+        steps = list(reversed(order))
+        left = list(order)
+        while steps:
+            now, steps = steps[:2], steps[2:]
+            jumps = now if len(now) == 1 else [now[0], now[1], now[0] + now[1]]
+            total = block
+            for jump in jumps:
+                pairs = [(i, i + jump) for i in range(0, lanes, 2 * now[0])]
+                total = total + lax.ppermute(block, "dp", pairs)
+            summed = sums + swap(sums, lanes, left.pop(0))
+            block, sums = lax.optimization_barrier((total, summed))
+        return block, sums, left
+    local = master.reshape(rows, HID).astype(BF16)
     block = jnp.zeros((owners, rows, HID), BF16)
     block = jnp.where(jnp.arange(owners)[:, None, None] == place, local[None], block)
     block = sum_everywhere(block, lanes).reshape(owners * rows, HID)[: TOP + 1]
-    return jnp.pad(block, ((0, BLOCK_ROWS - TOP - 1), (0, 0))), sum_everywhere(sums, lanes)
-
-
-def facts_body(dense_ref, piece_ref, loss_ref, message_ref):
+    return jnp.pad(block, ((0, BLOCK_ROWS - TOP - 1), (0, 0))), sums, order
+
+
+def finish_blocks(own_len):
+    block = min(208, -(-own_len // 8) * 8)
+    return block, -(-own_len // block)
+
+
+def facts_body(dense_ref, piece_ref, loss_ref, message_ref, *part_refs):
     dense = dense_ref[...]
     piece = piece_ref[...]
+    start = 0
+    for ref in part_refs:
+        ref[...] = dense[start : start + ref.shape[0]]
+        start += ref.shape[0]
     squares = jnp.sum(dense * dense, axis=0, keepdims=True)
     squares = squares + jnp.sum(piece * piece, axis=0, keepdims=True)
     squares = jnp.sum(squares, axis=1, keepdims=True)
@@ -799,21 +816,30 @@
 
 
 def facts_message(dense, piece, loss):
-    return pl.pallas_call(
+    own_len = dense.shape[0]
+    block, steps = finish_blocks(own_len)
+    first = block * (steps // 2)
+    lengths = [length for length in (first, own_len - first) if length]
+    shapes = [(piece.shape[0] + 8, 128)] + [(length, 128) for length in lengths]
+    message, *parts = pl.pallas_call(
         facts_body,
-        out_shape=jax.ShapeDtypeStruct((piece.shape[0] + 8, 128), F32),
+        out_shape=[jax.ShapeDtypeStruct(shape, F32) for shape in shapes],
         name="facts_message",
     )(dense, piece, loss)
+    return message, parts
 
 
 def finish_body(
     parts,
     own_len,
+    switch,
     place_ref,
     scalars_ref,
-    messages_ref,
+    near_ref,
+    far_ref,
+    low_other_ref,
+    high_other_ref,
     mine_ref,
-    other_ref,
     first_ref,
     other_first_ref,
     second_ref,
@@ -831,7 +857,7 @@
     loss_ref,
     extra_ref,
 ):
-    height = messages_ref.shape[2] - 8
+    height = near_ref.shape[2] - 8
     place = place_ref[0]
     first_step = pl.program_id(0) == 0
 
@@ -846,13 +872,14 @@
             high = min(stop, own_len - shift)
 
             @pl.when(first_step & (place == owner))
-            def _(shift=shift, low=low, high=high):
+            def _(owner=owner, shift=shift, low=low, high=high):
                 for k in range(low // height, (high - 1) // height + 1):
                     a = max(low, k * height)
                     b = min(high, (k + 1) * height)
+                    source = near_ref if k % 2 == owner % 2 else far_ref
                     for g in range(2):
-                        extra_ref[g, a + shift : b + shift] = messages_ref[
-                            k, g, a - k * height : b - k * height
+                        extra_ref[g, a + shift : b + shift] = source[
+                            k // 2, g, a - k * height : b - k * height
                         ]
 
     block = master_ref.shape[0]
@@ -860,7 +887,8 @@
 
     factors = []
     for g in range(2):
-        facts = jnp.sum(messages_ref[:, g, height : height + 8, :], axis=0)
+        facts = jnp.sum(near_ref[:, g, height : height + 8, :], axis=0)
+        facts = facts + jnp.sum(far_ref[:, g, height : height + 8, :], axis=0)
         norm = jnp.sqrt(facts[0:1, 0:1])
         factors.append(jnp.minimum(1.0, CLIP_NORM / (norm + 1e-06)))
         if g == 0:
@@ -868,8 +896,8 @@
             loss_ref[...] = facts[1:2, 0:1]
     master = master_ref[...]
 
-    def inner_step(g, dense_ref, one_ref, two_ref):
-        clipped = (dense_ref[...] + extra_ref[g, here]) * factors[g]
+    def inner_step(g, dense, one_ref, two_ref):
+        clipped = (dense + extra_ref[g, here]) * factors[g]
         first_next = BETA_ONE * one_ref[...] + (1.0 - BETA_ONE) * clipped
         second_next = BETA_TWO * two_ref[...] + (1.0 - BETA_TWO) * clipped * clipped
         first_hat = first_next / scalars_ref[0]
@@ -879,11 +907,12 @@
         )
         return clipped, first_next, second_next, master - inner
 
-    clipped, first_next, second_next, drift = inner_step(0, mine_ref, first_ref, second_ref)
+    clipped, first_next, second_next, drift = inner_step(0, mine_ref[...], first_ref, second_ref)
     clipped_ref[:, 0, :] = clipped
     first_out[:, 0, :] = first_next
     second_out[:, 0, :] = second_next
-    _, _, _, other_drift = inner_step(1, other_ref, other_first_ref, other_second_ref)
+    other = jnp.where(pl.program_id(0) < switch, low_other_ref[...], high_other_ref[...])
+    _, _, _, other_drift = inner_step(1, other, other_first_ref, other_second_ref)
     moved = (drift + other_drift) / 2.0
     moved_ref[...] = moved
     momentum_next = OUTER_MOMENTUM * momentum_ref[...] + moved
@@ -893,10 +922,9 @@
     low_ref[...] = final.astype(BF16)
 
 
-def finish(parts, place, scalars, messages, *arrays):
+def finish(parts, place, scalars, near, far, others, *arrays):
     own_len = arrays[0].shape[0]
-    block = min(208, -(-own_len // 8) * 8)
-    steps = -(-own_len // block)
+    block, steps = finish_blocks(own_len)
     scalar = pl.BlockSpec(memory_space=pltpu.SMEM)
 
     def spec(array):
@@ -908,14 +936,19 @@
     outs += [jax.ShapeDtypeStruct((own_len, 128), F32)] * 3
     outs += [jax.ShapeDtypeStruct((own_len, 128), BF16)]
     return pl.pallas_call(
-        lambda *refs: finish_body(parts, own_len, *refs),
+        lambda *refs: finish_body(parts, own_len, steps // 2, *refs),
         grid=(steps,),
-        in_specs=[scalar, scalar, whole(messages.shape)] + [spec(array) for array in arrays],
+        in_specs=[scalar, scalar, whole(near.shape), whole(far.shape)]
+        + [
+            pl.BlockSpec((block, 128), lambda k: (jnp.minimum(k, max(steps // 2 - 1, 0)), 0)),
+            pl.BlockSpec((block, 128), lambda k: (jnp.maximum(k - steps // 2, 0), 0)),
+        ]
+        + [spec(array) for array in arrays],
         out_specs=[spec(array) for array in outs] + [whole((1, 1))] * 2,
         out_shape=outs + [jax.ShapeDtypeStruct((1, 1), F32)] * 2,
         scratch_shapes=[pltpu.VMEM((2, block * steps, 128), F32)],
         name="finish",
-    )(place, scalars, messages, *arrays)
+    )(place, scalars, near, far, *others, *arrays)
 
 
 def on_device(
@@ -953,10 +986,19 @@
     envs_here, steps_here = advantage.shape
     batch = envs_here * steps_here
     total_frames = batch * lanes
-    block, sums = first_rows_everywhere(low_rows, sums, lanes, place)
+    block, sums, left = first_rows_everywhere(master, sums, lanes, place)
+    while len(left) > 2:
+        sums = sums + swap(sums, lanes, left.pop(0))
     x = frames[0].transpose(0, 2, 3, 1)
+    came = swap(sums, lanes, left.pop(0)) if left else jnp.zeros_like(sums)
     t1, b1, t2, b2, t3, b3, back3, back2 = conv_weights(block)
+    t1, came = lax.optimization_barrier((t1, came))
+    sums = sums + came
+    came = swap(sums, lanes, left.pop(0)) if left else jnp.zeros_like(sums)
     a1, a2, a3 = conv_forward(x, t1, b1, t2, b2, t3, b3)
+    a3, came = lax.optimization_barrier((a3, came))
+    sums = sums + came
+
     tail = TOP + FEATURES + 1
     head_owner = tail // rows
     head_flat = gathered[head_owner:].reshape((lanes - head_owner) * rows, HID)
@@ -999,9 +1041,11 @@
     head_part = jnp.pad(head_part, ((0, count - real), (0, 0)))
     small = jnp.concatenate([lower + upper, head_part], axis=0)
     piece = scatter_sum(small.reshape(lanes, count // lanes, 128), lanes, place)
-    message = facts_message(dense_owned, piece, loss_local)
-    messages, dense_other = gather_blocks(
-        jnp.stack([message, other_group(message)]), other_group(dense_owned), lanes, place
+    message, dense_parts = facts_message(dense_owned, piece, loss_local)
+    both = jnp.stack([message, other_group(message)])
+    both, *dense_parts = lax.optimization_barrier((both, *dense_parts))
+    near, far, dense_parts = gather_blocks(
+        both, [other_group(part) for part in dense_parts], lanes, place
     )
 
     own_len = 4 * rows
@@ -1018,9 +1062,10 @@
         parts,
         place.reshape(1),
         scalars,
-        messages,
+        near,
+        far,
+        (dense_parts[0], dense_parts[-1]),
         dense_owned,
-        dense_other,
         view(first_flat),
         view(other_first),
         view(second_flat),

time: 216 us -> 209 us (0.968)
  waiting for transfers between devices: 48.5 us -> 40.6 us
  starting transfers between devices: 25.9 us -> 28.9 us
  other arithmetic: 10.9 us -> 8.62 us
    ppermute x12, waiting for transfers between devices: 41.1 us -> 35.9 us  [swap(): return lax.ppermute(value, 'dp', [(i, i ^ step) for i in range(lanes)])]
    ppermute x4 -> x6, starting transfers between devices: 9.88 us -> 13.5 us  [first_rows_everywhere(): total = total + lax.ppermute(block, 'dp', pairs)]
    ppermute x4 -> x5, waiting for transfers between devices: 6.65 us -> 3.31 us  [other_group(): return lax.ppermute(value, 'group', [(0, 1), (1, 0)])]
    ppermute x4 -> x5, starting transfers between devices: 5.1 us -> 6.63 us  [other_group(): return lax.ppermute(value, 'group', [(0, 1), (1, 0)])]
  transfers between devices with their start and end apart: 22 -> 25, of which waited for: 15 -> 14; matrix products, arithmetic and copies ran while one was open for 4% -> 4% of each run, Pallas kernels for 42% -> 44%
where the time goes in v5:
time: 209 us; the launch traced here: 208 us
  Pallas kernels  110 us (53%)
  waiting for transfers between devices  40.6 us (19%)
  starting transfers between devices  28.9 us (14%)
  between operations  15.3 us (7%)
  other arithmetic  8.62 us (4%)
  local copies, waits for them, and re-layouts  4.27 us (2%)
    pallas_call x1, Pallas kernels, lower_backward(): pl.pallas_call(lower_body, grid=(envs // 2, 5), in_specs=pixel_specs() +...  36.6 us
    ppermute x12, waiting for transfers between devices, swap(): return lax.ppermute(value, 'dp', [(i, i ^ step) for i in range(lanes)])  35.9 us
    pallas_call x1, Pallas kernels, upper_backward(): pl.pallas_call(upper_body, grid=(frames // 256,), in_specs=[pl.BlockSpec(...  27.1 us
    pallas_call x1, Pallas kernels, conv_forward(): pl.pallas_call(forward_body, grid=(envs // 2,), in_specs=[pl.BlockSpec(me...  23.2 us
    ppermute x6, starting transfers between devices, first_rows_everywhere(): total = total + lax.ppermute(block, 'dp', pairs)  13.5 us
    pallas_call x1, Pallas kernels, dense_step(): pl.pallas_call(lambda *refs: dense_body(scale, *refs), in_specs=[away, aw...  10.9 us
    ppermute x12, starting transfers between devices, swap(): return lax.ppermute(value, 'dp', [(i, i ^ step) for i in range(lanes)])  8.74 us
    ppermute x5, starting transfers between devices, other_group(): return lax.ppermute(value, 'group', [(0, 1), (1, 0)])  6.63 us
  transfers between devices with their start and end apart: 25, of which 14 were waited for; matrix products, arithmetic and copies ran while one was open for 4% of the time, Pallas kernels for 44%

profile of v5, /device:TPU:0, one launch (start us, length us, event | category | flops | bytes accessed | tf_op | source)
XLA Modules:
  0.0 208.0 jit_solution(8973265267593620280)
XLA Ops:
  7.2 1.0 convert.3
  8.3 0.8 convert_element_type.25
  9.4 7.0 %collective-permute-start.2 = (bf16[168,512]{1,0:T(8,128)(2,1)S(1)}, bf16[168,512]{1,0:T(8,128)(2,1)S(1)}, u32[]{:S(2)}, u32[]{:S(2)}) collective-permute-start(bf16[168,512]{1,0:T(8,128)(2,1)S(1)} %broadcast_select_fusion), channel_id=1, source_target_pairs={{0,12},{16,28}} | collective-permute-start | bytes 516104 | tf_op jit(solution)/shard_map/ppermute | solution.py:786
  16.4 1.3 collective-permute-start.1
  17.7 1.3 collective-permute-start
  19.0 2.0 advantages.1
  21.0 1.4 collective-permute-done.3
  22.4 0.7 add.77
  23.1 1.4 collective-permute-done
  24.6 1.3 collective-permute-start.6
  25.9 1.3 collective-permute-start.5
  27.2 1.3 collective-permute-start.4
  28.6 3.6 %collective-permute-done.7 = f32[8,128]{1,0:T(8,128)S(1)} collective-permute-done((f32[8,128]{1,0:T(8,128)S(1)}, f32[8,128]{1,0:T(8,128)S(1)}, u32[]{:S(2)}, u32[]{:S(2)}) %collective-permute-start.7) | collective-permute-done | bytes 4128 | tf_op jit(solution)/shard_map/ppermute | solution.py:731
  32.2 0.7 add_add_fusion.conv_ref
  32.9 2.3 %conv_weights.1 = (bf16[128,192]{1,0:T(8,128)(2,1)}, f32[64,256]{1,0:T(8,128)}, bf16[128,256]{1,0:T(8,128)(2,1)}, f32[64,256]{1,0:T(8,128)}, bf16[192,192]{1,0:T...) custom-call(bf16[168,512]{1,0:T(8,128)(2,1)} %add_add_fusion.conv_ref), custom_call_target="tpu_custom_call" | custom-call | tf_op jit(solution)/shard_map/conv_weights/pallas_call | solution.py:175
  35.2 1.3 collective-permute-done.8
  36.5 3.4 %collective-permute-start.9 = (f32[8,128]{1,0:T(8,128)S(1)}, f32[8,128]{1,0:T(8,128)S(1)}, u32[]{:S(2)}, u32[]{:S(2)}) collective-permute-start(f32[8,128]{1,0:T(8,128)S(1)} %add.82), channel_id=1, source_target_pairs={{0,8},{1,9},{2,10},{3,11},{4,12},{5,13},{6,14},{7,15},{8,0},{9,1},... | collective-permute-start | bytes 12296 | tf_op jit(solution)/shard_map/ppermute | solution.py:731
  39.9 23.2 %conv_forward.1 = (bf16[20,20,32,512]{3,2,1,0:T(8,128)(2,1)}, bf16[9,10,64,512]{3,2,1,0:T(8,128)(2,1)}, bf16[7,7,64,512]{3,2,1,0:T(8,128)(2,1)}) custom-call(bf16[4,84,336,128]{3,2,1,0:T(8,128)(2,1)} %bitcast.123, bf16[128,192]{1,0:T(8,128)(2,1)} %get-tuple-element.69.t1_ref, f32[64,256]{1,0:T(8,128)} %get-tuple-element.70.b1_ref, ...), custom_call_target="tpu_custom_call" | custom-call | tf_op jit(solution)/shard_map/conv_forward/pallas_call | solution.py:292
  63.7 0.7 slice.83
  64.9 0.7 pad.8.refs_2_
  65.6 10.9 %dense_step.1 = (f32[16,828,128]{2,1,0:T(8,128)}, bf16[3136,512]{1,0:T(8,128)(2,1)}, bf16[512,512]{1,0:T(8,128)(2,1)}, f32[32,512]{1,0:T(8,128)}, f32[32,1]{1,0:T(8,128)}, /*index=5*/f32[1,1]{1,0:T(1,128)}) custom-call(bf16[3136,512]{1,0:T(8,128)(2,1)} %bitcast.129, bf16[16,207,512]{2,1,0:T(8,128)(2,1)} %all-gather.2.cloned.1.call-done.refs_1_, ...), custom_call_target="tpu_custom_call" | custom-call | tf_op jit(solution)/shard_map/dense_step/pallas_call | solution.py:465
  76.5 1.0 reduce
  77.6 0.9 collective-permute-start.10
  78.4 1.0 reduce.1
  79.5 1.3 collective-permute-start.11
  81.5 27.1 %upper_backward.1 = (bf16[11,11,64,512]{3,2,1,0:T(8,128)(2,1)}, f32[672,128]{1,0:T(8,128)}) custom-call(bf16[20,20,32,512]{3,2,1,0:T(8,128)(2,1)} %get-tuple-element.81.a1_hbm.a1_ref, bf16[9,10,64,512]{3,2,1,0:T(8,128)(2,1)} %get-tuple-element.82.a2_ref, bf16[7,7,64,512]{3,2,1,0:T(8,128)(2,1)} %get-tuple-element.77.a3_ref, ...), custom_call_target="tpu_custom_call" | custom-call | tf_op jit(solution)/shard_map/upper_backward/pallas_call | solution.py:621
  108.6 36.6 %lower_backward.1 = f32[672,128]{1,0:T(8,128)} custom-call(bf16[4,84,336,128]{3,2,1,0:T(8,128)(2,1)} %bitcast.124, bf16[4,84,336,128]{3,2,1,0:T(8,128)(2,1)} %bitcast.125, bf16[4,84,336,128]{3,2,1,0:T(8,128)(2,1)} %bitcast.126, bf16[4,84,336,128]{3,2,1,0:T(8,128)(2,1)} %bitcast.127, bf16[4,84,336,128]{3,2,1,0:T(8,128)(2,1)} %bitcast.128, ...), custom_call_target="tpu_custom_call" | custom-call | tf_op jit(solution)/shard_map/lower_backward/pallas_call | solution.py:709
  145.2 1.0 add.85
  146.4 1.4 collective-permute-done.12
  147.9 2.0 collective-permute-start.13
  149.9 4.3 %collective-permute-done.13 = f32[4,48,128]{2,1,0:T(8,128)S(1)} collective-permute-done((f32[4,48,128]{2,1,0:T(8,128)S(1)}, f32[4,48,128]{2,1,0:T(8,128)S(1)}, u32[]{:S(2)}, u32[]{:S(2)}) %collective-permute-start.13) | collective-permute-done | bytes 98336 | tf_op jit(solution)/shard_map/ppermute | solution.py:731
  154.3 1.6 collective-permute-start.14
  155.8 5.8 %collective-permute-done.14 = f32[2,48,128]{2,1,0:T(8,128)S(1)} collective-permute-done((f32[2,48,128]{2,1,0:T(8,128)S(1)}, f32[2,48,128]{2,1,0:T(8,128)S(1)}, u32[]{:S(2)}, u32[]{:S(2)}) %collective-permute-start.14) | collective-permute-done | bytes 49184 | tf_op jit(solution)/shard_map/ppermute | solution.py:731
  161.8 4.7 %collective-permute-done.15 = f32[1,48,128]{2,1,0:T(8,128)S(1)} collective-permute-done((f32[1,48,128]{2,1,0:T(8,128)S(1)}, f32[1,48,128]{2,1,0:T(8,128)S(1)}, u32[]{:S(2)}, u32[]{:S(2)}) %collective-permute-start.15) | collective-permute-done | bytes 24608 | tf_op jit(solution)/shard_map/ppermute | solution.py:731
  166.5 0.6 fusion.3.piece_ref
  167.1 2.5 %facts_message.1 = (f32[56,128]{1,0:T(8,128)}, f32[416,128]{1,0:T(8,128)}, f32[412,128]{1,0:T(8,128)}) custom-call(f32[828,128]{1,0:T(8,128)} %bitcast.137, f32[48,128]{1,0:T(8,128)} %fusion.3.piece_ref, f32[1,1]{1,0:T(1,128)} %get-tuple-element.95.loss_ref), custom_call_target="tpu_custom_call" | custom-call | tf_op jit(solution)/shard_map/facts_message/pallas_call | solution.py:824
  169.6 1.9 collective-permute-start.16
  171.5 2.1 %collective-permute-done.16 = f32[56,128]{1,0:T(8,128)S(1)} collective-permute-done((f32[56,128]{1,0:T(8,128)}, f32[56,128]{1,0:T(8,128)S(1)}, u32[]{:S(2)}, u32[]{:S(2)}) %collective-permute-start.16) | collective-permute-done | bytes 28704 | tf_op jit(solution)/shard_map/ppermute | solution.py:977
  173.7 0.8 pad_maximum_fusion.2
  174.4 1.9 collective-permute-start.18
  177.0 4.6 %collective-permute-done.17 = f32[1,2,56,128]{3,2,1,0:T(8,128)S(1)} collective-permute-done((f32[1,2,56,128]{3,2,1,0:T(8,128)S(1)}, f32[1,2,56,128]{3,2,1,0:T(8,128)S(1)}, u32[]{:S(2)}, u32[]{:S(2)}) %collective-permute-start.17) | collective-permute-done | bytes 57376 | tf_op jit(solution)/shard_map/ppermute | solution.py:731
  181.6 0.7 collective-permute-start.19
  182.3 1.2 collective-permute-done.20.refs_5_
  183.4 3.0 %collective-permute-done.19 = f32[2,2,56,128]{3,2,1,0:T(8,128)S(1)} collective-permute-done((f32[2,2,56,128]{3,2,1,0:T(8,128)S(1)}, f32[2,2,56,128]{3,2,1,0:T(8,128)S(1)}, u32[]{:S(2)}, u32[]{:S(2)}) %collective-permute-start.19) | collective-permute-done | bytes 114720 | tf_op jit(solution)/shard_map/ppermute | solution.py:731
  186.5 0.8 collective-permute-start.21
  187.4 5.3 %collective-permute-done.21 = f32[4,2,56,128]{3,2,1,0:T(8,128)S(1)} collective-permute-done((f32[4,2,56,128]{3,2,1,0:T(8,128)S(1)}, f32[4,2,56,128]{3,2,1,0:T(8,128)S(1)}, u32[]{:S(2)}, u32[]{:S(2)}) %collective-permute-start.21) | collective-permute-done | bytes 229408 | tf_op jit(solution)/shard_map/ppermute | solution.py:731
  194.6 0.8 copy-done.3
  195.4 5.7 %finish.1 = (f32[828,1,128]{2,1,0:T(1,128)}, f32[828,1,128]{2,1,0:T(1,128)}, f32[828,1,128]{2,1,0:T(1,128)}, f32[828,128]{1,0:T(8,128)}, f32[828,128]{1,0:T(8,12...) custom-call(s32[1]{0:T(128)} %bitcast.refs_0_, ...), custom_call_target="tpu_custom_call" | custom-call | tf_op jit(solution)/shard_map/finish/pallas_call | solution.py:938
  (83 shorter events, 4.5 us)
Async XLA Ops:
  7.2 56.6 %all-gather.2.cloned.1.call-start = ((), (), s32[]{:S(2)}) async-start(), calls=%async_computation.1 | async-start | bytes 3620864 | tf_op jit(solution)/shard_map/all_gather | solution.py:981
  9.1 158.0 %reduce-scatter.2.cloned.1.call-start = ((), (), s32[]{:S(2)}) async-start(), calls=%async_computation.2 | async-start | bytes 7241728 | tf_op jit(solution)/shard_map/reduce_scatter | solution.py:1018
  9.4 13.7 %collective-permute-start.2 = (bf16[168,512]{1,0:T(8,128)(2,1)S(1)}, bf16[168,512]{1,0:T(8,128)(2,1)S(1)}, u32[]{:S(2)}, u32[]{:S(2)}) collective-permute-start(bf16[168,512]{1,0:T(8,128)(2,1)S(1)} %broadcast_select_fusion), channel_id=1, source_target_pairs={{0,12},{16,28}} | collective-permute-start | bytes 516104 | tf_op jit(solution)/shard_map/ppermute | solution.py:786
  16.4 6.7 %collective-permute-start.1 = (bf16[168,512]{1,0:T(8,128)(2,1)S(1)}, bf16[168,512]{1,0:T(8,128)(2,1)S(1)}, u32[]{:S(2)}, u32[]{:S(2)}) collective-permute-start(bf16[168,512]{1,0:T(8,128)(2,1)S(1)} %broadcast_select_fusion), channel_id=1, source_target_pairs={{0,4},{16,20}} | collective-permute-start | bytes 516104 | tf_op jit(solution)/shard_map/ppermute | solution.py:786
  17.7 6.7 %collective-permute-start = (bf16[168,512]{1,0:T(8,128)(2,1)S(1)}, bf16[168,512]{1,0:T(8,128)(2,1)S(1)}, u32[]{:S(2)}, u32[]{:S(2)}) collective-permute-start(bf16[168,512]{1,0:T(8,128)(2,1)S(1)} %broadcast_select_fusion), channel_id=1, source_target_pairs={{0,8},{16,24}} | collective-permute-start | bytes 516104 | tf_op jit(solution)/shard_map/ppermute | solution.py:786
  21.0 1.4 collective-permute-start.3
  24.6 7.6 %collective-permute-start.6 = (bf16[168,512]{1,0:T(8,128)(2,1)S(1)}, bf16[168,512]{1,0:T(8,128)(2,1)S(1)}, u32[]{:S(2)}, u32[]{:S(2)}) collective-permute-start(bf16[168,512]{1,0:T(8,128)(2,1)S(1)} %add_add_fusion.1), channel_id=1, source_target_pairs={{0,3},{4,7},{8,11},{12,15},{16,19},{20,23},{24,27},{28,31}} | collective-permute-start | bytes 516104 | tf_op jit(solution)/shard_map/ppermute | solution.py:786
  25.9 6.3 %collective-permute-start.5 = (bf16[168,512]{1,0:T(8,128)(2,1)S(1)}, bf16[168,512]{1,0:T(8,128)(2,1)S(1)}, u32[]{:S(2)}, u32[]{:S(2)}) collective-permute-start(bf16[168,512]{1,0:T(8,128)(2,1)S(1)} %add_add_fusion.1), channel_id=1, source_target_pairs={{0,1},{4,5},{8,9},{12,13},{16,17},{20,21},{24,25},{28,29}} | collective-permute-start | bytes 516104 | tf_op jit(solution)/shard_map/ppermute | solution.py:786
  27.2 5.0 %collective-permute-start.4 = (bf16[168,512]{1,0:T(8,128)(2,1)S(1)}, bf16[168,512]{1,0:T(8,128)(2,1)S(1)}, u32[]{:S(2)}, u32[]{:S(2)}) collective-permute-start(bf16[168,512]{1,0:T(8,128)(2,1)S(1)} %add_add_fusion.1), channel_id=1, source_target_pairs={{0,2},{4,6},{8,10},{12,14},{16,18},{20,22},{24,26},{28,30}} | collective-permute-start | bytes 516104 | tf_op jit(solution)/shard_map/ppermute | solution.py:786
  28.5 3.7 %collective-permute-start.7 = (f32[8,128]{1,0:T(8,128)S(1)}, f32[8,128]{1,0:T(8,128)S(1)}, u32[]{:S(2)}, u32[]{:S(2)}) collective-permute-start(f32[8,128]{1,0:T(8,128)S(1)} %add.77), channel_id=1, source_target_pairs={{0,2},{1,3},{2,0},{3,1},{4,6},{5,7},{6,4},{7,5},{8,10},{9,11},{10,... | collective-permute-start | bytes 12296 | tf_op jit(solution)/shard_map/ppermute | solution.py:731
  32.9 3.6 %collective-permute-start.8 = (f32[8,128]{1,0:T(8,128)S(1)}, f32[8,128]{1,0:T(8,128)S(1)}, u32[]{:S(2)}, u32[]{:S(2)}) collective-permute-start(f32[8,128]{1,0:T(8,128)S(1)} %add.81), channel_id=1, source_target_pairs={{0,4},{1,5},{2,6},{3,7},{4,0},{5,1},{6,2},{7,3},{8,12},{9,13},{10,... | collective-permute-start | bytes 12296 | tf_op jit(solution)/shard_map/ppermute | solution.py:731
  36.5 26.6 %collective-permute-start.9 = (f32[8,128]{1,0:T(8,128)S(1)}, f32[8,128]{1,0:T(8,128)S(1)}, u32[]{:S(2)}, u32[]{:S(2)}) collective-permute-start(f32[8,128]{1,0:T(8,128)S(1)} %add.82), channel_id=1, source_target_pairs={{0,8},{1,9},{2,10},{3,11},{4,12},{5,13},{6,14},{7,15},{8,0},{9,1},... | collective-permute-start | bytes 12296 | tf_op jit(solution)/shard_map/ppermute | solution.py:731
  65.6 11.0 %copy-start.4 = (f32[1,105984]{1,0:T(1,128)S(1)}, f32[1,105984]{1,0:T(1,128)}, u32[]{:S(2)}) copy-start(f32[1,105984]{1,0:T(1,128)} %param.22) | copy-start | bytes 1271812
  76.5 2.0 copy-start.5
  76.5 4.3 %copy-start.9 = (f32[32,512]{1,0:T(8,128)S(1)}, f32[32,512]{1,0:T(8,128)}, u32[]{:S(2)}) copy-start(f32[32,512]{1,0:T(8,128)} %get-tuple-element.93) | copy-start | bytes 196612
  76.5 4.8 %copy-start.10 = (f32[32,1]{1,0:T(8,128)S(1)}, f32[32,1]{1,0:T(8,128)}, u32[]{:S(2)}) copy-start(f32[32,1]{1,0:T(8,128)} %get-tuple-element.94) | copy-start | bytes 388
  77.6 31.0 %copy-start.1 = (f32[105984]{0:T(1024)}, f32[105984]{0:T(1024)S(1)}, u32[]{:S(2)}) copy-start(f32[105984]{0:T(1024)S(1)} %reduce) | copy-start | bytes 1271812
  77.6 31.0 %collective-permute-start.10 = (f32[105984]{0:T(1024)S(1)}, f32[105984]{0:T(1024)}, u32[]{:S(2)}, u32[]{:S(2)}) collective-permute-start(f32[105984]{0:T(1024)S(1)} %reduce), channel_id=1, source_target_pairs={{0,16},{16,0},{1,17},{17,1},{2,18},{18,2},{3,19},{19,3},{4,20},{20... | collective-permute-start | bytes 1271816 | tf_op jit(solution)/shard_map/ppermute | solution.py:977
  79.4 29.2 %copy-start.2 = (f32[105984]{0:T(1024)}, f32[105984]{0:T(1024)S(1)}, u32[]{:S(2)}) copy-start(f32[105984]{0:T(1024)S(1)} %reduce.1) | copy-start | bytes 1271812
  79.5 29.2 %collective-permute-start.11 = (f32[105984]{0:T(1024)S(1)}, f32[105984]{0:T(1024)}, u32[]{:S(2)}, u32[]{:S(2)}) collective-permute-start(f32[105984]{0:T(1024)S(1)} %reduce.1), channel_id=1, source_target_pairs={{0,16},{16,0},{1,17},{17,1},{2,18},{18,2},{3,19},{19,3},{4,20},{20... | collective-permute-start | bytes 1271816 | tf_op jit(solution)/shard_map/ppermute | solution.py:977
  108.6 36.6 %copy-start.6 = (f32[672,128]{1,0:T(8,128)S(1)}, f32[672,128]{1,0:T(8,128)}, u32[]{:S(2)}) copy-start(f32[672,128]{1,0:T(8,128)} %get-tuple-element.92) | copy-start | bytes 1032196
  146.3 1.5 collective-permute-start.12
  147.9 6.3 %collective-permute-start.13 = (f32[4,48,128]{2,1,0:T(8,128)S(1)}, f32[4,48,128]{2,1,0:T(8,128)S(1)}, u32[]{:S(2)}, u32[]{:S(2)}) collective-permute-start(f32[4,48,128]{2,1,0:T(8,128)S(1)} %select_bitcast_fusion.5), channel_id=1, source_target_pairs={{0,2},{1,3},{2,0},{3,1},{4,6},{5,7},{6,4},{7,5},{8,10},{9,11},{10,... | collective-permute-start | bytes 294920 | tf_op jit(solution)/shard_map/ppermute | solution.py:731
  154.3 7.4 %collective-permute-start.14 = (f32[2,48,128]{2,1,0:T(8,128)S(1)}, f32[2,48,128]{2,1,0:T(8,128)S(1)}, u32[]{:S(2)}, u32[]{:S(2)}) collective-permute-start(f32[2,48,128]{2,1,0:T(8,128)S(1)} %select_bitcast_fusion.8), channel_id=1, source_target_pairs={{0,4},{1,5},{2,6},{3,7},{4,0},{5,1},{6,2},{7,3},{8,12},{9,13},{10,... | collective-permute-start | bytes 147464 | tf_op jit(solution)/shard_map/ppermute | solution.py:731
  161.7 4.8 %collective-permute-start.15 = (f32[1,48,128]{2,1,0:T(8,128)S(1)}, f32[1,48,128]{2,1,0:T(8,128)S(1)}, u32[]{:S(2)}, u32[]{:S(2)}) collective-permute-start(f32[1,48,128]{2,1,0:T(8,128)S(1)} %select_bitcast_fusion.9), channel_id=1, source_target_pairs={{0,8},{1,9},{2,10},{3,11},{4,12},{5,13},{6,14},{7,15},{8,0},{9,1},... | collective-permute-start | bytes 73736 | tf_op jit(solution)/shard_map/ppermute | solution.py:731
  169.6 4.1 %collective-permute-start.16 = (f32[56,128]{1,0:T(8,128)}, f32[56,128]{1,0:T(8,128)S(1)}, u32[]{:S(2)}, u32[]{:S(2)}) collective-permute-start(f32[56,128]{1,0:T(8,128)} %get-tuple-element.96), channel_id=1, source_target_pairs={{0,16},{16,0},{1,17},{17,1},{2,18},{18,2},{3,19},{19,3},{4,20},{20... | collective-permute-start | bytes 86024 | tf_op jit(solution)/shard_map/ppermute | solution.py:977
  174.4 7.1 %collective-permute-start.18 = (f32[416,128]{1,0:T(8,128)}, f32[416,128]{1,0:T(8,128)S(1)}, u32[]{:S(2)}, u32[]{:S(2)}) collective-permute-start(f32[416,128]{1,0:T(8,128)} %get-tuple-element.100), channel_id=1, source_target_pairs={{0,16},{16,0},{1,17},{17,1},{2,18},{18,2},{3,19},{19,3},{4,20},{20... | collective-permute-start | bytes 638984 | tf_op jit(solution)/shard_map/ppermute | solution.py:977
  176.4 5.2 %collective-permute-start.17 = (f32[1,2,56,128]{3,2,1,0:T(8,128)S(1)}, f32[1,2,56,128]{3,2,1,0:T(8,128)S(1)}, u32[]{:S(2)}, u32[]{:S(2)}) collective-permute-start(f32[1,2,56,128]{3,2,1,0:T(8,128)S(1)} %bitcast.145), channel_id=1, source_target_pairs={{0,8},{1,9},{2,10},{3,11},{4,12},{5,13},{6,14},{7,15},{8,0},{9,1},... | collective-permute-start | bytes 172040 | tf_op jit(solution)/shard_map/ppermute | solution.py:731
  176.4 7.0 %collective-permute-start.20 = (f32[412,128]{1,0:T(8,128)}, f32[412,128]{1,0:T(8,128)S(1)}, u32[]{:S(2)}, u32[]{:S(2)}) collective-permute-start(f32[412,128]{1,0:T(8,128)} %get-tuple-element.102), channel_id=1, source_target_pairs={{0,16},{16,0},{1,17},{17,1},{2,18},{18,2},{3,19},{19,3},{4,20},{20... | collective-permute-start | bytes 632840 | tf_op jit(solution)/shard_map/ppermute | solution.py:977
  181.6 13.1 %copy-start.7 = (f32[416,128]{1,0:T(8,128)}, f32[416,128]{1,0:T(8,128)S(1)}, u32[]{:S(2)}) copy-start(f32[416,128]{1,0:T(8,128)S(1)} %collective-permute-done.18.refs_4_) | copy-start | bytes 638980
  181.6 4.9 %collective-permute-start.19 = (f32[2,2,56,128]{3,2,1,0:T(8,128)S(1)}, f32[2,2,56,128]{3,2,1,0:T(8,128)S(1)}, u32[]{:S(2)}, u32[]{:S(2)}) collective-permute-start(f32[2,2,56,128]{3,2,1,0:T(8,128)S(1)} %maximum_bitcast_fusion), channel_id=1, source_target_pairs={{0,4},{1,5},{2,6},{3,7},{4,0},{5,1},{6,2},{7,3},{8,12},{9,13},{10,... | collective-permute-start | bytes 344072 | tf_op jit(solution)/shard_map/ppermute | solution.py:731
  183.4 11.2 %copy-start.8 = (f32[412,128]{1,0:T(8,128)}, f32[412,128]{1,0:T(8,128)S(1)}, u32[]{:S(2)}) copy-start(f32[412,128]{1,0:T(8,128)S(1)} %collective-permute-done.20.refs_5_) | copy-start | bytes 632836
  186.5 6.1 %collective-permute-start.21 = (f32[4,2,56,128]{3,2,1,0:T(8,128)S(1)}, f32[4,2,56,128]{3,2,1,0:T(8,128)S(1)}, u32[]{:S(2)}, u32[]{:S(2)}) collective-permute-start(f32[4,2,56,128]{3,2,1,0:T(8,128)S(1)} %bitcast.141), channel_id=1, source_target_pairs={{0,2},{1,3},{2,0},{3,1},{4,6},{5,7},{6,4},{7,5},{8,10},{9,11},{10,... | collective-permute-start | bytes 688136 | tf_op jit(solution)/shard_map/ppermute | solution.py:731
  192.7 1.9 copy-start
  192.7 1.9 collective-permute-start.22
  194.6 0.8 copy-start.3
Sparse Core Ops, SparseCore 0:
  10.8 50.0 all-gather.1
  76.6 89.4 reduce-scatter.1

commit v6 on v5

--- a/solution.py
+++ b/solution.py
@@ -531,15 +531,7 @@
             d3_ref[p] = jnp.zeros((8, C3, 256), BF16)
 
     for p in (0, 10):
-        d2_ref[p] = jnp.zeros((11, C2, 256), BF16)
-
-    def edge(p, carry):
-        d2_ref[p, 0] = jnp.zeros((C2, 256), BF16)
-        d2_ref[p, 10] = jnp.zeros((C2, 256), BF16)
-        return carry
-
-    lax.fori_loop(1, 10, edge, 0)
-
+        d2_ref[p, 1:10] = jnp.zeros((9, C2, 256), BF16)
     zero = jnp.zeros((), BF16)
     for p in range(7):
         back = mm(wd_ref[448 * p : 448 * p + 448], d_hidden_ref[...]).reshape(7, C3, 256)
@@ -731,6 +723,10 @@
     return lax.ppermute(value, "dp", [(i, i ^ step) for i in range(lanes)])
 
 
+def other_group(value):
+    return lax.ppermute(value, "group", [(0, 1), (1, 0)])
+
+
 def halving_order(lanes):
     return [1 << k for k in range(lanes.bit_length() - 1)]
 
@@ -752,12 +748,18 @@
 
 
 def gather_blocks(block, beside, lanes, place):
-    blocks = block[None]
     arrived = []
     for k, step in enumerate(reversed(halving_order(lanes))):
-        other = swap(blocks, lanes, step)
-        if k < len(beside):
-            other, part = lax.optimization_barrier((other, beside[k]))
+        if k == 0:
+            both = [(i, (i ^ step) ^ lanes) for i in range(2 * lanes)]
+            blocks = jnp.stack([block, other_group(block)])[None]
+            other = jnp.stack(
+                [swap(block, lanes, step), lax.ppermute(block, ("group", "dp"), both)]
+            )[None]
+        else:
+            other = swap(blocks, lanes, step)
+        if 0 < k <= len(beside):
+            other, part = lax.optimization_barrier((other, beside[k - 1]))
             arrived.append(part)
         if step == 1:
             return blocks, other, arrived
@@ -973,9 +975,6 @@
     groups = lax.axis_size("group")
     assert groups == 2 and rows * HID == shard_len and frames.shape[2] == 128
 
-    def other_group(value):
-        return lax.ppermute(value, "group", [(0, 1), (1, 0)])
-
     master_rows = master.reshape(rows, HID)
     low_rows = master_rows.astype(BF16)
     gathered = lax.all_gather(low_rows, "dp", axis=0)
@@ -987,6 +986,11 @@
     batch = envs_here * steps_here
     total_frames = batch * lanes
     block, sums, left = first_rows_everywhere(master, sums, lanes, place)
+    moment_step = step_count[0].astype(F32)
+    scalars = jnp.stack(
+        [1.0 - jnp.power(BETA_ONE, moment_step), 1.0 - jnp.power(BETA_TWO, moment_step)]
+    )
+    block, scalars = lax.optimization_barrier((block, scalars))
     while len(left) > 2:
         sums = sums + swap(sums, lanes, left.pop(0))
     x = frames[0].transpose(0, 2, 3, 1)
@@ -1042,17 +1046,11 @@
     small = jnp.concatenate([lower + upper, head_part], axis=0)
     piece = scatter_sum(small.reshape(lanes, count // lanes, 128), lanes, place)
     message, dense_parts = facts_message(dense_owned, piece, loss_local)
-    both = jnp.stack([message, other_group(message)])
-    both, *dense_parts = lax.optimization_barrier((both, *dense_parts))
     near, far, dense_parts = gather_blocks(
-        both, [other_group(part) for part in dense_parts], lanes, place
+        message, [other_group(part) for part in dense_parts], lanes, place
     )
 
     own_len = 4 * rows
-    moment_step = step_count[0].astype(F32)
-    scalars = jnp.stack(
-        [1.0 - jnp.power(BETA_ONE, moment_step), 1.0 - jnp.power(BETA_TWO, moment_step)]
-    )
     parts = ((0, 4 * (TOP + 1), 0), (4 * BLOCK_ROWS, real, 4 * tail))
 
     def view(value):

time: 209 us -> 206 us (0.986)
  waiting for transfers between devices: 40.6 us -> 35.3 us
  starting transfers between devices: 28.9 us -> 31.5 us
    ppermute x12, waiting for transfers between devices: 35.9 us -> 27.3 us  [swap(): return lax.ppermute(value, 'dp', [(i, i ^ step) for i in range(lanes)])]
    ppermute x12, starting transfers between devices: 8.74 us -> 11.3 us  [swap(): return lax.ppermute(value, 'dp', [(i, i ^ step) for i in range(lanes)])]
  transfers between devices with their start and end apart: 25 -> 26, of which waited for: 14 -> 12; matrix products, arithmetic and copies ran while one was open for 4% -> 4% of each run, Pallas kernels for 44% -> 44%
where the time goes in v6:
time: 206 us; the launch traced here: 205 us
  Pallas kernels  110 us (53%)
  waiting for transfers between devices  35.3 us (17%)
  starting transfers between devices  31.5 us (15%)
  between operations  15.3 us (7%)
  other arithmetic  8.67 us (4%)
  local copies, waits for them, and re-layouts  4.29 us (2%)
    pallas_call x1, Pallas kernels, lower_backward(): pl.pallas_call(lower_body, grid=(envs // 2, 5), in_specs=pixel_specs() +...  36.5 us
    ppermute x12, waiting for transfers between devices, swap(): return lax.ppermute(value, 'dp', [(i, i ^ step) for i in range(lanes)])  27.3 us
    pallas_call x1, Pallas kernels, upper_backward(): pl.pallas_call(upper_body, grid=(frames // 256,), in_specs=[pl.BlockSpec(...  26.9 us
    pallas_call x1, Pallas kernels, conv_forward(): pl.pallas_call(forward_body, grid=(envs // 2,), in_specs=[pl.BlockSpec(me...  23.2 us
    ppermute x6, starting transfers between devices, first_rows_everywhere(): total = total + lax.ppermute(block, 'dp', pairs)  13.5 us
    ppermute x12, starting transfers between devices, swap(): return lax.ppermute(value, 'dp', [(i, i ^ step) for i in range(lanes)])  11.3 us
    pallas_call x1, Pallas kernels, dense_step(): pl.pallas_call(lambda *refs: dense_body(scale, *refs), in_specs=[away, aw...  10.9 us
    ppermute x5, starting transfers between devices, other_group(): return lax.ppermute(value, 'group', [(0, 1), (1, 0)])  6.2 us
  transfers between devices with their start and end apart: 26, of which 12 were waited for; matrix products, arithmetic and copies ran while one was open for 4% of the time, Pallas kernels for 44%

profile of v6, /device:TPU:0, one launch (start us, length us, event | category | flops | bytes accessed | tf_op | source)
XLA Modules:
  0.0 205.0 jit_solution(10175840144616976631)
XLA Ops:
  7.2 1.0 convert.3
  8.3 0.8 convert_element_type.25
  9.4 7.0 %collective-permute-start.2 = (bf16[168,512]{1,0:T(8,128)(2,1)S(1)}, bf16[168,512]{1,0:T(8,128)(2,1)S(1)}, u32[]{:S(2)}, u32[]{:S(2)}) collective-permute-start(bf16[168,512]{1,0:T(8,128)(2,1)S(1)} %broadcast_select_fusion), channel_id=1, source_target_pairs={{0,12},{16,28}} | collective-permute-start | bytes 516104 | tf_op jit(solution)/shard_map/ppermute | solution.py:788
  16.4 1.3 collective-permute-start.1
  17.7 1.3 collective-permute-start
  19.0 2.0 advantages.1
  21.0 1.4 collective-permute-done.3
  22.4 0.7 add.74
  23.1 1.4 collective-permute-done
  24.6 1.3 collective-permute-start.6
  25.9 1.3 collective-permute-start.5
  27.2 1.3 collective-permute-start.4
  29.3 2.9 %collective-permute-done.7 = f32[8,128]{1,0:T(8,128)S(1)} collective-permute-done((f32[8,128]{1,0:T(8,128)S(1)}, f32[8,128]{1,0:T(8,128)S(1)}, u32[]{:S(2)}, u32[]{:S(2)}) %collective-permute-start.7) | collective-permute-done | bytes 4128 | tf_op jit(solution)/shard_map/ppermute | solution.py:723
  32.2 0.7 add_add_fusion.conv_ref
  33.5 2.3 %conv_weights.1 = (bf16[128,192]{1,0:T(8,128)(2,1)}, f32[64,256]{1,0:T(8,128)}, bf16[128,256]{1,0:T(8,128)(2,1)}, f32[64,256]{1,0:T(8,128)}, bf16[192,192]{1,0:T...) custom-call(bf16[168,512]{1,0:T(8,128)(2,1)} %add_add_fusion.conv_ref), custom_call_target="tpu_custom_call" | custom-call | tf_op jit(solution)/shard_map/conv_weights/pallas_call | solution.py:175
  35.8 0.8 collective-permute-done.8
  36.6 3.3 %collective-permute-start.9 = (f32[8,128]{1,0:T(8,128)S(1)}, f32[8,128]{1,0:T(8,128)S(1)}, u32[]{:S(2)}, u32[]{:S(2)}) collective-permute-start(f32[8,128]{1,0:T(8,128)S(1)} %add.82), channel_id=1, source_target_pairs={{0,8},{1,9},{2,10},{3,11},{4,12},{5,13},{6,14},{7,15},{8,0},{9,1},... | collective-permute-start | bytes 12296 | tf_op jit(solution)/shard_map/ppermute | solution.py:723
  39.9 23.2 %conv_forward.1 = (bf16[20,20,32,512]{3,2,1,0:T(8,128)(2,1)}, bf16[9,10,64,512]{3,2,1,0:T(8,128)(2,1)}, bf16[7,7,64,512]{3,2,1,0:T(8,128)(2,1)}) custom-call(bf16[4,84,336,128]{3,2,1,0:T(8,128)(2,1)} %bitcast.118, bf16[128,192]{1,0:T(8,128)(2,1)} %get-tuple-element.70.t1_ref, f32[64,256]{1,0:T(8,128)} %get-tuple-element.71.b1_ref, ...), custom_call_target="tpu_custom_call" | custom-call | tf_op jit(solution)/shard_map/conv_forward/pallas_call | solution.py:292
  63.7 0.7 slice.83
  64.9 0.7 pad.8.refs_2_
  65.6 10.9 %dense_step.1 = (f32[16,828,128]{2,1,0:T(8,128)}, bf16[3136,512]{1,0:T(8,128)(2,1)}, bf16[512,512]{1,0:T(8,128)(2,1)}, f32[32,512]{1,0:T(8,128)}, f32[32,1]{1,0:T(8,128)}, /*index=5*/f32[1,1]{1,0:T(1,128)}) custom-call(bf16[3136,512]{1,0:T(8,128)(2,1)} %bitcast.124, bf16[16,207,512]{2,1,0:T(8,128)(2,1)} %all-gather.2.cloned.1.call-done.refs_1_, ...), custom_call_target="tpu_custom_call" | custom-call | tf_op jit(solution)/shard_map/dense_step/pallas_call | solution.py:465
  76.5 1.0 reduce
  77.5 0.9 collective-permute-start.10
  78.4 1.0 reduce.1
  79.4 1.3 collective-permute-start.11
  81.5 26.9 %upper_backward.1 = (bf16[11,11,64,512]{3,2,1,0:T(8,128)(2,1)}, f32[672,128]{1,0:T(8,128)}) custom-call(bf16[20,20,32,512]{3,2,1,0:T(8,128)(2,1)} %get-tuple-element.82.a1_hbm.a1_ref, bf16[9,10,64,512]{3,2,1,0:T(8,128)(2,1)} %get-tuple-element.83.a2_ref, bf16[7,7,64,512]{3,2,1,0:T(8,128)(2,1)} %get-tuple-element.78.a3_ref, ...), custom_call_target="tpu_custom_call" | custom-call | tf_op jit(solution)/shard_map/upper_backward/pallas_call | solution.py:613
  108.5 36.5 %lower_backward.1 = f32[672,128]{1,0:T(8,128)} custom-call(bf16[4,84,336,128]{3,2,1,0:T(8,128)(2,1)} %bitcast.119, bf16[4,84,336,128]{3,2,1,0:T(8,128)(2,1)} %bitcast.120, bf16[4,84,336,128]{3,2,1,0:T(8,128)(2,1)} %bitcast.121, bf16[4,84,336,128]{3,2,1,0:T(8,128)(2,1)} %bitcast.122, bf16[4,84,336,128]{3,2,1,0:T(8,128)(2,1)} %bitcast.123, ...), custom_call_target="tpu_custom_call" | custom-call | tf_op jit(solution)/shard_map/lower_backward/pallas_call | solution.py:701
  145.0 1.1 add.85
  146.2 1.4 collective-permute-done.12
  147.7 2.1 %collective-permute-start.13 = (f32[4,48,128]{2,1,0:T(8,128)S(1)}, f32[4,48,128]{2,1,0:T(8,128)S(1)}, u32[]{:S(2)}, u32[]{:S(2)}) collective-permute-start(f32[4,48,128]{2,1,0:T(8,128)S(1)} %select_bitcast_fusion.5), channel_id=1, source_target_pairs={{0,2},{1,3},{2,0},{3,1},{4,6},{5,7},{6,4},{7,5},{8,10},{9,11},{10,... | collective-permute-start | bytes 294920 | tf_op jit(solution)/shard_map/ppermute | solution.py:723
  149.8 4.7 %collective-permute-done.13 = f32[4,48,128]{2,1,0:T(8,128)S(1)} collective-permute-done((f32[4,48,128]{2,1,0:T(8,128)S(1)}, f32[4,48,128]{2,1,0:T(8,128)S(1)}, u32[]{:S(2)}, u32[]{:S(2)}) %collective-permute-start.13) | collective-permute-done | bytes 98336 | tf_op jit(solution)/shard_map/ppermute | solution.py:723
  154.5 1.6 collective-permute-start.14
  156.0 5.7 %collective-permute-done.14 = f32[2,48,128]{2,1,0:T(8,128)S(1)} collective-permute-done((f32[2,48,128]{2,1,0:T(8,128)S(1)}, f32[2,48,128]{2,1,0:T(8,128)S(1)}, u32[]{:S(2)}, u32[]{:S(2)}) %collective-permute-start.14) | collective-permute-done | bytes 49184 | tf_op jit(solution)/shard_map/ppermute | solution.py:723
  161.8 4.7 %collective-permute-done.15 = f32[1,48,128]{2,1,0:T(8,128)S(1)} collective-permute-done((f32[1,48,128]{2,1,0:T(8,128)S(1)}, f32[1,48,128]{2,1,0:T(8,128)S(1)}, u32[]{:S(2)}, u32[]{:S(2)}) %collective-permute-start.15) | collective-permute-done | bytes 24608 | tf_op jit(solution)/shard_map/ppermute | solution.py:723
  167.2 2.5 %facts_message.1 = (f32[56,128]{1,0:T(8,128)}, f32[416,128]{1,0:T(8,128)}, f32[412,128]{1,0:T(8,128)}) custom-call(f32[828,128]{1,0:T(8,128)} %bitcast.132, f32[48,128]{1,0:T(8,128)} %fusion.5.piece_ref, f32[1,1]{1,0:T(1,128)} %get-tuple-element.96.loss_ref), custom_call_target="tpu_custom_call" | custom-call | tf_op jit(solution)/shard_map/facts_message/pallas_call | solution.py:826
  169.6 1.5 collective-permute-start.18
  171.6 2.4 %collective-permute-start.16 = (f32[56,128]{1,0:T(8,128)}, f32[56,128]{1,0:T(8,128)S(1)}, u32[]{:S(2)}, u32[]{:S(2)}) collective-permute-start(f32[56,128]{1,0:T(8,128)} %get-tuple-element.97), channel_id=1, source_target_pairs={{0,8},{1,9},{2,10},{3,11},{4,12},{5,13},{6,14},{7,15},{8,0},{9,1},... | collective-permute-start | bytes 86024 | tf_op jit(solution)/shard_map/ppermute | solution.py:723
  174.0 1.5 collective-permute-start.20
  175.6 1.5 collective-permute-done.17
  177.1 0.8 fusion.4
  177.8 0.8 collective-permute-start.19
  178.7 4.0 %collective-permute-done.19 = f32[2,2,56,128]{3,2,1,0:T(8,128)S(1)} collective-permute-done((f32[2,2,56,128]{3,2,1,0:T(8,128)S(1)}, f32[2,2,56,128]{3,2,1,0:T(8,128)S(1)}, u32[]{:S(2)}, u32[]{:S(2)}) %collective-permute-start.19) | collective-permute-done | bytes 114720 | tf_op jit(solution)/shard_map/ppermute | solution.py:723
  182.8 0.8 collective-permute-start.21
  183.6 1.0 collective-permute-start.22
  184.5 5.1 %collective-permute-done.22.refs_5_ = f32[412,128]{1,0:T(8,128)S(1)} collective-permute-done((f32[412,128]{1,0:T(8,128)}, f32[412,128]{1,0:T(8,128)S(1)}, u32[]{:S(2)}, u32[]{:S(2)}) %collective-permute-start.22) | collective-permute-done | bytes 210976 | tf_op jit(solution)/shard_map/ppermute | solution.py:727
  189.8 1.8 collective-permute-done.23.refs_3_
  191.6 0.8 copy-done.3
  192.4 5.7 %finish.1 = (f32[828,1,128]{2,1,0:T(1,128)}, f32[828,1,128]{2,1,0:T(1,128)}, f32[828,1,128]{2,1,0:T(1,128)}, f32[828,128]{1,0:T(8,128)}, f32[828,128]{1,0:T(8,12...) custom-call(s32[1]{0:T(128)} %bitcast.refs_0_, ...), custom_call_target="tpu_custom_call" | custom-call | tf_op jit(solution)/shard_map/finish/pallas_call | solution.py:940
  (84 shorter events, 4.5 us)
Async XLA Ops:
  7.2 56.6 %all-gather.2.cloned.1.call-start = ((), (), s32[]{:S(2)}) async-start(), calls=%async_computation.1 | async-start | bytes 3620864 | tf_op jit(solution)/shard_map/all_gather | solution.py:980
  9.1 158.0 %reduce-scatter.2.cloned.1.call-start = ((), (), s32[]{:S(2)}) async-start(), calls=%async_computation.2 | async-start | bytes 7241728 | tf_op jit(solution)/shard_map/reduce_scatter | solution.py:1022
  9.4 13.7 %collective-permute-start.2 = (bf16[168,512]{1,0:T(8,128)(2,1)S(1)}, bf16[168,512]{1,0:T(8,128)(2,1)S(1)}, u32[]{:S(2)}, u32[]{:S(2)}) collective-permute-start(bf16[168,512]{1,0:T(8,128)(2,1)S(1)} %broadcast_select_fusion), channel_id=1, source_target_pairs={{0,12},{16,28}} | collective-permute-start | bytes 516104 | tf_op jit(solution)/shard_map/ppermute | solution.py:788
  16.4 6.7 %collective-permute-start.1 = (bf16[168,512]{1,0:T(8,128)(2,1)S(1)}, bf16[168,512]{1,0:T(8,128)(2,1)S(1)}, u32[]{:S(2)}, u32[]{:S(2)}) collective-permute-start(bf16[168,512]{1,0:T(8,128)(2,1)S(1)} %broadcast_select_fusion), channel_id=1, source_target_pairs={{0,4},{16,20}} | collective-permute-start | bytes 516104 | tf_op jit(solution)/shard_map/ppermute | solution.py:788
  17.7 6.7 %collective-permute-start = (bf16[168,512]{1,0:T(8,128)(2,1)S(1)}, bf16[168,512]{1,0:T(8,128)(2,1)S(1)}, u32[]{:S(2)}, u32[]{:S(2)}) collective-permute-start(bf16[168,512]{1,0:T(8,128)(2,1)S(1)} %broadcast_select_fusion), channel_id=1, source_target_pairs={{0,8},{16,24}} | collective-permute-start | bytes 516104 | tf_op jit(solution)/shard_map/ppermute | solution.py:788
  21.0 1.4 collective-permute-start.3
  24.6 7.6 %collective-permute-start.6 = (bf16[168,512]{1,0:T(8,128)(2,1)S(1)}, bf16[168,512]{1,0:T(8,128)(2,1)S(1)}, u32[]{:S(2)}, u32[]{:S(2)}) collective-permute-start(bf16[168,512]{1,0:T(8,128)(2,1)S(1)} %add_add_fusion.1), channel_id=1, source_target_pairs={{0,3},{4,7},{8,11},{12,15},{16,19},{20,23},{24,27},{28,31}} | collective-permute-start | bytes 516104 | tf_op jit(solution)/shard_map/ppermute | solution.py:788
  25.9 6.3 %collective-permute-start.5 = (bf16[168,512]{1,0:T(8,128)(2,1)S(1)}, bf16[168,512]{1,0:T(8,128)(2,1)S(1)}, u32[]{:S(2)}, u32[]{:S(2)}) collective-permute-start(bf16[168,512]{1,0:T(8,128)(2,1)S(1)} %add_add_fusion.1), channel_id=1, source_target_pairs={{0,1},{4,5},{8,9},{12,13},{16,17},{20,21},{24,25},{28,29}} | collective-permute-start | bytes 516104 | tf_op jit(solution)/shard_map/ppermute | solution.py:788
  27.2 5.0 %collective-permute-start.4 = (bf16[168,512]{1,0:T(8,128)(2,1)S(1)}, bf16[168,512]{1,0:T(8,128)(2,1)S(1)}, u32[]{:S(2)}, u32[]{:S(2)}) collective-permute-start(bf16[168,512]{1,0:T(8,128)(2,1)S(1)} %add_add_fusion.1), channel_id=1, source_target_pairs={{0,2},{4,6},{8,10},{12,14},{16,18},{20,22},{24,26},{28,30}} | collective-permute-start | bytes 516104 | tf_op jit(solution)/shard_map/ppermute | solution.py:788
  28.5 3.7 %collective-permute-start.7 = (f32[8,128]{1,0:T(8,128)S(1)}, f32[8,128]{1,0:T(8,128)S(1)}, u32[]{:S(2)}, u32[]{:S(2)}) collective-permute-start(f32[8,128]{1,0:T(8,128)S(1)} %add.74), channel_id=1, source_target_pairs={{0,2},{1,3},{2,0},{3,1},{4,6},{5,7},{6,4},{7,5},{8,10},{9,11},{10,... | collective-permute-start | bytes 12296 | tf_op jit(solution)/shard_map/ppermute | solution.py:723
  32.9 3.6 %collective-permute-start.8 = (f32[8,128]{1,0:T(8,128)S(1)}, f32[8,128]{1,0:T(8,128)S(1)}, u32[]{:S(2)}, u32[]{:S(2)}) collective-permute-start(f32[8,128]{1,0:T(8,128)S(1)} %add.78), channel_id=1, source_target_pairs={{0,4},{1,5},{2,6},{3,7},{4,0},{5,1},{6,2},{7,3},{8,12},{9,13},{10,... | collective-permute-start | bytes 12296 | tf_op jit(solution)/shard_map/ppermute | solution.py:723
  36.6 26.6 %collective-permute-start.9 = (f32[8,128]{1,0:T(8,128)S(1)}, f32[8,128]{1,0:T(8,128)S(1)}, u32[]{:S(2)}, u32[]{:S(2)}) collective-permute-start(f32[8,128]{1,0:T(8,128)S(1)} %add.82), channel_id=1, source_target_pairs={{0,8},{1,9},{2,10},{3,11},{4,12},{5,13},{6,14},{7,15},{8,0},{9,1},... | collective-permute-start | bytes 12296 | tf_op jit(solution)/shard_map/ppermute | solution.py:723
  65.6 10.9 %copy-start.4 = (f32[1,105984]{1,0:T(1,128)S(1)}, f32[1,105984]{1,0:T(1,128)}, u32[]{:S(2)}) copy-start(f32[1,105984]{1,0:T(1,128)} %param.22) | copy-start | bytes 1271812
  76.4 2.0 copy-start.5
  76.4 4.3 %copy-start.9 = (f32[32,512]{1,0:T(8,128)S(1)}, f32[32,512]{1,0:T(8,128)}, u32[]{:S(2)}) copy-start(f32[32,512]{1,0:T(8,128)} %get-tuple-element.94) | copy-start | bytes 196612
  76.4 4.8 %copy-start.10 = (f32[32,1]{1,0:T(8,128)S(1)}, f32[32,1]{1,0:T(8,128)}, u32[]{:S(2)}) copy-start(f32[32,1]{1,0:T(8,128)} %get-tuple-element.95) | copy-start | bytes 388
  77.5 30.9 %copy-start.1 = (f32[105984]{0:T(1024)}, f32[105984]{0:T(1024)S(1)}, u32[]{:S(2)}) copy-start(f32[105984]{0:T(1024)S(1)} %reduce) | copy-start | bytes 1271812
  77.5 30.9 %collective-permute-start.10 = (f32[105984]{0:T(1024)S(1)}, f32[105984]{0:T(1024)}, u32[]{:S(2)}, u32[]{:S(2)}) collective-permute-start(f32[105984]{0:T(1024)S(1)} %reduce), channel_id=1, source_target_pairs={{0,16},{16,0},{1,17},{17,1},{2,18},{18,2},{3,19},{19,3},{4,20},{20... | collective-permute-start | bytes 1271816 | tf_op jit(solution)/shard_map/ppermute | solution.py:727
  79.4 29.0 %copy-start.2 = (f32[105984]{0:T(1024)}, f32[105984]{0:T(1024)S(1)}, u32[]{:S(2)}) copy-start(f32[105984]{0:T(1024)S(1)} %reduce.1) | copy-start | bytes 1271812
  79.4 29.0 %collective-permute-start.11 = (f32[105984]{0:T(1024)S(1)}, f32[105984]{0:T(1024)}, u32[]{:S(2)}, u32[]{:S(2)}) collective-permute-start(f32[105984]{0:T(1024)S(1)} %reduce.1), channel_id=1, source_target_pairs={{0,16},{16,0},{1,17},{17,1},{2,18},{18,2},{3,19},{19,3},{4,20},{20... | collective-permute-start | bytes 1271816 | tf_op jit(solution)/shard_map/ppermute | solution.py:727
  108.5 36.5 %copy-start.6 = (f32[672,128]{1,0:T(8,128)S(1)}, f32[672,128]{1,0:T(8,128)}, u32[]{:S(2)}) copy-start(f32[672,128]{1,0:T(8,128)} %get-tuple-element.93) | copy-start | bytes 1032196
  146.1 1.5 collective-permute-start.12
  147.7 6.7 %collective-permute-start.13 = (f32[4,48,128]{2,1,0:T(8,128)S(1)}, f32[4,48,128]{2,1,0:T(8,128)S(1)}, u32[]{:S(2)}, u32[]{:S(2)}) collective-permute-start(f32[4,48,128]{2,1,0:T(8,128)S(1)} %select_bitcast_fusion.5), channel_id=1, source_target_pairs={{0,2},{1,3},{2,0},{3,1},{4,6},{5,7},{6,4},{7,5},{8,10},{9,11},{10,... | collective-permute-start | bytes 294920 | tf_op jit(solution)/shard_map/ppermute | solution.py:723
  154.5 7.2 %collective-permute-start.14 = (f32[2,48,128]{2,1,0:T(8,128)S(1)}, f32[2,48,128]{2,1,0:T(8,128)S(1)}, u32[]{:S(2)}, u32[]{:S(2)}) collective-permute-start(f32[2,48,128]{2,1,0:T(8,128)S(1)} %select_bitcast_fusion.6), channel_id=1, source_target_pairs={{0,4},{1,5},{2,6},{3,7},{4,0},{5,1},{6,2},{7,3},{8,12},{9,13},{10,... | collective-permute-start | bytes 147464 | tf_op jit(solution)/shard_map/ppermute | solution.py:723
  161.7 4.8 %collective-permute-start.15 = (f32[1,48,128]{2,1,0:T(8,128)S(1)}, f32[1,48,128]{2,1,0:T(8,128)S(1)}, u32[]{:S(2)}, u32[]{:S(2)}) collective-permute-start(f32[1,48,128]{2,1,0:T(8,128)S(1)} %select_bitcast_fusion.7), channel_id=1, source_target_pairs={{0,8},{1,9},{2,10},{3,11},{4,12},{5,13},{6,14},{7,15},{8,0},{9,1},... | collective-permute-start | bytes 73736 | tf_op jit(solution)/shard_map/ppermute | solution.py:723
  169.6 5.9 %collective-permute-start.18 = (f32[56,128]{1,0:T(8,128)}, f32[56,128]{1,0:T(8,128)S(1)}, u32[]{:S(2)}, u32[]{:S(2)}) collective-permute-start(f32[56,128]{1,0:T(8,128)} %get-tuple-element.97), channel_id=1, source_target_pairs={{0,16},{16,0},{1,17},{17,1},{2,18},{18,2},{3,19},{19,3},{4,20},{20... | collective-permute-start | bytes 86024 | tf_op jit(solution)/shard_map/ppermute | solution.py:727
  171.2 5.9 %collective-permute-start.17 = (f32[56,128]{1,0:T(8,128)}, f32[56,128]{1,0:T(8,128)S(1)}, u32[]{:S(2)}, u32[]{:S(2)}) collective-permute-start(f32[56,128]{1,0:T(8,128)} %get-tuple-element.97), channel_id=1, source_target_pairs={{0,24},{1,25},{2,26},{3,27},{4,28},{5,29},{6,30},{7,31},{8,16},{9,... | collective-permute-start | bytes 86024 | tf_op jit(solution)/shard_map/ppermute | solution.py:757
  171.6 5.4 %collective-permute-start.16 = (f32[56,128]{1,0:T(8,128)}, f32[56,128]{1,0:T(8,128)S(1)}, u32[]{:S(2)}, u32[]{:S(2)}) collective-permute-start(f32[56,128]{1,0:T(8,128)} %get-tuple-element.97), channel_id=1, source_target_pairs={{0,8},{1,9},{2,10},{3,11},{4,12},{5,13},{6,14},{7,15},{8,0},{9,1},... | collective-permute-start | bytes 86024 | tf_op jit(solution)/shard_map/ppermute | solution.py:723
  174.0 8.7 %collective-permute-start.20 = (f32[416,128]{1,0:T(8,128)}, f32[416,128]{1,0:T(8,128)S(1)}, u32[]{:S(2)}, u32[]{:S(2)}) collective-permute-start(f32[416,128]{1,0:T(8,128)} %get-tuple-element.98), channel_id=1, source_target_pairs={{0,16},{16,0},{1,17},{17,1},{2,18},{18,2},{3,19},{19,3},{4,20},{20... | collective-permute-start | bytes 638984 | tf_op jit(solution)/shard_map/ppermute | solution.py:727
  177.8 4.9 %collective-permute-start.19 = (f32[2,2,56,128]{3,2,1,0:T(8,128)S(1)}, f32[2,2,56,128]{3,2,1,0:T(8,128)S(1)}, u32[]{:S(2)}, u32[]{:S(2)}) collective-permute-start(f32[2,2,56,128]{3,2,1,0:T(8,128)S(1)} %maximum_bitcast_fusion), channel_id=1, source_target_pairs={{0,4},{1,5},{2,6},{3,7},{4,0},{5,1},{6,2},{7,3},{8,12},{9,13},{10,... | collective-permute-start | bytes 344072 | tf_op jit(solution)/shard_map/ppermute | solution.py:723
  182.7 8.9 %copy-start.7 = (f32[416,128]{1,0:T(8,128)}, f32[416,128]{1,0:T(8,128)S(1)}, u32[]{:S(2)}) copy-start(f32[416,128]{1,0:T(8,128)S(1)} %collective-permute-done.20.refs_4_) | copy-start | bytes 638980
  182.8 6.8 %collective-permute-start.21 = (f32[4,2,56,128]{3,2,1,0:T(8,128)S(1)}, f32[4,2,56,128]{3,2,1,0:T(8,128)S(1)}, u32[]{:S(2)}, u32[]{:S(2)}) collective-permute-start(f32[4,2,56,128]{3,2,1,0:T(8,128)S(1)} %bitcast.136), channel_id=1, source_target_pairs={{0,2},{1,3},{2,0},{3,1},{4,6},{5,7},{6,4},{7,5},{8,10},{9,11},{10,... | collective-permute-start | bytes 688136 | tf_op jit(solution)/shard_map/ppermute | solution.py:723
  183.6 6.1 %collective-permute-start.22 = (f32[412,128]{1,0:T(8,128)}, f32[412,128]{1,0:T(8,128)S(1)}, u32[]{:S(2)}, u32[]{:S(2)}) collective-permute-start(f32[412,128]{1,0:T(8,128)} %get-tuple-element.100), channel_id=1, source_target_pairs={{0,16},{16,0},{1,17},{17,1},{2,18},{18,2},{3,19},{19,3},{4,20},{20... | collective-permute-start | bytes 632840 | tf_op jit(solution)/shard_map/ppermute | solution.py:727
  189.6 2.0 copy-start.8
  189.7 1.9 copy-start
  189.7 1.9 collective-permute-start.23
  191.6 0.8 copy-start.3
Sparse Core Ops, SparseCore 0:
  10.8 50.0 all-gather.1
  76.6 89.2 reduce-scatter.1

commit v7 on v6

--- a/solution.py
+++ b/solution.py
@@ -778,7 +778,7 @@
         row = lax.broadcasted_iota(jnp.int32, (BLOCK_ROWS, 1), 0)
         block = jnp.where((place == 0) & (row <= TOP), block, jnp.zeros((), BF16))
         steps = list(reversed(order))
-        left = list(order)
+        left = order[1:2] + list(reversed(order[2:])) + order[:1]
         while steps:
             now, steps = steps[:2], steps[2:]
             jumps = now if len(now) == 1 else [now[0], now[1], now[0] + now[1]]

time: 206 us -> 206 us (level)
  transfers between devices with their start and end apart: 26 -> 26, of which waited for: 12 -> 11; matrix products, arithmetic and copies ran while one was open for 4% -> 4% of each run, Pallas kernels for 44% -> 44%
where the time goes in v7:
time: 206 us; the launch traced here: 205 us
  Pallas kernels  110 us (53%)
  waiting for transfers between devices  36.6 us (18%)
  starting transfers between devices  30.6 us (15%)
  between operations  15.3 us (7%)
  other arithmetic  8.59 us (4%)
  local copies, waits for them, and re-layouts  4.29 us (2%)
    pallas_call x1, Pallas kernels, lower_backward(): pl.pallas_call(lower_body, grid=(envs // 2, 5), in_specs=pixel_specs() +...  36.4 us
    ppermute x12, waiting for transfers between devices, swap(): return lax.ppermute(value, 'dp', [(i, i ^ step) for i in range(lanes)])  28.9 us
    pallas_call x1, Pallas kernels, upper_backward(): pl.pallas_call(upper_body, grid=(frames // 256,), in_specs=[pl.BlockSpec(...  26.9 us
    pallas_call x1, Pallas kernels, conv_forward(): pl.pallas_call(forward_body, grid=(envs // 2,), in_specs=[pl.BlockSpec(me...  23.5 us
    ppermute x6, starting transfers between devices, first_rows_everywhere(): total = total + lax.ppermute(block, 'dp', pairs)  13.5 us
    ppermute x12, starting transfers between devices, swap(): return lax.ppermute(value, 'dp', [(i, i ^ step) for i in range(lanes)])  11.6 us
    pallas_call x1, Pallas kernels, dense_step(): pl.pallas_call(lambda *refs: dense_body(scale, *refs), in_specs=[away, aw...  10.9 us
    ppermute x5, waiting for transfers between devices, other_group(): return lax.ppermute(value, 'group', [(0, 1), (1, 0)])  5.87 us
  transfers between devices with their start and end apart: 26, of which 11 were waited for; matrix products, arithmetic and copies ran while one was open for 4% of the time, Pallas kernels for 44%

profile of v7, /device:TPU:0, one launch (start us, length us, event | category | flops | bytes accessed | tf_op | source)
XLA Modules:
  0.0 205.5 jit_solution(9655433262226745381)
XLA Ops:
  7.2 1.0 convert.3
  8.3 0.8 convert_element_type.25
  9.4 7.0 %collective-permute-start.2 = (bf16[168,512]{1,0:T(8,128)(2,1)S(1)}, bf16[168,512]{1,0:T(8,128)(2,1)S(1)}, u32[]{:S(2)}, u32[]{:S(2)}) collective-permute-start(bf16[168,512]{1,0:T(8,128)(2,1)S(1)} %broadcast_select_fusion), channel_id=1, source_target_pairs={{0,12},{16,28}} | collective-permute-start | bytes 516104 | tf_op jit(solution)/shard_map/ppermute | solution.py:788
  16.4 1.3 collective-permute-start.1
  17.7 1.3 collective-permute-start
  19.0 2.0 advantages.1
  21.0 3.8 %collective-permute-done.3 = f32[8,128]{1,0:T(8,128)S(1)} collective-permute-done((f32[8,128]{1,0:T(8,128)}, f32[8,128]{1,0:T(8,128)S(1)}, u32[]{:S(2)}, u32[]{:S(2)}) %collective-permute-start.3) | collective-permute-done | bytes 4128 | tf_op jit(solution)/shard_map/ppermute | solution.py:723
  24.8 0.7 add.74
  25.7 1.3 collective-permute-start.6
  27.0 1.3 collective-permute-start.5
  28.3 1.3 collective-permute-start.4
  29.6 2.4 %collective-permute-start.7 = (f32[8,128]{1,0:T(8,128)S(1)}, f32[8,128]{1,0:T(8,128)S(1)}, u32[]{:S(2)}, u32[]{:S(2)}) collective-permute-start(f32[8,128]{1,0:T(8,128)S(1)} %add.74), channel_id=1, source_target_pairs={{0,8},{1,9},{2,10},{3,11},{4,12},{5,13},{6,14},{7,15},{8,0},{9,1},... | collective-permute-start | bytes 12296 | tf_op jit(solution)/shard_map/ppermute | solution.py:723
  32.7 1.5 collective-permute-done.7
  34.2 0.7 add_add_fusion.conv_ref
  35.0 0.6 pad_maximum_fusion.5.refs_1_
  35.6 2.3 %conv_weights.1 = (bf16[128,192]{1,0:T(8,128)(2,1)}, f32[64,256]{1,0:T(8,128)}, bf16[128,256]{1,0:T(8,128)(2,1)}, f32[64,256]{1,0:T(8,128)}, bf16[192,192]{1,0:T...) custom-call(bf16[168,512]{1,0:T(8,128)(2,1)} %add_add_fusion.conv_ref), custom_call_target="tpu_custom_call" | custom-call | tf_op jit(solution)/shard_map/conv_weights/pallas_call | solution.py:175
  37.8 0.7 collective-permute-done.8
  38.6 23.5 %conv_forward.1 = (bf16[20,20,32,512]{3,2,1,0:T(8,128)(2,1)}, bf16[9,10,64,512]{3,2,1,0:T(8,128)(2,1)}, bf16[7,7,64,512]{3,2,1,0:T(8,128)(2,1)}) custom-call(bf16[4,84,336,128]{3,2,1,0:T(8,128)(2,1)} %bitcast.118, bf16[128,192]{1,0:T(8,128)(2,1)} %get-tuple-element.70.t1_ref, f32[64,256]{1,0:T(8,128)} %get-tuple-element.71.b1_ref, ...), custom_call_target="tpu_custom_call" | custom-call | tf_op jit(solution)/shard_map/conv_forward/pallas_call | solution.py:292
  62.7 0.7 slice.83
  63.8 0.7 pad.8.refs_2_
  64.5 10.9 %dense_step.1 = (f32[16,828,128]{2,1,0:T(8,128)}, bf16[3136,512]{1,0:T(8,128)(2,1)}, bf16[512,512]{1,0:T(8,128)(2,1)}, f32[32,512]{1,0:T(8,128)}, f32[32,1]{1,0:T(8,128)}, /*index=5*/f32[1,1]{1,0:T(1,128)}) custom-call(bf16[3136,512]{1,0:T(8,128)(2,1)} %bitcast.124, bf16[16,207,512]{2,1,0:T(8,128)(2,1)} %all-gather.2.cloned.1.call-done.refs_1_, ...), custom_call_target="tpu_custom_call" | custom-call | tf_op jit(solution)/shard_map/dense_step/pallas_call | solution.py:465
  75.4 1.0 reduce
  76.4 1.6 collective-permute-start.10
  78.0 1.0 reduce.1
  80.4 26.9 %upper_backward.1 = (bf16[11,11,64,512]{3,2,1,0:T(8,128)(2,1)}, f32[672,128]{1,0:T(8,128)}) custom-call(bf16[20,20,32,512]{3,2,1,0:T(8,128)(2,1)} %get-tuple-element.82.a1_hbm.a1_ref, bf16[9,10,64,512]{3,2,1,0:T(8,128)(2,1)} %get-tuple-element.83.a2_ref, bf16[7,7,64,512]{3,2,1,0:T(8,128)(2,1)} %get-tuple-element.78.a3_ref, ...), custom_call_target="tpu_custom_call" | custom-call | tf_op jit(solution)/shard_map/upper_backward/pallas_call | solution.py:613
  107.3 36.4 %lower_backward.1 = f32[672,128]{1,0:T(8,128)} custom-call(bf16[4,84,336,128]{3,2,1,0:T(8,128)(2,1)} %bitcast.119, bf16[4,84,336,128]{3,2,1,0:T(8,128)(2,1)} %bitcast.120, bf16[4,84,336,128]{3,2,1,0:T(8,128)(2,1)} %bitcast.121, bf16[4,84,336,128]{3,2,1,0:T(8,128)(2,1)} %bitcast.122, bf16[4,84,336,128]{3,2,1,0:T(8,128)(2,1)} %bitcast.123, ...), custom_call_target="tpu_custom_call" | custom-call | tf_op jit(solution)/shard_map/lower_backward/pallas_call | solution.py:701
  143.8 1.0 add.85
  145.0 1.4 collective-permute-done.12
  146.4 0.9 collective-permute-start.13
  147.3 6.6 %collective-permute-done.13 = f32[4,48,128]{2,1,0:T(8,128)S(1)} collective-permute-done((f32[4,48,128]{2,1,0:T(8,128)S(1)}, f32[4,48,128]{2,1,0:T(8,128)S(1)}, u32[]{:S(2)}, u32[]{:S(2)}) %collective-permute-start.13) | collective-permute-done | bytes 98336 | tf_op jit(solution)/shard_map/ppermute | solution.py:723
  154.0 1.5 collective-permute-start.14
  155.5 5.9 %collective-permute-done.14 = f32[2,48,128]{2,1,0:T(8,128)S(1)} collective-permute-done((f32[2,48,128]{2,1,0:T(8,128)S(1)}, f32[2,48,128]{2,1,0:T(8,128)S(1)}, u32[]{:S(2)}, u32[]{:S(2)}) %collective-permute-start.14) | collective-permute-done | bytes 49184 | tf_op jit(solution)/shard_map/ppermute | solution.py:723
  161.9 4.3 %collective-permute-done.15 = f32[1,48,128]{2,1,0:T(8,128)S(1)} collective-permute-done((f32[1,48,128]{2,1,0:T(8,128)S(1)}, f32[1,48,128]{2,1,0:T(8,128)S(1)}, u32[]{:S(2)}, u32[]{:S(2)}) %collective-permute-start.15) | collective-permute-done | bytes 24608 | tf_op jit(solution)/shard_map/ppermute | solution.py:723
  166.3 0.6 fusion.5.piece_ref
  166.9 2.5 %facts_message.1 = (f32[56,128]{1,0:T(8,128)}, f32[416,128]{1,0:T(8,128)}, f32[412,128]{1,0:T(8,128)}) custom-call(f32[828,128]{1,0:T(8,128)} %bitcast.132, f32[48,128]{1,0:T(8,128)} %fusion.5.piece_ref, f32[1,1]{1,0:T(1,128)} %get-tuple-element.96.loss_ref), custom_call_target="tpu_custom_call" | custom-call | tf_op jit(solution)/shard_map/facts_message/pallas_call | solution.py:826
  169.3 1.2 collective-permute-start.18
  170.6 0.7 collective-permute-start.17
  171.2 2.5 %collective-permute-start.16 = (f32[56,128]{1,0:T(8,128)}, f32[56,128]{1,0:T(8,128)S(1)}, u32[]{:S(2)}, u32[]{:S(2)}) collective-permute-start(f32[56,128]{1,0:T(8,128)} %get-tuple-element.97), channel_id=1, source_target_pairs={{0,8},{1,9},{2,10},{3,11},{4,12},{5,13},{6,14},{7,15},{8,0},{9,1},... | collective-permute-start | bytes 86024 | tf_op jit(solution)/shard_map/ppermute | solution.py:723
  173.7 1.2 collective-permute-start.20
  175.0 1.8 collective-permute-done.17
  176.8 0.8 fusion.4
  177.5 2.6 %collective-permute-start.19 = (f32[2,2,56,128]{3,2,1,0:T(8,128)S(1)}, f32[2,2,56,128]{3,2,1,0:T(8,128)S(1)}, u32[]{:S(2)}, u32[]{:S(2)}) collective-permute-start(f32[2,2,56,128]{3,2,1,0:T(8,128)S(1)} %maximum_bitcast_fusion), channel_id=1, source_target_pairs={{0,4},{1,5},{2,6},{3,7},{4,0},{5,1},{6,2},{7,3},{8,12},{9,13},{10,... | collective-permute-start | bytes 344072 | tf_op jit(solution)/shard_map/ppermute | solution.py:723
  180.1 2.8 %collective-permute-done.19 = f32[2,2,56,128]{3,2,1,0:T(8,128)S(1)} collective-permute-done((f32[2,2,56,128]{3,2,1,0:T(8,128)S(1)}, f32[2,2,56,128]{3,2,1,0:T(8,128)S(1)}, u32[]{:S(2)}, u32[]{:S(2)}) %collective-permute-start.19) | collective-permute-done | bytes 114720 | tf_op jit(solution)/shard_map/ppermute | solution.py:723
  183.0 1.1 collective-permute-start.21
  184.2 5.9 %collective-permute-done.22.refs_5_ = f32[412,128]{1,0:T(8,128)S(1)} collective-permute-done((f32[412,128]{1,0:T(8,128)}, f32[412,128]{1,0:T(8,128)S(1)}, u32[]{:S(2)}, u32[]{:S(2)}) %collective-permute-start.22) | collective-permute-done | bytes 210976 | tf_op jit(solution)/shard_map/ppermute | solution.py:727
  190.3 1.8 collective-permute-done.23.refs_3_
  192.1 0.8 copy-done.3
  192.9 5.7 %finish.1 = (f32[828,1,128]{2,1,0:T(1,128)}, f32[828,1,128]{2,1,0:T(1,128)}, f32[828,1,128]{2,1,0:T(1,128)}, f32[828,128]{1,0:T(8,128)}, f32[828,128]{1,0:T(8,12...) custom-call(s32[1]{0:T(128)} %bitcast.refs_0_, ...), custom_call_target="tpu_custom_call" | custom-call | tf_op jit(solution)/shard_map/finish/pallas_call | solution.py:940
  (84 shorter events, 4.0 us)
Async XLA Ops:
  7.2 55.5 %all-gather.2.cloned.1.call-start = ((), (), s32[]{:S(2)}) async-start(), calls=%async_computation.1 | async-start | bytes 3620864 | tf_op jit(solution)/shard_map/all_gather | solution.py:980
  9.1 157.8 %reduce-scatter.2.cloned.1.call-start = ((), (), s32[]{:S(2)}) async-start(), calls=%async_computation.2 | async-start | bytes 7241728 | tf_op jit(solution)/shard_map/reduce_scatter | solution.py:1022
  9.4 16.1 %collective-permute-start.2 = (bf16[168,512]{1,0:T(8,128)(2,1)S(1)}, bf16[168,512]{1,0:T(8,128)(2,1)S(1)}, u32[]{:S(2)}, u32[]{:S(2)}) collective-permute-start(bf16[168,512]{1,0:T(8,128)(2,1)S(1)} %broadcast_select_fusion), channel_id=1, source_target_pairs={{0,12},{16,28}} | collective-permute-start | bytes 516104 | tf_op jit(solution)/shard_map/ppermute | solution.py:788
  16.4 9.1 %collective-permute-start.1 = (bf16[168,512]{1,0:T(8,128)(2,1)S(1)}, bf16[168,512]{1,0:T(8,128)(2,1)S(1)}, u32[]{:S(2)}, u32[]{:S(2)}) collective-permute-start(bf16[168,512]{1,0:T(8,128)(2,1)S(1)} %broadcast_select_fusion), channel_id=1, source_target_pairs={{0,4},{16,20}} | collective-permute-start | bytes 516104 | tf_op jit(solution)/shard_map/ppermute | solution.py:788
  17.7 7.8 %collective-permute-start = (bf16[168,512]{1,0:T(8,128)(2,1)S(1)}, bf16[168,512]{1,0:T(8,128)(2,1)S(1)}, u32[]{:S(2)}, u32[]{:S(2)}) collective-permute-start(bf16[168,512]{1,0:T(8,128)(2,1)S(1)} %broadcast_select_fusion), channel_id=1, source_target_pairs={{0,8},{16,24}} | collective-permute-start | bytes 516104 | tf_op jit(solution)/shard_map/ppermute | solution.py:788
  21.0 3.8 %collective-permute-start.3 = (f32[8,128]{1,0:T(8,128)}, f32[8,128]{1,0:T(8,128)S(1)}, u32[]{:S(2)}, u32[]{:S(2)}) collective-permute-start(f32[8,128]{1,0:T(8,128)} %get-tuple-element.62), channel_id=1, source_target_pairs={{0,2},{1,3},{2,0},{3,1},{4,6},{5,7},{6,4},{7,5},{8,10},{9,11},{10,... | collective-permute-start | bytes 12296 | tf_op jit(solution)/shard_map/ppermute | solution.py:723
  25.7 8.5 %collective-permute-start.6 = (bf16[168,512]{1,0:T(8,128)(2,1)S(1)}, bf16[168,512]{1,0:T(8,128)(2,1)S(1)}, u32[]{:S(2)}, u32[]{:S(2)}) collective-permute-start(bf16[168,512]{1,0:T(8,128)(2,1)S(1)} %add_add_fusion.1), channel_id=1, source_target_pairs={{0,3},{4,7},{8,11},{12,15},{16,19},{20,23},{24,27},{28,31}} | collective-permute-start | bytes 516104 | tf_op jit(solution)/shard_map/ppermute | solution.py:788
  27.0 7.2 %collective-permute-start.5 = (bf16[168,512]{1,0:T(8,128)(2,1)S(1)}, bf16[168,512]{1,0:T(8,128)(2,1)S(1)}, u32[]{:S(2)}, u32[]{:S(2)}) collective-permute-start(bf16[168,512]{1,0:T(8,128)(2,1)S(1)} %add_add_fusion.1), channel_id=1, source_target_pairs={{0,1},{4,5},{8,9},{12,13},{16,17},{20,21},{24,25},{28,29}} | collective-permute-start | bytes 516104 | tf_op jit(solution)/shard_map/ppermute | solution.py:788
  28.3 5.9 %collective-permute-start.4 = (bf16[168,512]{1,0:T(8,128)(2,1)S(1)}, bf16[168,512]{1,0:T(8,128)(2,1)S(1)}, u32[]{:S(2)}, u32[]{:S(2)}) collective-permute-start(bf16[168,512]{1,0:T(8,128)(2,1)S(1)} %add_add_fusion.1), channel_id=1, source_target_pairs={{0,2},{4,6},{8,10},{12,14},{16,18},{20,22},{24,26},{28,30}} | collective-permute-start | bytes 516104 | tf_op jit(solution)/shard_map/ppermute | solution.py:788
  29.6 4.6 %collective-permute-start.7 = (f32[8,128]{1,0:T(8,128)S(1)}, f32[8,128]{1,0:T(8,128)S(1)}, u32[]{:S(2)}, u32[]{:S(2)}) collective-permute-start(f32[8,128]{1,0:T(8,128)S(1)} %add.74), channel_id=1, source_target_pairs={{0,8},{1,9},{2,10},{3,11},{4,12},{5,13},{6,14},{7,15},{8,0},{9,1},... | collective-permute-start | bytes 12296 | tf_op jit(solution)/shard_map/ppermute | solution.py:723
  35.0 3.6 %collective-permute-start.8 = (f32[8,128]{1,0:T(8,128)S(1)}, f32[8,128]{1,0:T(8,128)S(1)}, u32[]{:S(2)}, u32[]{:S(2)}) collective-permute-start(f32[8,128]{1,0:T(8,128)S(1)} %add.78), channel_id=1, source_target_pairs={{0,4},{1,5},{2,6},{3,7},{4,0},{5,1},{6,2},{7,3},{8,12},{9,13},{10,... | collective-permute-start | bytes 12296 | tf_op jit(solution)/shard_map/ppermute | solution.py:723
  38.6 23.5 %collective-permute-start.9 = (f32[8,128]{1,0:T(8,128)S(1)}, f32[8,128]{1,0:T(8,128)S(1)}, u32[]{:S(2)}, u32[]{:S(2)}) collective-permute-start(f32[8,128]{1,0:T(8,128)S(1)} %add.82), channel_id=1, source_target_pairs={{0,1},{1,0},{2,3},{3,2},{4,5},{5,4},{6,7},{7,6},{8,9},{9,8},{10,11... | collective-permute-start | bytes 12296 | tf_op jit(solution)/shard_map/ppermute | solution.py:723
  64.5 10.9 %copy-start.4 = (f32[1,105984]{1,0:T(1,128)S(1)}, f32[1,105984]{1,0:T(1,128)}, u32[]{:S(2)}) copy-start(f32[1,105984]{1,0:T(1,128)} %param.22) | copy-start | bytes 1271812
  75.3 2.7 %copy-start.5 = (f32[1,105984]{1,0:T(1,128)S(1)}, f32[1,105984]{1,0:T(1,128)}, u32[]{:S(2)}) copy-start(f32[1,105984]{1,0:T(1,128)} %param.23) | copy-start | bytes 1271812
  75.3 4.3 %copy-start.9 = (f32[32,512]{1,0:T(8,128)S(1)}, f32[32,512]{1,0:T(8,128)}, u32[]{:S(2)}) copy-start(f32[32,512]{1,0:T(8,128)} %get-tuple-element.94) | copy-start | bytes 196612
  75.4 4.8 %copy-start.10 = (f32[32,1]{1,0:T(8,128)S(1)}, f32[32,1]{1,0:T(8,128)}, u32[]{:S(2)}) copy-start(f32[32,1]{1,0:T(8,128)} %get-tuple-element.95) | copy-start | bytes 388
  76.4 30.9 %copy-start.1 = (f32[105984]{0:T(1024)}, f32[105984]{0:T(1024)S(1)}, u32[]{:S(2)}) copy-start(f32[105984]{0:T(1024)S(1)} %reduce) | copy-start | bytes 1271812
  76.4 30.9 %collective-permute-start.10 = (f32[105984]{0:T(1024)S(1)}, f32[105984]{0:T(1024)}, u32[]{:S(2)}, u32[]{:S(2)}) collective-permute-start(f32[105984]{0:T(1024)S(1)} %reduce), channel_id=1, source_target_pairs={{0,16},{16,0},{1,17},{17,1},{2,18},{18,2},{3,19},{19,3},{4,20},{20... | collective-permute-start | bytes 1271816 | tf_op jit(solution)/shard_map/ppermute | solution.py:727
  79.0 28.3 %copy-start.2 = (f32[105984]{0:T(1024)}, f32[105984]{0:T(1024)S(1)}, u32[]{:S(2)}) copy-start(f32[105984]{0:T(1024)S(1)} %reduce.1) | copy-start | bytes 1271812
  79.1 28.3 %collective-permute-start.11 = (f32[105984]{0:T(1024)S(1)}, f32[105984]{0:T(1024)}, u32[]{:S(2)}, u32[]{:S(2)}) collective-permute-start(f32[105984]{0:T(1024)S(1)} %reduce.1), channel_id=1, source_target_pairs={{0,16},{16,0},{1,17},{17,1},{2,18},{18,2},{3,19},{19,3},{4,20},{20... | collective-permute-start | bytes 1271816 | tf_op jit(solution)/shard_map/ppermute | solution.py:727
  107.3 36.5 %copy-start.6 = (f32[672,128]{1,0:T(8,128)S(1)}, f32[672,128]{1,0:T(8,128)}, u32[]{:S(2)}) copy-start(f32[672,128]{1,0:T(8,128)} %get-tuple-element.93) | copy-start | bytes 1032196
  144.9 1.5 collective-permute-start.12
  146.4 7.5 %collective-permute-start.13 = (f32[4,48,128]{2,1,0:T(8,128)S(1)}, f32[4,48,128]{2,1,0:T(8,128)S(1)}, u32[]{:S(2)}, u32[]{:S(2)}) collective-permute-start(f32[4,48,128]{2,1,0:T(8,128)S(1)} %select_bitcast_fusion.5), channel_id=1, source_target_pairs={{0,2},{1,3},{2,0},{3,1},{4,6},{5,7},{6,4},{7,5},{8,10},{9,11},{10,... | collective-permute-start | bytes 294920 | tf_op jit(solution)/shard_map/ppermute | solution.py:723
  154.0 7.4 %collective-permute-start.14 = (f32[2,48,128]{2,1,0:T(8,128)S(1)}, f32[2,48,128]{2,1,0:T(8,128)S(1)}, u32[]{:S(2)}, u32[]{:S(2)}) collective-permute-start(f32[2,48,128]{2,1,0:T(8,128)S(1)} %select_bitcast_fusion.6), channel_id=1, source_target_pairs={{0,4},{1,5},{2,6},{3,7},{4,0},{5,1},{6,2},{7,3},{8,12},{9,13},{10,... | collective-permute-start | bytes 147464 | tf_op jit(solution)/shard_map/ppermute | solution.py:723
  161.4 4.8 %collective-permute-start.15 = (f32[1,48,128]{2,1,0:T(8,128)S(1)}, f32[1,48,128]{2,1,0:T(8,128)S(1)}, u32[]{:S(2)}, u32[]{:S(2)}) collective-permute-start(f32[1,48,128]{2,1,0:T(8,128)S(1)} %select_bitcast_fusion.7), channel_id=1, source_target_pairs={{0,8},{1,9},{2,10},{3,11},{4,12},{5,13},{6,14},{7,15},{8,0},{9,1},... | collective-permute-start | bytes 73736 | tf_op jit(solution)/shard_map/ppermute | solution.py:723
  169.3 5.6 %collective-permute-start.18 = (f32[56,128]{1,0:T(8,128)}, f32[56,128]{1,0:T(8,128)S(1)}, u32[]{:S(2)}, u32[]{:S(2)}) collective-permute-start(f32[56,128]{1,0:T(8,128)} %get-tuple-element.97), channel_id=1, source_target_pairs={{0,16},{16,0},{1,17},{17,1},{2,18},{18,2},{3,19},{19,3},{4,20},{20... | collective-permute-start | bytes 86024 | tf_op jit(solution)/shard_map/ppermute | solution.py:727
  170.6 6.2 %collective-permute-start.17 = (f32[56,128]{1,0:T(8,128)}, f32[56,128]{1,0:T(8,128)S(1)}, u32[]{:S(2)}, u32[]{:S(2)}) collective-permute-start(f32[56,128]{1,0:T(8,128)} %get-tuple-element.97), channel_id=1, source_target_pairs={{0,24},{1,25},{2,26},{3,27},{4,28},{5,29},{6,30},{7,31},{8,16},{9,... | collective-permute-start | bytes 86024 | tf_op jit(solution)/shard_map/ppermute | solution.py:757
  171.2 5.5 %collective-permute-start.16 = (f32[56,128]{1,0:T(8,128)}, f32[56,128]{1,0:T(8,128)S(1)}, u32[]{:S(2)}, u32[]{:S(2)}) collective-permute-start(f32[56,128]{1,0:T(8,128)} %get-tuple-element.97), channel_id=1, source_target_pairs={{0,8},{1,9},{2,10},{3,11},{4,12},{5,13},{6,14},{7,15},{8,0},{9,1},... | collective-permute-start | bytes 86024 | tf_op jit(solution)/shard_map/ppermute | solution.py:723
  173.7 9.2 %collective-permute-start.20 = (f32[416,128]{1,0:T(8,128)}, f32[416,128]{1,0:T(8,128)S(1)}, u32[]{:S(2)}, u32[]{:S(2)}) collective-permute-start(f32[416,128]{1,0:T(8,128)} %get-tuple-element.98), channel_id=1, source_target_pairs={{0,16},{16,0},{1,17},{17,1},{2,18},{18,2},{3,19},{19,3},{4,20},{20... | collective-permute-start | bytes 638984 | tf_op jit(solution)/shard_map/ppermute | solution.py:727
  177.5 5.4 %collective-permute-start.19 = (f32[2,2,56,128]{3,2,1,0:T(8,128)S(1)}, f32[2,2,56,128]{3,2,1,0:T(8,128)S(1)}, u32[]{:S(2)}, u32[]{:S(2)}) collective-permute-start(f32[2,2,56,128]{3,2,1,0:T(8,128)S(1)} %maximum_bitcast_fusion), channel_id=1, source_target_pairs={{0,4},{1,5},{2,6},{3,7},{4,0},{5,1},{6,2},{7,3},{8,12},{9,13},{10,... | collective-permute-start | bytes 344072 | tf_op jit(solution)/shard_map/ppermute | solution.py:723
  182.9 9.2 %copy-start.7 = (f32[416,128]{1,0:T(8,128)}, f32[416,128]{1,0:T(8,128)S(1)}, u32[]{:S(2)}) copy-start(f32[416,128]{1,0:T(8,128)S(1)} %collective-permute-done.20.refs_4_) | copy-start | bytes 638980
  183.0 7.1 %collective-permute-start.21 = (f32[4,2,56,128]{3,2,1,0:T(8,128)S(1)}, f32[4,2,56,128]{3,2,1,0:T(8,128)S(1)}, u32[]{:S(2)}, u32[]{:S(2)}) collective-permute-start(f32[4,2,56,128]{3,2,1,0:T(8,128)S(1)} %bitcast.136), channel_id=1, source_target_pairs={{0,2},{1,3},{2,0},{3,1},{4,6},{5,7},{6,4},{7,5},{8,10},{9,11},{10,... | collective-permute-start | bytes 688136 | tf_op jit(solution)/shard_map/ppermute | solution.py:723
  184.0 6.1 %collective-permute-start.22 = (f32[412,128]{1,0:T(8,128)}, f32[412,128]{1,0:T(8,128)S(1)}, u32[]{:S(2)}, u32[]{:S(2)}) collective-permute-start(f32[412,128]{1,0:T(8,128)} %get-tuple-element.100), channel_id=1, source_target_pairs={{0,16},{16,0},{1,17},{17,1},{2,18},{18,2},{3,19},{19,3},{4,20},{20... | collective-permute-start | bytes 632840 | tf_op jit(solution)/shard_map/ppermute | solution.py:727
  190.1 2.0 copy-start.8
  190.2 1.9 copy-start
  190.2 1.9 collective-permute-start.23
  192.1 0.8 copy-start.3
Sparse Core Ops, SparseCore 0:
  10.8 49.9 all-gather.1
  75.5 89.9 reduce-scatter.1
